TPU v7x, 128 devices: a whole 4x4x4 slice. The times are simulated.
128 devices in a mesh: rows: 32 (over x, z, core), units: 4 (over y).
Axes of the slice: x: 4, y: 4, z: 4, core: 2. Of those that a mesh axis runs over, the one named last changes fastest.
Arguments:
- residuals: bfloat16 [524288, 2048], P(('rows', 'units')), may hold values from -24 to 24
- loadings: bfloat16 [524288, 256], P(('rows', 'units')), may hold values from -6 to 6
- zero_points: bfloat16 [1024, 2048], P('units'), may hold values from -0.375 to 0.375
- sketch_matrix: bfloat16 [2048, 256], replicated, may hold values from -0.125 to 0.125
- use_lists: int32 [4096, 4], P(('rows', 'units')), may hold values from 0 to 15, all different within a row
Outputs:
- star_basis: float32 [524288, 256], P(('rows', 'units'))
- bin_modes: float32 [2048, 256], P(('rows', 'units'))
Inputs may be any that keep to these rules, and one draw needn't show every extreme that they name: `use_lists`: each row names 4 different groups; every group is named by some row.
All inputs are finite; a program needn't handle non-finite values.
Results may differ from a plain program's by a relative error of at most 0.003.
Values may be sent and summed in bfloat16 or wider, within the bound.
No kernel may reach another device: no remote copies, remote signals or barrier semaphores. Data moves between devices by JAX's collectives and lax.ppermute only.
A program may use at most 192 MiB of HBM per device.

v0:
```python
import jax
import jax.numpy as jnp
from jax import lax
from jax.sharding import PartitionSpec as P

GROUP = 64
USES = 4
BLOCK_STARS = 128


def on_device(residuals, loadings, zero_points, sketch_matrix, use_lists):
    gathered = lax.all_gather(zero_points, "units", axis=0, tiled=True)
    local_rows, width_bins = residuals.shape
    group_count = gathered.shape[0] // GROUP
    block_count = use_lists.shape[0]
    tables = gathered.reshape(group_count, GROUP, width_bins)
    chosen = tables[use_lists].reshape(block_count, USES * GROUP, width_bins)
    offsets = jnp.einsum(
        "bsk,bkn->bsn",
        loadings.reshape(block_count, BLOCK_STARS, USES * GROUP),
        chosen,
        preferred_element_type=jnp.float32,
    )
    corrected = (
        residuals.reshape(block_count, BLOCK_STARS, width_bins).astype(jnp.float32) - offsets
    ).astype(jnp.bfloat16)
    corrected = corrected.reshape(local_rows, width_bins)
    sketched = jnp.dot(corrected, sketch_matrix, preferred_element_type=jnp.float32)
    sketch_low = sketched.astype(jnp.bfloat16)
    devices_all = lax.axis_size(("rows", "units"))
    total_stars = local_rows * devices_all
    gram_local = jnp.dot(sketched.T, sketched, precision=lax.Precision.HIGHEST) / total_stars
    lower_factor = jnp.linalg.cholesky(lax.psum(gram_local, ("rows", "units")))
    star_basis = lax.linalg.triangular_solve(
        lower_factor, sketched, left_side=False, lower=True, transpose_a=True
    )
    bin_share = width_bins // devices_all
    full_terms = jnp.einsum("sn,sm->nm", corrected, sketch_low, preferred_element_type=jnp.float32)
    summed_all = lax.psum(full_terms, ("rows", "units"))
    first_bin = lax.axis_index(("rows", "units")) * bin_share
    summed = lax.dynamic_slice_in_dim(summed_all, first_bin, bin_share, 0)
    raw_modes = summed / total_stars
    bin_modes = lax.linalg.triangular_solve(
        lower_factor, raw_modes, left_side=False, lower=True, transpose_a=True
    )
    return (star_basis, bin_modes)


def solution(mesh):
    in_specs = (
        P(("rows", "units"), None),
        P(("rows", "units"), None),
        P("units", None),
        P(),
        P(("rows", "units"), None),
    )
    out_specs = (P(("rows", "units"), None), P(("rows", "units"), None))
    return jax.shard_map(
        on_device, mesh=mesh, in_specs=in_specs, out_specs=out_specs, check_vma=False
    )
```

profile of v0, /device:TPU:0, one launch (start us, length us, event | category | flops | bytes accessed | tf_op | source)
XLA Modules:
  0.0 364.3 jit_solution(14588423251606039512)
XLA Ops:
  8.0 0.7 compare_select_fusion
  8.9 51.5 %all-gather.2.cloned.1.call-done = bf16[1024,2048]{1,0:T(8,128)(2,1)} async-done(((bf16[256,2048]{1,0:T(8,128)(2,1)}), bf16[1024,2048]{1,0:T(8,128)(2,1)}) %all-gather.2.cloned.1.call-update) | async-done | bytes 4194320 | tf_op jit(solution)/shard_map/all_gather | solution.py:12
  60.4 14.9 %gather_fusion = bf16[128,64,2048]{2,1,0:T(8,128)(2,1)} fusion(bf16[16,64,2048]{2,1,0:T(8,128)(2,1)} %bitcast.51, s32[1024]{0:T(1024)S(1)} %pad_clamp_fusion), kind=kCustom, calls=%fused_computation | custom fusion | bytes 67109376 | tf_op jit(solution)/shard_map/gather | solution.py:17
  75.3 23.4 %fusion = bf16[32,128,2048]{2,1,0:T(8,128)(2,1)} fusion(bf16[32,128,2048]{2,1,0:T(8,128)(2,1)} %bitcast.53, bf16[32,128,256]{2,1,0:T(8,128)(2,1)S(1)} %bitcast.50, bf16[32,256,2048]{2,1,0:T(8,128)(2,1)} %bitcast.52), kind=kOutput, calls=%fused_computation.4 | convolution fusion | flops 4320133120 | bytes 69206016 | tf_op jit(solution)/shard_map/bsk,bkn->bsn/dot_general | solution.py:18
  98.7 10.0 %fusion.16 = f32[4096,256]{1,0:T(8,128)S(1)} fusion(bf16[4096,2048]{1,0:T(8,128)(2,1)} %bitcast.54, bf16[2048,256]{1,0:T(8,128)(2,1)S(1)} %copy-done.5), kind=kOutput, calls=%fused_computation.44 | convolution fusion | flops 4294967296 | bytes 22020096 | tf_op jit(solution)/shard_map/dot_general | solution.py:28
  109.3 6.3 %fusion.3 = f32[2048,256]{1,0:T(8,128)} fusion(bf16[4096,2048]{1,0:T(8,128)(2,1)S(1)} %bitcast.55, f32[4096,256]{1,0:T(8,128)S(1)} %fusion.16), kind=kOutput, calls=%fused_computation.9 | convolution fusion | flops 4296015872 | bytes 23068672 | tf_op jit(solution)/shard_map/sn,sm->nm/dot_general | solution.py:38
  115.6 7.4 %convolution_multiply_fusion = f32[256,256]{0,1:T(8,128)} fusion(f32[4096,256]{1,0:T(8,128)S(1)} %fusion.16), kind=kOutput, calls=%fused_computation.11 | convolution fusion | flops 3221291008 | bytes 4456448 | tf_op jit(solution)/shard_map/dot_general | solution.py:32
  123.1 152.7 %all-reduce.4.cloned.1.call-done = (f32[256,256]{0,1:T(8,128)}, f32[2048,256]{1,0:T(8,128)}) async-done(((f32[256,256]{0,1:T(8,128)}, f32[2048,256]{1,0:T(8,128)}), (f32[256,256]{0,1:T(8,128)}, f32[2048,256]{1,0:T(8,128)})) %all-reduce.4.cloned.1.call-update) | async-done | bytes 2359312 | tf_op jit(solution)/shard_map/psum | solution.py:33
  275.8 1.3 copy.13
  277.0 1.0 fusion.5
  278.0 11.7 %cholesky.50 = f32[128,128]{1,0:T(8,128)S(1)} custom-call(f32[128,128]{1,0:T(8,128)S(1)} %cholesky.118), custom_call_target="Cholesky" | custom-call | tf_op jit(solution)/shard_map/jit(cholesky)/cholesky | solution.py:33
  289.8 9.8 %custom-call.16 = f32[1,128,128]{1,2,0:T(8,128)S(1)} custom-call(f32[1,128,128]{2,1,0:T(8,128)S(1)} %get-tuple-element.29), custom_call_target="InvertDiagBlocksLowerTriangular" | custom-call | tf_op jit(solution)/shard_map/jit(cholesky)/cholesky | solution.py:33
  300.1 11.7 %cholesky.105 = f32[128,128]{1,0:T(8,128)S(1)} custom-call(f32[128,128]{1,0:T(8,128)S(1)} %convolution_subtract_fusion.1), custom_call_target="Cholesky" | custom-call | tf_op jit(solution)/shard_map/jit(cholesky)/cholesky | solution.py:33
  311.9 0.7 compare_reduce_fusion
  313.9 3.9 %while.1 = (s32[]{:T(128)}, f32[256,256]{1,0:T(8,128)S(1)}, s32[2,2]{1,0:T(2,128)S(1)}, f32[2,128,128]{2,1,0:T(8,128)S(1)}, s32[]{:T(128)}) while((s32[]{:T(128)}, f32[256,256]{1,0:T(8,128)S(1)}, s32[2,2]{1,0:T(2,128)S(1)}, f32[2,128,128]{2,1,0:T(8,128)S(1)}, s32[]{:T(128)}) %tuple.29), condition=%wide.while_cond, body=%wide.while_body.sunk | while | flops 2 | bytes 131181 | solution.py:34
  314.5 1.3 bitcast_dynamic-update-slice_fusion.2
  316.5 1.3 bitcast_dynamic-update-slice_fusion.2
  317.8 19.9 %custom-call.17 = f32[2,128,128]{1,2,0:T(8,128)S(1)} custom-call(f32[2,128,128]{2,1,0:T(8,128)S(1)} %get-tuple-element.9), custom_call_target="InvertDiagBlocksLowerTriangular" | custom-call | tf_op jit(solution)/shard_map/triangular_solve | solution.py:34
  337.8 3.7 %fusion.1 = f32[4096,128]{0,1:T(8,128)S(1)} fusion(f32[4096,256]{1,0:T(8,128)} %copy-done.2, f32[2,128,128]{1,2,0:T(8,128)S(1)} %custom-call.17), kind=kOutput, calls=%fused_computation.7 | convolution fusion | flops 805306368 | bytes 4259840 | tf_op jit(solution)/shard_map/triangular_solve | solution.py:34
  341.5 0.7 dynamic-slice_multiply_fusion
  343.4 3.6 convolution_subtract_fusion
  347.0 2.0 fusion.11
  349.0 2.4 pad_maximum_fusion
  351.4 5.6 %copy.14 = f32[4096,256]{1,0:T(8,128)} copy(f32[4096,256]{0,1:T(8,128)} %pad_maximum_fusion) | data formatting | bytes 8388608
  (37 shorter events, 4.5 us)
Async XLA Ops:
  7.2 68.1 %copy-start = (bf16[4096,256]{1,0:T(8,128)(2,1)S(1)}, bf16[4096,256]{1,0:T(8,128)(2,1)}, u32[]{:S(2)}) copy-start(bf16[4096,256]{1,0:T(8,128)(2,1)} %param.6) | copy-start | bytes 6291460
  7.2 53.2 %all-gather.2.cloned.1.call-start = ((), (), s32[]{:S(2)}) async-start(), calls=%async_computation | async-start | bytes 5242880 | tf_op jit(solution)/shard_map/all_gather | solution.py:12
  7.9 267.8 %all-reduce.4.cloned.1.call-start = ((), (), s32[]{:S(2)}) async-start(), calls=%async_computation.1 | async-start | bytes 4718592 | tf_op jit(solution)/shard_map/psum | solution.py:33
  75.3 23.4 %copy-start.5 = (bf16[2048,256]{1,0:T(8,128)(2,1)S(1)}, bf16[2048,256]{1,0:T(8,128)(2,1)}, u32[]{:S(2)}) copy-start(bf16[2048,256]{1,0:T(8,128)(2,1)} %param.8) | copy-start | bytes 3145732
  98.7 10.5 %copy-start.4 = (bf16[32,128,2048]{2,1,0:T(8,128)(2,1)S(1)}, bf16[32,128,2048]{2,1,0:T(8,128)(2,1)}, u32[]{:S(2)}) copy-start(bf16[32,128,2048]{2,1,0:T(8,128)(2,1)} %fusion) | copy-start | bytes 50331652
  109.3 6.3 %copy-start.2 = (f32[4096,256]{1,0:T(8,128)}, f32[4096,256]{1,0:T(8,128)S(1)}, u32[]{:S(2)}) copy-start(f32[4096,256]{1,0:T(8,128)S(1)} %fusion.16) | copy-start | bytes 12582916
  337.7 5.7 %copy-start.3 = (f32[4096,256]{1,0:T(8,128)S(1)}, f32[4096,256]{1,0:T(8,128)}, u32[]{:S(2)}) copy-start(f32[4096,256]{1,0:T(8,128)} %copy-done.2) | copy-start | bytes 12582916
  349.0 8.0 %copy-start.1 = (bf16[4096,256]{1,0:T(8,128)(2,1)S(1)}, bf16[4096,256]{1,0:T(8,128)(2,1)}, u32[]{:S(2)}) copy-start(bf16[4096,256]{1,0:T(8,128)(2,1)} %param.6) | copy-start | bytes 6291460
Sparse Core Ops, SparseCore 0:
  9.7 50.6 all-gather.1
  123.2 152.5 all-reduce.3
where the time goes:
time: 369 us; the launch traced here: 364 us
  waiting for transfers between devices  205 us (56%)
  other arithmetic  59.4 us (16%)
  matrix products  57.6 us (16%)
  local copies, waits for them, and re-layouts  26.4 us (7%)
  between operations  15.9 us (4%)
    psum x1, waiting for transfers between devices, on_device(): lower_factor = jnp.linalg.cholesky(lax.psum(gram_local, ('rows', 'units')))  153 us
    all_gather x1, waiting for transfers between devices, on_device(): gathered = lax.all_gather(zero_points, 'units', axis=0, tiled=True)  51.5 us
    another operation x6, other arithmetic, on_device(): lower_factor = jnp.linalg.cholesky(lax.psum(gram_local, ('rows', 'units')))  34 us
    dot_general x1, matrix products, on_device(): jnp.einsum('bsk,bkn->bsn', loadings.reshape(block_count, BLOCK_STARS, USE...  23.4 us
    another operation x4, other arithmetic, on_device(): lax.linalg.triangular_solve(lower_factor, sketched, left_side=False, lowe...  22.4 us
    gather x1, local copies, waits for them, and re-layouts, on_device(): chosen = tables[use_lists].reshape(block_count, USES * GROUP, width_bins)  14.9 us
    dot_general x1, matrix products, on_device(): jnp.dot(corrected, sketch_matrix, preferred_element_type=jnp.float32)  10 us
    another operation x3, matrix products, on_device(): lax.linalg.triangular_solve(lower_factor, sketched, left_side=False, lowe...  9.33 us
  transfers between devices with their start and end apart: 2, of which 2 were waited for; matrix products, arithmetic and copies ran while one was open for 0% of the time, Pallas kernels for 0%

commit v1 on v0

v1 whole, which is shorter than its diff:
```python
import functools

import jax
import jax.numpy as jnp
from jax import lax
from jax.experimental import pallas as pl
from jax.experimental.pallas import tpu as pltpu
from jax.sharding import PartitionSpec as P

GROUP = 64
USES = 4
BLOCK_STARS = 128
MODES = 256
STARS = 524288
AXES = ("rows", "units")
F32 = jnp.float32
BF16 = jnp.bfloat16
HIGHEST = lax.Precision.HIGHEST
BIG = pltpu.CompilerParams(vmem_limit_bytes=60 << 20)


def split_low(value):
    high = value.astype(BF16)
    return high, (value - high.astype(F32)).astype(BF16)


def dot_rows(a, b):
    return lax.dot_general(a, b, (((0,), (0,)), ((), ())), preferred_element_type=F32)


def dot_last(a, b, precision=None):
    return lax.dot_general(
        a, b, (((1,), (1,)), ((), ())), preferred_element_type=F32, precision=precision
    )


def permutation(move):
    pairs = []
    for x in range(4):
        for z in range(4):
            for c in range(2):
                for y in range(4):
                    u, w, d, v = move(x, z, c, y)
                    pairs.append((((x * 4 + z) * 2 + c) * 4 + y, ((u * 4 + w) * 2 + d) * 4 + v))
    return pairs


SWAP = permutation(lambda x, z, c, y: (x, z, 1 - c, y))
SHIFTS = {
    "x": [permutation(lambda x, z, c, y, k=k: ((x + k) % 4, z, c, y)) for k in (1, 2, 3)],
    "y": [permutation(lambda x, z, c, y, k=k: (x, z, c, (y + k) % 4)) for k in (1, 2, 3)],
    "z": [permutation(lambda x, z, c, y, k=k: (x, (z + k) % 4, c, y)) for k in (1, 2, 3)],
}


def shift_all(axis, pieces):
    return [lax.ppermute(p, AXES, SHIFTS[axis][k]) for k, p in enumerate(pieces)]


def project_kernel(place, zero_ref, sketch_ref, full_ref, half_ref):
    full_ref[...] = jnp.dot(zero_ref[...], sketch_ref[...], preferred_element_type=F32)
    half = full_ref.shape[0] // 2
    half_ref[...] = full_ref[pl.ds(pl.multiple_of(place[2] * half, half), half), :]


def project(place, zero_points, sketch_matrix):
    units = zero_points.shape[0]
    return pl.pallas_call(
        project_kernel,
        grid_spec=pltpu.PrefetchScalarGridSpec(
            num_scalar_prefetch=1,
            grid=(1,),
            in_specs=[
                pl.BlockSpec(zero_points.shape, lambda i, p: (0, 0)),
                pl.BlockSpec(sketch_matrix.shape, lambda i, p: (0, 0)),
            ],
            out_specs=[
                pl.BlockSpec((units, MODES), lambda i, p: (0, 0)),
                pl.BlockSpec((units // 2, MODES), lambda i, p: (0, 0)),
            ],
        ),
        out_shape=[
            jax.ShapeDtypeStruct((units, MODES), F32),
            jax.ShapeDtypeStruct((units // 2, MODES), F32),
        ],
        name="project",
    )(place, zero_points, sketch_matrix)


def sketch_kernel(res_ref, sketch_ref, out_ref):
    out_ref[...] = jnp.dot(res_ref[...], sketch_ref[...], preferred_element_type=F32)


def sketch(residuals, sketch_matrix, tile=512):
    rows, bins = residuals.shape
    return pl.pallas_call(
        sketch_kernel,
        grid=(rows // tile,),
        in_specs=[
            pl.BlockSpec((tile, bins), lambda i: (i, 0)),
            pl.BlockSpec((bins, MODES), lambda i: (0, 0)),
        ],
        out_specs=pl.BlockSpec((tile, MODES), lambda i: (i, 0)),
        out_shape=jax.ShapeDtypeStruct((rows, MODES), F32),
        cost_estimate=pl.CostEstimate(
            flops=2 * rows * bins * MODES, bytes_accessed=rows * bins * 2 + rows * MODES * 4, transcendentals=0
        ),
        name="sketch",
    )(residuals, sketch_matrix)


def correct_kernel(blocks, place, uses, part_ref, load_ref, own_ref, sw1, sw2, sw3, ha1, ha2, ha3,
                   high_ref, low_ref, gram_keep, gram_send, w_keep, w_send1, w_send2, w_send3,
                   table_high, table_low, gram_hh, gram_hl, weights):
    step = pl.program_id(0)
    units = own_ref.shape[0]
    half = units // 2
    y, c = place[3], place[2]

    @pl.when(step == 0)
    def _():
        gram_hh[...] = jnp.zeros_like(gram_hh)
        gram_hl[...] = jnp.zeros_like(gram_hl)
        weights[...] = jnp.zeros_like(weights)

        def put(start, value):
            high, low = split_low(value)
            rows = pl.ds(pl.multiple_of(start, 128), value.shape[0])
            table_high[rows, :] = high
            table_low[rows, :] = low

        put(y * units, own_ref[...])
        for k, (mine, other) in enumerate(((ha1, sw1), (ha2, sw2), (ha3, sw3))):
            base = lax.rem(y + 3 - k, 4) * units
            put(base + c * half, mine[...])
            put(base + (1 - c) * half, other[...])

    for block in range(blocks):
        rows = pl.ds(block * BLOCK_STARS, BLOCK_STARS)
        groups = [uses[step * blocks + block, use] for use in range(USES)]
        starts = [pl.multiple_of(g * GROUP, GROUP) for g in groups]
        load = load_ref[rows, :]
        high_table = jnp.concatenate([table_high[pl.ds(s, GROUP), :] for s in starts], axis=0)
        low_table = jnp.concatenate([table_low[pl.ds(s, GROUP), :] for s in starts], axis=0)
        offset = jnp.dot(load, high_table, preferred_element_type=F32)
        offset = offset + jnp.dot(load, low_table, preferred_element_type=F32)
        high, low = split_low(part_ref[rows, :] - offset)
        high_ref[rows, :] = high
        low_ref[rows, :] = low
        product = dot_rows(load, high)
        for use in range(USES):
            weights[pl.ds(starts[use], GROUP), :] += product[use * GROUP:(use + 1) * GROUP, :]
    gram_hh[...] += dot_rows(high_ref[...], high_ref[...])
    gram_hl[...] += dot_rows(high_ref[...], low_ref[...])

    @pl.when(step == pl.num_programs(0) - 1)
    def _():
        cross = gram_hl[...]
        gram = gram_hh[...] + cross + cross.T
        packed = jnp.concatenate([gram[:128, :128], gram[128:, :128], gram[128:, 128:]], axis=0)
        gram_hh[...] = gram
        first = c == 0
        gram_keep[...] = jnp.where(first, packed[:192], packed[192:])
        gram_send[...] = jnp.where(first, packed[192:], packed[:192])
        w_keep[...] = weights[pl.ds(pl.multiple_of(y * units, 256), units), :]
        for k, ref in enumerate((w_send1, w_send2, w_send3)):
            base = lax.rem(y + k + 1, 4) * units
            ref[...] = weights[pl.ds(pl.multiple_of(base, 256), units), :].astype(BF16)


def correct(place, use_lists, part, loadings, own, halves, swapped, blocks=4):
    rows = part.shape[0]
    tile = blocks * BLOCK_STARS
    units = own.shape[0]
    whole = lambda i, p, u: (0, 0)
    row = lambda i, p, u: (i, 0)
    return pl.pallas_call(
        functools.partial(correct_kernel, blocks),
        grid_spec=pltpu.PrefetchScalarGridSpec(
            num_scalar_prefetch=2,
            grid=(rows // tile,),
            in_specs=[
                pl.BlockSpec((tile, MODES), row),
                pl.BlockSpec((tile, MODES), row),
                pl.BlockSpec((units, MODES), whole),
            ] + [pl.BlockSpec((units // 2, MODES), whole)] * 6,
            out_specs=[
                pl.BlockSpec((tile, MODES), row),
                pl.BlockSpec((tile, MODES), row),
                pl.BlockSpec((192, 128), whole),
                pl.BlockSpec((192, 128), whole),
            ] + [pl.BlockSpec((units, MODES), whole)] * 4,
            scratch_shapes=[
                pltpu.VMEM((4 * units, MODES), BF16),
                pltpu.VMEM((4 * units, MODES), BF16),
                pltpu.VMEM((MODES, MODES), F32),
                pltpu.VMEM((MODES, MODES), F32),
                pltpu.VMEM((4 * units, MODES), F32),
            ],
        ),
        out_shape=[
            jax.ShapeDtypeStruct((rows, MODES), BF16),
            jax.ShapeDtypeStruct((rows, MODES), BF16),
            jax.ShapeDtypeStruct((192, 128), F32),
            jax.ShapeDtypeStruct((192, 128), F32),
            jax.ShapeDtypeStruct((units, MODES), F32),
        ] + [jax.ShapeDtypeStruct((units, MODES), BF16)] * 3,
        cost_estimate=pl.CostEstimate(
            flops=2 * rows * MODES * MODES * 5, bytes_accessed=rows * MODES * 10, transcendentals=0
        ),
        name="correct",
    )(place, use_lists, part, loadings, own, *swapped, *halves)


def raw_kernel(res_ref, high_ref, out_ref):
    @pl.when(pl.program_id(0) == 0)
    def _():
        out_ref[...] = jnp.zeros_like(out_ref)

    out_ref[...] += dot_rows(high_ref[...], res_ref[...])


def raw_sums(residuals, high, tile=1024):
    rows, bins = residuals.shape
    return pl.pallas_call(
        raw_kernel,
        grid=(rows // tile,),
        in_specs=[
            pl.BlockSpec((tile, bins), lambda i: (i, 0)),
            pl.BlockSpec((tile, MODES), lambda i: (i, 0)),
        ],
        out_specs=pl.BlockSpec((MODES, bins), lambda i: (0, 0)),
        out_shape=jax.ShapeDtypeStruct((MODES, bins), F32),
        cost_estimate=pl.CostEstimate(
            flops=2 * rows * bins * MODES, bytes_accessed=rows * bins * 2 + bins * MODES * 4, transcendentals=0
        ),
        name="raw_sums",
    )(residuals, high)


def finish_kernel(place, raw_ref, zero_ref, w_keep, w1, w2, w3, keep_ref, send_ref, ordered):
    weights = w_keep[...] + w1[...].astype(F32) + w2[...].astype(F32) + w3[...].astype(F32)
    total = raw_ref[...] - dot_rows(weights.astype(BF16), zero_ref[...])
    bins = total.T
    for chip in range(16):
        for pair in range(8):
            source = (chip * 8 + pair) * 16
            target = (pair * 16 + chip) * 16
            ordered[target:target + 16, :] = bins[source:source + 16, :]
    half = keep_ref.shape[0]
    c = place[2]
    keep_ref[...] = ordered[pl.ds(pl.multiple_of(c * half, half), half), :]
    send_ref[...] = ordered[pl.ds(pl.multiple_of((1 - c) * half, half), half), :].astype(BF16)


def finish_raw(place, raw, zero_points, w_keep, w_got):
    bins = raw.shape[1]
    units = zero_points.shape[0]
    whole = lambda i, p: (0, 0)
    return pl.pallas_call(
        finish_kernel,
        grid_spec=pltpu.PrefetchScalarGridSpec(
            num_scalar_prefetch=1,
            grid=(1,),
            in_specs=[
                pl.BlockSpec((MODES, bins), whole),
                pl.BlockSpec((units, bins), whole),
            ] + [pl.BlockSpec((units, MODES), whole)] * 4,
            out_specs=[pl.BlockSpec((bins // 2, MODES), whole)] * 2,
            scratch_shapes=[pltpu.VMEM((bins, MODES), F32)],
        ),
        out_shape=[
            jax.ShapeDtypeStruct((bins // 2, MODES), F32),
            jax.ShapeDtypeStruct((bins // 2, MODES), BF16),
        ],
        cost_estimate=pl.CostEstimate(
            flops=2 * units * bins * MODES, bytes_accessed=bins * MODES * 10, transcendentals=0
        ),
        name="finish_raw",
    )(place, raw, zero_points, w_keep, *w_got)


def quarter_kernel(axis, got_count, place, *refs):
    kept, got = refs[0], refs[1:1 + got_count]
    keep_ref, sends = refs[1 + got_count], refs[2 + got_count:5 + got_count]
    total = refs[5 + got_count]
    value = kept[...]
    for ref in got:
        value = value + ref[...].astype(F32)
    total[...] = value
    rows = keep_ref.shape[0]
    me = place[axis]
    keep_ref[...] = total[pl.ds(pl.multiple_of(me * rows, rows), rows), :]
    for k, ref in enumerate(sends):
        start = lax.rem(me + k + 1, 4) * rows
        ref[...] = total[pl.ds(pl.multiple_of(start, rows), rows), :].astype(ref.dtype)


def quarter(place, axis, kept, got, send_type):
    rows = kept.shape[0] // 4
    whole = lambda i, p: (0, 0)
    out = pl.pallas_call(
        functools.partial(quarter_kernel, axis, len(got)),
        grid_spec=pltpu.PrefetchScalarGridSpec(
            num_scalar_prefetch=1,
            grid=(1,),
            in_specs=[pl.BlockSpec(kept.shape, whole)] * (1 + len(got)),
            out_specs=[pl.BlockSpec((rows, MODES), whole)] * 4,
            scratch_shapes=[pltpu.VMEM(kept.shape, F32)],
        ),
        out_shape=[jax.ShapeDtypeStruct((rows, MODES), F32)]
        + [jax.ShapeDtypeStruct((rows, MODES), send_type)] * 3,
        name="quarter",
    )(place, kept, *got)
    return out[0], out[1:]


def invert_factor(matrix, out_ref, row0):
    lanes = 128
    tiles = 16
    row_in_tile = lax.broadcasted_iota(jnp.int32, (8, lanes), 0)
    rows = lax.broadcasted_iota(jnp.int32, (lanes, lanes), 0)
    cols = lax.broadcasted_iota(jnp.int32, (lanes, lanes), 1)
    unit = (rows == cols).astype(F32)
    work = [matrix[8 * i:8 * i + 8, :] for i in range(tiles)]
    inverse = [unit[8 * i:8 * i + 8, :] for i in range(tiles)]

    def spread(value):
        return jnp.broadcast_to(value, (8, lanes))

    for j in range(0, lanes, 2):
        tile, at = divmod(j, 8)
        r1, r2 = work[tile][at:at + 1, :], work[tile][at + 1:at + 2, :]
        x1, x2 = inverse[tile][at:at + 1, :], inverse[tile][at + 1:at + 2, :]
        a = jnp.broadcast_to(r1[:, j:j + 1], (1, lanes))
        b = jnp.broadcast_to(r1[:, j + 1:j + 2], (1, lanes))
        d = jnp.broadcast_to(r2[:, j + 1:j + 2], (1, lanes))
        det = a * d - b * b
        scale = 1.0 / det
        t1, t2 = spread((d * r1 - b * r2) * scale), spread((a * r2 - b * r1) * scale)
        u1, u2 = spread((d * x1 - b * x2) * scale), spread((a * x2 - b * x1) * scale)
        root = lax.rsqrt(a)
        out_ref[row0 + j:row0 + j + 1, :] = x1 * root
        out_ref[row0 + j + 1:row0 + j + 2, :] = (a * x2 - b * x1) * (root * lax.rsqrt(det))
        for i in range(tile, tiles):
            if i == tile:
                if at == 6:
                    continue
                below = row_in_tile > at + 1
                m1 = jnp.where(below, spread(work[i][:, j:j + 1]), 0.0)
                m2 = jnp.where(below, spread(work[i][:, j + 1:j + 2]), 0.0)
            else:
                m1, m2 = spread(work[i][:, j:j + 1]), spread(work[i][:, j + 1:j + 2])
            work[i] = work[i] - (m1 * t1 + m2 * t2)
            inverse[i] = inverse[i] - (m1 * u1 + m2 * u2)


def dot_plain(a, b):
    return jnp.dot(a, b, preferred_element_type=F32, precision=HIGHEST)


def basis_kernel(place, mine_ref, other_ref, high_ref, low_ref, out_ref, inverse_ref, top, bottom, inv_high, inv_low):
    @pl.when(pl.program_id(0) == 0)
    def _():
        first = place[2] == 0
        mine, other = mine_ref[...] * (1.0 / STARS), other_ref[...] * (1.0 / STARS)
        packed = jnp.concatenate(
            [jnp.where(first, mine, other), jnp.where(first, other, mine)], axis=0
        )
        invert_factor(packed[:128], top, 0)
        upper = top[...]
        lower = dot_last(packed[128:256], upper, HIGHEST)
        invert_factor(packed[256:] - dot_last(lower, lower, HIGHEST), bottom, 0)
        corner = bottom[...]
        left = -dot_plain(corner, dot_plain(lower, upper))
        inverse_ref[:128, :128] = upper
        inverse_ref[:128, 128:] = jnp.zeros_like(upper)
        inverse_ref[128:, :128] = left
        inverse_ref[128:, 128:] = corner
        high, low = split_low(inverse_ref[...])
        inv_high[...] = high
        inv_low[...] = low

    out_ref[...] = (
        dot_last(high_ref[...], inv_high[...])
        + dot_last(high_ref[...], inv_low[...])
        + dot_last(low_ref[...], inv_high[...])
    )


def basis(place, mine, other, high, low, tile=512):
    rows = high.shape[0]
    whole = lambda i, p: (0, 0)
    row = lambda i, p: (i, 0)
    return pl.pallas_call(
        basis_kernel,
        grid_spec=pltpu.PrefetchScalarGridSpec(
            num_scalar_prefetch=1,
            grid=(rows // tile,),
            in_specs=[
                pl.BlockSpec((192, 128), whole),
                pl.BlockSpec((192, 128), whole),
                pl.BlockSpec((tile, MODES), row),
                pl.BlockSpec((tile, MODES), row),
            ],
            out_specs=[
                pl.BlockSpec((tile, MODES), row),
                pl.BlockSpec((MODES, MODES), whole),
            ],
            scratch_shapes=[
                pltpu.VMEM((128, 128), F32),
                pltpu.VMEM((128, 128), F32),
                pltpu.VMEM((MODES, MODES), BF16),
                pltpu.VMEM((MODES, MODES), BF16),
            ],
        ),
        out_shape=[
            jax.ShapeDtypeStruct((rows, MODES), F32),
            jax.ShapeDtypeStruct((MODES, MODES), F32),
        ],
        cost_estimate=pl.CostEstimate(
            flops=2 * rows * MODES * MODES * 3 + (1 << 34), bytes_accessed=rows * MODES * 8, transcendentals=0
        ),
        name="basis",
    )(place, mine, other, high, low)


def modes_kernel(kept, got1, got2, got3, inverse_ref, out_ref):
    raw = (kept[...] + got1[...] + got2[...] + got3[...]) * (1.0 / STARS)
    out_ref[...] = dot_last(raw, inverse_ref[...], HIGHEST)


def modes(kept, got, inverse):
    return pl.pallas_call(
        modes_kernel,
        out_shape=jax.ShapeDtypeStruct(kept.shape, F32),
        name="modes",
    )(kept, *got, inverse)


def on_device(residuals, loadings, zero_points, sketch_matrix, use_lists):
    r = lax.axis_index("rows")
    y = lax.axis_index("units")
    place = jnp.stack([r // 8, (r // 2) % 4, r % 2, y]).astype(jnp.int32)
    own, half = project(place, zero_points, sketch_matrix)
    halves = shift_all("y", [half] * 3)
    swapped = [lax.ppermute(h, AXES, SWAP) for h in halves]
    part = sketch(residuals, sketch_matrix)
    high, low, gram_keep, gram_send, w_keep, *w_sends = correct(
        place, use_lists, part, loadings, own, halves, swapped
    )
    gram = gram_keep + lax.ppermute(gram_send, AXES, SWAP)
    w_got = shift_all("y", w_sends)
    raw = raw_sums(residuals, high)
    for axis in "yxz":
        one, two, three = shift_all(axis, [gram] * 3)
        gram = (gram + two) + (one + three)
    other = lax.ppermute(gram, AXES, SWAP)
    keep, send = finish_raw(place, raw, zero_points, w_keep, w_got)
    keep, sends = quarter(place, 3, keep, [lax.ppermute(send, AXES, SWAP)], BF16)
    keep, sends = quarter(place, 0, keep, shift_all("y", sends), F32)
    keep, sends = quarter(place, 1, keep, shift_all("x", sends), F32)
    got = shift_all("z", sends)
    star_basis, inverse = basis(place, gram, other, high, low)
    bin_modes = modes(keep, got, inverse)
    return (star_basis, bin_modes)


def solution(mesh):
    in_specs = (
        P(("rows", "units"), None),
        P(("rows", "units"), None),
        P("units", None),
        P(),
        P(("rows", "units"), None),
    )
    out_specs = (P(("rows", "units"), None), P(("rows", "units"), None))
    return jax.shard_map(
        on_device, mesh=mesh, in_specs=in_specs, out_specs=out_specs, check_vma=False
    )
```

time: 369 us -> 141 us (0.38); the launches traced: 364 us -> 140 us
  waiting for transfers between devices: 205 us -> 16.8 us
  Pallas kernels: 0 us -> 74.5 us
  other arithmetic: 59.4 us -> 1.63 us
  matrix products: 57.6 us -> 0 us
  starting transfers between devices: 0.08 us -> 41.2 us
  local copies, waits for them, and re-layouts: 26.4 us -> 5.46 us
  between operations: 15.9 us -> 0.88 us
    psum x1 -> x0, waiting for transfers between devices: 153 us -> none  [on_device(): lower_factor = jnp.linalg.cholesky(lax.psum(gram_local, ('rows', 'units')))]
    pallas_call x0 -> x10, Pallas kernels: none -> 74.5 us  [the longest x1 21.3 us: basis(): pl.pallas_call(basis_kernel, grid_spec=pltpu.PrefetchScalarGridSpec(num_s...]
    another operation x11 -> x1, other arithmetic: 57 us -> 0.65 us  [on_device(): place = jnp.stack([r // 8, r // 2 % 4, r % 2, y]).astype(jnp.int32)]
    all_gather x1 -> x0, waiting for transfers between devices: 51.5 us -> none  [on_device(): gathered = lax.all_gather(zero_points, 'units', axis=0, tiled=True)]
    dot_general x4 -> x0, matrix products: 47.2 us -> none  [the longest x1 23.4 us: on_device(): jnp.einsum('bsk,bkn->bsn', loadings.reshape(block_count, BLOCK_STARS, USE...]
    ppermute x0 -> x30, starting transfers between devices: none -> 41.2 us  [the longest x24 40.5 us: shift_all(): lax.ppermute(p, AXES, SHIFTS[axis][k])]
    ppermute x0 -> x30, waiting for transfers between devices: none -> 16.8 us  [the longest x24 16.8 us: shift_all(): lax.ppermute(p, AXES, SHIFTS[axis][k])]
    gather x1 -> x0, local copies, waits for them, and re-layouts: 14.9 us -> none  [on_device(): chosen = tables[use_lists].reshape(block_count, USES * GROUP, width_bins)]
  transfers between devices with their start and end apart: 2 -> 30, of which waited for: 2 -> 9; matrix products, arithmetic and copies ran while one was open for 0% -> 1% of each run, Pallas kernels for 0% -> 40%
where the time goes in v1:
time: 141 us; the launch traced here: 140 us
  Pallas kernels  74.5 us (53%)
  starting transfers between devices  41.2 us (29%)
  waiting for transfers between devices  16.8 us (12%)
  local copies, waits for them, and re-layouts  5.46 us (4%)
  other arithmetic  1.63 us (1%)
    ppermute x24, starting transfers between devices, shift_all(): lax.ppermute(p, AXES, SHIFTS[axis][k])  40.5 us
    pallas_call x1, Pallas kernels, basis(): pl.pallas_call(basis_kernel, grid_spec=pltpu.PrefetchScalarGridSpec(num_s...  21.3 us
    ppermute x24, waiting for transfers between devices, shift_all(): lax.ppermute(p, AXES, SHIFTS[axis][k])  16.8 us
    pallas_call x1, Pallas kernels, correct(): pl.pallas_call(functools.partial(correct_kernel, blocks), grid_spec=pltpu...  12.8 us
    pallas_call x1, Pallas kernels, sketch(): pl.pallas_call(sketch_kernel, grid=(rows // tile,), in_specs=[pl.BlockSpe...  12.2 us
    pallas_call x1, Pallas kernels, raw_sums(): pl.pallas_call(raw_kernel, grid=(rows // tile,), in_specs=[pl.BlockSpec((...  10.2 us
    pallas_call x3, Pallas kernels, quarter(): pl.pallas_call(functools.partial(quarter_kernel, axis, len(got)), grid_sp...  7.85 us
    unnamed x45, local copies, waits for them, and re-layouts  5.46 us
  transfers between devices with their start and end apart: 30, of which 9 were waited for; matrix products, arithmetic and copies ran while one was open for 1% of the time, Pallas kernels for 40%

profile of v1, /device:TPU:0, one launch (start us, length us, event | category | flops | bytes accessed | tf_op | source)
XLA Modules:
  0.0 140.5 jit_solution(5262631759857752186)
XLA Ops:
  1.3 3.4 %project.1 = (f32[256,256]{1,0:T(8,128)}, f32[128,256]{1,0:T(8,128)}) custom-call(s32[4]{0:T(128)} %pad_add_fusion.place, bf16[256,2048]{1,0:T(8,128)(2,1)} %zero_ref.3, bf16[2048,256]{1,0:T(8,128)(2,1)} %sketch_ref.3), custom_call_target="tpu_custom_call" | custom-call | tf_op jit(solution)/shard_map/project/pallas_call | solution.py:68
  6.4 2.9 %collective-permute-start.2 = (f32[128,256]{1,0:T(8,128)}, f32[128,256]{1,0:T(8,128)S(1)}, u32[]{:S(2)}, u32[]{:S(2)}) collective-permute-start(f32[128,256]{1,0:T(8,128)} %get-tuple-element.29), channel_id=1, source_target_pairs={{0,2},{1,3},{2,0},{3,1},{4,6},{5,7},{6,4},{7,5},{8,10},{9,11},{10,... | collective-permute-start | bytes 393224 | tf_op jit(solution)/shard_map/ppermute | solution.py:57
  11.5 4.0 %collective-permute-done.2.ha2 = f32[128,256]{1,0:T(8,128)S(1)} collective-permute-done((f32[128,256]{1,0:T(8,128)}, f32[128,256]{1,0:T(8,128)S(1)}, u32[]{:S(2)}, u32[]{:S(2)}) %collective-permute-start.2) | collective-permute-done | bytes 131104 | tf_op jit(solution)/shard_map/ppermute | solution.py:57
  16.0 12.2 %sketch.1.part_ref = f32[4096,256]{1,0:T(8,128)} custom-call(bf16[4096,2048]{1,0:T(8,128)(2,1)} %res_ref.3, bf16[2048,256]{1,0:T(8,128)(2,1)} %sketch_ref.3), custom_call_target="tpu_custom_call" | custom-call | flops 4294967296 | bytes 20971520 | tf_op jit(solution)/shard_map/sketch/pallas_call | solution.py:96
  29.7 12.8 %correct.1 = (bf16[4096,256]{1,0:T(8,128)(2,1)}, bf16[4096,256]{1,0:T(8,128)(2,1)}, f32[192,128]{1,0:T(8,128)}, f32[192,128]{1,0:T(8,128)}, f32[256,256]{1,0:T(8...) custom-call(s32[4]{0:T(128)} %pad_add_fusion.place, s32[32,4]{1,0:T(8,128)} %copy.7.uses, ...), custom_call_target="tpu_custom_call" | custom-call | flops 2684354560 | bytes 10485760 | tf_op jit(solution)/shard_map/correct/pallas_call | solution.py:177
  43.5 2.4 %collective-permute-start.18 = (bf16[256,256]{1,0:T(8,128)(2,1)}, bf16[256,256]{1,0:T(8,128)(2,1)S(1)}, u32[]{:S(2)}, u32[]{:S(2)}) collective-permute-start(bf16[256,256]{1,0:T(8,128)(2,1)} %get-tuple-element.37), channel_id=1, source_target_pairs={{0,2},{1,3},{2,0},{3,1},{4,6},{5,7},{6,4},{7,5},{8,10},{9,11},{10,... | collective-permute-start | bytes 393224 | tf_op jit(solution)/shard_map/ppermute | solution.py:57
  49.7 3.2 %collective-permute-start.9 = (f32[192,128]{1,0:T(8,128)S(1)}, f32[192,128]{1,0:T(8,128)S(1)}, u32[]{:S(2)}, u32[]{:S(2)}) collective-permute-start(f32[192,128]{1,0:T(8,128)S(1)} %add.41), channel_id=1, source_target_pairs={{0,3},{1,0},{2,1},{3,2},{4,7},{5,4},{6,5},{7,6},{8,11},{9,8},{10,9... | collective-permute-start | bytes 294920 | tf_op jit(solution)/shard_map/ppermute | solution.py:57
  53.0 10.2 %raw_sums.1.raw_ref = f32[256,2048]{1,0:T(8,128)} custom-call(bf16[4096,2048]{1,0:T(8,128)(2,1)} %res_ref.3, bf16[4096,256]{1,0:T(8,128)(2,1)} %get-tuple-element.32.high_ref), custom_call_target="tpu_custom_call" | custom-call | flops 4294967296 | bytes 18874368 | tf_op jit(solution)/shard_map/raw_sums/pallas_call | solution.py:225
  63.9 4.8 %finish_raw.1 = (f32[1024,256]{1,0:T(8,128)}, bf16[1024,256]{1,0:T(8,128)(2,1)}) custom-call(s32[4]{0:T(128)} %pad_add_fusion.place, f32[256,2048]{1,0:T(8,128)} %raw_sums.1.raw_ref, bf16[256,2048]{1,0:T(8,128)(2,1)} %zero_ref.3, f32[256,256]{1,0:T(8,128)} %get-tuple-element.35.w_keep, bf16[256,256]{1,0:T(8,128)(2,1)} %copy-done.1, ...), custom_call_target="tpu_custom_call" | custom-call | flops 268435456 | bytes 5242880 | tf_op jit(solution)/shard_map/finish_raw/pallas_call | solution.py:260
  68.8 3.1 %collective-permute-start.10 = (f32[192,128]{1,0:T(8,128)S(1)}, f32[192,128]{1,0:T(8,128)S(1)}, u32[]{:S(2)}, u32[]{:S(2)}) collective-permute-start(f32[192,128]{1,0:T(8,128)S(1)} %add_add_fusion.2), channel_id=1, source_target_pairs={{0,64},{1,65},{2,66},{3,67},{4,68},{5,69},{6,70},{7,71},{8,72},{9,... | collective-permute-start | bytes 294920 | tf_op jit(solution)/shard_map/ppermute | solution.py:57
  72.4 2.6 %collective-permute-start.12 = (f32[192,128]{1,0:T(8,128)S(1)}, f32[192,128]{1,0:T(8,128)S(1)}, u32[]{:S(2)}, u32[]{:S(2)}) collective-permute-start(f32[192,128]{1,0:T(8,128)S(1)} %add_add_fusion.2), channel_id=1, source_target_pairs={{0,96},{1,97},{2,98},{3,99},{4,100},{5,101},{6,102},{7,103},{8,104... | collective-permute-start | bytes 294920 | tf_op jit(solution)/shard_map/ppermute | solution.py:57
  75.8 2.2 %collective-permute-done.11 = f32[192,128]{1,0:T(8,128)S(1)} collective-permute-done((f32[192,128]{1,0:T(8,128)S(1)}, f32[192,128]{1,0:T(8,128)S(1)}, u32[]{:S(2)}, u32[]{:S(2)}) %collective-permute-start.11) | collective-permute-done | bytes 98336 | tf_op jit(solution)/shard_map/ppermute | solution.py:57
  78.0 4.0 %collective-permute-start.13 = (f32[192,128]{1,0:T(8,128)S(1)}, f32[192,128]{1,0:T(8,128)S(1)}, u32[]{:S(2)}, u32[]{:S(2)}) collective-permute-start(f32[192,128]{1,0:T(8,128)S(1)} %add_add_fusion.1), channel_id=1, source_target_pairs={{0,16},{1,17},{2,18},{3,19},{4,20},{5,21},{6,22},{7,23},{8,24},{9,... | collective-permute-start | bytes 294920 | tf_op jit(solution)/shard_map/ppermute | solution.py:57
  83.0 2.2 %collective-permute-start.15 = (f32[192,128]{1,0:T(8,128)S(1)}, f32[192,128]{1,0:T(8,128)S(1)}, u32[]{:S(2)}, u32[]{:S(2)}) collective-permute-start(f32[192,128]{1,0:T(8,128)S(1)} %add_add_fusion.1), channel_id=1, source_target_pairs={{0,24},{1,25},{2,26},{3,27},{4,28},{5,29},{6,30},{7,31},{8,0},{9,1... | collective-permute-start | bytes 294920 | tf_op jit(solution)/shard_map/ppermute | solution.py:57
  86.0 3.0 %quarter.3 = (f32[256,256]{1,0:T(8,128)}, bf16[256,256]{1,0:T(8,128)(2,1)}, bf16[256,256]{1,0:T(8,128)(2,1)}, bf16[256,256]{1,0:T(8,128)(2,1)}) custom-call(s32[4]{0:T(128)} %pad_add_fusion.place, f32[1024,256]{1,0:T(8,128)} %get-tuple-element.39.refs_0_, bf16[1024,256]{1,0:T(8,128)(2,1)} %copy-done), custom_call_target="tpu_custom_call" | custom-call | tf_op jit(solution)/shard_map/quarter/pallas_call | solution.py:302
  89.0 2.1 %collective-permute-start.22 = (bf16[256,256]{1,0:T(8,128)(2,1)}, bf16[256,256]{1,0:T(8,128)(2,1)S(1)}, u32[]{:S(2)}, u32[]{:S(2)}) collective-permute-start(bf16[256,256]{1,0:T(8,128)(2,1)} %get-tuple-element.43), channel_id=1, source_target_pairs={{0,2},{1,3},{2,0},{3,1},{4,6},{5,7},{6,4},{7,5},{8,10},{9,11},{10,... | collective-permute-start | bytes 393224 | tf_op jit(solution)/shard_map/ppermute | solution.py:57
  92.9 4.3 %collective-permute-done.21.refs_1_ = bf16[256,256]{1,0:T(8,128)(2,1)S(1)} collective-permute-done((bf16[256,256]{1,0:T(8,128)(2,1)}, bf16[256,256]{1,0:T(8,128)(2,1)S(1)}, u32[]{:S(2)}, u32[]{:S(2)}) %collective-permute-start.21) | collective-permute-done | bytes 131104 | tf_op jit(solution)/shard_map/ppermute | solution.py:57
  98.5 2.6 %quarter.4 = (f32[64,256]{1,0:T(8,128)}, f32[64,256]{1,0:T(8,128)}, f32[64,256]{1,0:T(8,128)}, f32[64,256]{1,0:T(8,128)}) custom-call(s32[4]{0:T(128)} %pad_add_fusion.place, f32[256,256]{1,0:T(8,128)} %get-tuple-element.41.refs_0_, bf16[256,256]{1,0:T(8,128)(2,1)} %copy-done.4, bf16[256,256]{1,0:T(8,128)(2,1)} %copy-done.5, bf16[256,256]{1,0:T(8,128)(2,1)} %copy-done.6), custom_call_target="tpu_custom_call" | custom-call | tf_op jit(solution)/shard_map/quarter/pallas_call | solution.py:302
  101.1 1.8 %collective-permute-start.24 = (f32[64,256]{1,0:T(8,128)}, f32[64,256]{1,0:T(8,128)S(1)}, u32[]{:S(2)}, u32[]{:S(2)}) collective-permute-start(f32[64,256]{1,0:T(8,128)} %get-tuple-element.46), channel_id=1, source_target_pairs={{0,32},{1,33},{2,34},{3,35},{4,36},{5,37},{6,38},{7,39},{8,40},{9,... | collective-permute-start | bytes 196616 | tf_op jit(solution)/shard_map/ppermute | solution.py:57
  102.9 2.5 %collective-permute-start.25 = (f32[64,256]{1,0:T(8,128)}, f32[64,256]{1,0:T(8,128)S(1)}, u32[]{:S(2)}, u32[]{:S(2)}) collective-permute-start(f32[64,256]{1,0:T(8,128)} %get-tuple-element.47), channel_id=1, source_target_pairs={{0,64},{1,65},{2,66},{3,67},{4,68},{5,69},{6,70},{7,71},{8,72},{9,... | collective-permute-start | bytes 196616 | tf_op jit(solution)/shard_map/ppermute | solution.py:57
  107.0 1.8 %collective-permute-done.25.refs_2_ = f32[64,256]{1,0:T(8,128)S(1)} collective-permute-done((f32[64,256]{1,0:T(8,128)}, f32[64,256]{1,0:T(8,128)S(1)}, u32[]{:S(2)}, u32[]{:S(2)}) %collective-permute-start.25) | collective-permute-done | bytes 65568 | tf_op jit(solution)/shard_map/ppermute | solution.py:57
  110.4 2.2 %quarter.5 = (f32[16,256]{1,0:T(8,128)}, f32[16,256]{1,0:T(8,128)}, f32[16,256]{1,0:T(8,128)}, f32[16,256]{1,0:T(8,128)}) custom-call(s32[4]{0:T(128)} %pad_add_fusion.place, f32[64,256]{1,0:T(8,128)} %get-tuple-element.45.refs_0_, f32[64,256]{1,0:T(8,128)} %copy-done.8, f32[64,256]{1,0:T(8,128)} %copy-done.9, f32[64,256]{1,0:T(8,128)} %copy-done.10), custom_call_target="tpu_custom_call" | custom-call | tf_op jit(solution)/shard_map/quarter/pallas_call | solution.py:302
  116.6 21.3 %basis.1 = (f32[4096,256]{1,0:T(8,128)}, f32[256,256]{1,0:T(8,128)}) custom-call(s32[4]{0:T(128)} %pad_add_fusion.place, f32[192,128]{1,0:T(8,128)} %copy-done.7, f32[192,128]{1,0:T(8,128)} %copy-done.21, bf16[4096,256]{1,0:T(8,128)(2,1)} %get-tuple-element.32.high_ref, bf16[4096,256]{1,0:T(8,128)(2,1)} %get-tuple-element.33.low_ref), custom_call_target="tpu_custom_call" | custom-call | flops 18790481920 | bytes 8388608 | tf_op jit(solution)/shard_map/basis/pallas_call | solution.py:395
  138.5 1.9 %modes.1 = f32[16,256]{1,0:T(8,128)} custom-call(f32[16,256]{1,0:T(8,128)} %get-tuple-element.49.kept, f32[16,256]{1,0:T(8,128)} %copy-done.11, f32[16,256]{1,0:T(8,128)} %copy-done.12, f32[16,256]{1,0:T(8,128)} %copy-done.13, f32[256,256]{1,0:T(8,128)} %get-tuple-element.53.inverse_ref), custom_call_target="tpu_custom_call" | custom-call | tf_op jit(solution)/shard_map/modes/pallas_call | solution.py:434
  (96 shorter events, 26.1 us)
Async XLA Ops:
  4.7 6.8 %collective-permute-start = (f32[128,256]{1,0:T(8,128)}, f32[128,256]{1,0:T(8,128)S(1)}, u32[]{:S(2)}, u32[]{:S(2)}) collective-permute-start(f32[128,256]{1,0:T(8,128)} %get-tuple-element.29), channel_id=1, source_target_pairs={{0,1},{1,2},{2,3},{3,0},{4,5},{5,6},{6,7},{7,4},{8,9},{9,10},{10,1... | collective-permute-start | bytes 393224 | tf_op jit(solution)/shard_map/ppermute | solution.py:57
  6.4 9.1 %collective-permute-start.2 = (f32[128,256]{1,0:T(8,128)}, f32[128,256]{1,0:T(8,128)S(1)}, u32[]{:S(2)}, u32[]{:S(2)}) collective-permute-start(f32[128,256]{1,0:T(8,128)} %get-tuple-element.29), channel_id=1, source_target_pairs={{0,2},{1,3},{2,0},{3,1},{4,6},{5,7},{6,4},{7,5},{8,10},{9,11},{10,... | collective-permute-start | bytes 393224 | tf_op jit(solution)/shard_map/ppermute | solution.py:57
  9.3 6.2 %collective-permute-start.4 = (f32[128,256]{1,0:T(8,128)}, f32[128,256]{1,0:T(8,128)S(1)}, u32[]{:S(2)}, u32[]{:S(2)}) collective-permute-start(f32[128,256]{1,0:T(8,128)} %get-tuple-element.29), channel_id=1, source_target_pairs={{0,3},{1,0},{2,1},{3,2},{4,7},{5,4},{6,5},{7,6},{8,11},{9,8},{10,9... | collective-permute-start | bytes 393224 | tf_op jit(solution)/shard_map/ppermute | solution.py:57
  11.5 17.4 %collective-permute-start.1 = (f32[128,256]{1,0:T(8,128)S(1)}, f32[128,256]{1,0:T(8,128)S(1)}, u32[]{:S(2)}, u32[]{:S(2)}) collective-permute-start(f32[128,256]{1,0:T(8,128)S(1)} %collective-permute-done.ha1), channel_id=1, source_target_pairs={{0,4},{1,5},{2,6},{3,7},{4,0},{5,1},{6,2},{7,3},{8,12},{9,13},{10,... | collective-permute-start | bytes 393224 | tf_op jit(solution)/shard_map/ppermute | solution.py:447
  15.5 13.4 %collective-permute-start.3 = (f32[128,256]{1,0:T(8,128)S(1)}, f32[128,256]{1,0:T(8,128)S(1)}, u32[]{:S(2)}, u32[]{:S(2)}) collective-permute-start(f32[128,256]{1,0:T(8,128)S(1)} %collective-permute-done.2.ha2), channel_id=1, source_target_pairs={{0,4},{1,5},{2,6},{3,7},{4,0},{5,1},{6,2},{7,3},{8,12},{9,13},{10,... | collective-permute-start | bytes 393224 | tf_op jit(solution)/shard_map/ppermute | solution.py:447
  15.6 13.4 %collective-permute-start.5 = (f32[128,256]{1,0:T(8,128)S(1)}, f32[128,256]{1,0:T(8,128)S(1)}, u32[]{:S(2)}, u32[]{:S(2)}) collective-permute-start(f32[128,256]{1,0:T(8,128)S(1)} %collective-permute-done.4.ha3), channel_id=1, source_target_pairs={{0,4},{1,5},{2,6},{3,7},{4,0},{5,1},{6,2},{7,3},{8,12},{9,13},{10,... | collective-permute-start | bytes 393224 | tf_op jit(solution)/shard_map/ppermute | solution.py:447
  42.5 7.2 %collective-permute-start.17 = (bf16[256,256]{1,0:T(8,128)(2,1)}, bf16[256,256]{1,0:T(8,128)(2,1)S(1)}, u32[]{:S(2)}, u32[]{:S(2)}) collective-permute-start(bf16[256,256]{1,0:T(8,128)(2,1)} %get-tuple-element.36), channel_id=1, source_target_pairs={{0,1},{1,2},{2,3},{3,0},{4,5},{5,6},{6,7},{7,4},{8,9},{9,10},{10,1... | collective-permute-start | bytes 393224 | tf_op jit(solution)/shard_map/ppermute | solution.py:57
  43.5 19.7 %collective-permute-start.18 = (bf16[256,256]{1,0:T(8,128)(2,1)}, bf16[256,256]{1,0:T(8,128)(2,1)S(1)}, u32[]{:S(2)}, u32[]{:S(2)}) collective-permute-start(bf16[256,256]{1,0:T(8,128)(2,1)} %get-tuple-element.37), channel_id=1, source_target_pairs={{0,2},{1,3},{2,0},{3,1},{4,6},{5,7},{6,4},{7,5},{8,10},{9,11},{10,... | collective-permute-start | bytes 393224 | tf_op jit(solution)/shard_map/ppermute | solution.py:57
  45.9 17.3 %collective-permute-start.19 = (bf16[256,256]{1,0:T(8,128)(2,1)}, bf16[256,256]{1,0:T(8,128)(2,1)S(1)}, u32[]{:S(2)}, u32[]{:S(2)}) collective-permute-start(bf16[256,256]{1,0:T(8,128)(2,1)} %get-tuple-element.38), channel_id=1, source_target_pairs={{0,3},{1,0},{2,1},{3,2},{4,7},{5,4},{6,5},{7,6},{8,11},{9,8},{10,9... | collective-permute-start | bytes 393224 | tf_op jit(solution)/shard_map/ppermute | solution.py:57
  48.4 20.3 %collective-permute-start.7 = (f32[192,128]{1,0:T(8,128)S(1)}, f32[192,128]{1,0:T(8,128)S(1)}, u32[]{:S(2)}, u32[]{:S(2)}) collective-permute-start(f32[192,128]{1,0:T(8,128)S(1)} %add.41), channel_id=1, source_target_pairs={{0,2},{1,3},{2,0},{3,1},{4,6},{5,7},{6,4},{7,5},{8,10},{9,11},{10,... | collective-permute-start | bytes 294920 | tf_op jit(solution)/shard_map/ppermute | solution.py:57
  49.7 19.0 %collective-permute-start.8 = (f32[192,128]{1,0:T(8,128)S(1)}, f32[192,128]{1,0:T(8,128)S(1)}, u32[]{:S(2)}, u32[]{:S(2)}) collective-permute-start(f32[192,128]{1,0:T(8,128)S(1)} %add.41), channel_id=1, source_target_pairs={{0,1},{1,2},{2,3},{3,0},{4,5},{5,6},{6,7},{7,4},{8,9},{9,10},{10,1... | collective-permute-start | bytes 294920 | tf_op jit(solution)/shard_map/ppermute | solution.py:57
  49.7 19.0 %collective-permute-start.9 = (f32[192,128]{1,0:T(8,128)S(1)}, f32[192,128]{1,0:T(8,128)S(1)}, u32[]{:S(2)}, u32[]{:S(2)}) collective-permute-start(f32[192,128]{1,0:T(8,128)S(1)} %add.41), channel_id=1, source_target_pairs={{0,3},{1,0},{2,1},{3,2},{4,7},{5,4},{6,5},{7,6},{8,11},{9,8},{10,9... | collective-permute-start | bytes 294920 | tf_op jit(solution)/shard_map/ppermute | solution.py:57
  68.7 16.5 %collective-permute-start.20 = (bf16[1024,256]{1,0:T(8,128)(2,1)}, bf16[1024,256]{1,0:T(8,128)(2,1)S(1)}, u32[]{:S(2)}, u32[]{:S(2)}) collective-permute-start(bf16[1024,256]{1,0:T(8,128)(2,1)} %get-tuple-element.40), channel_id=1, source_target_pairs={{0,4},{1,5},{2,6},{3,7},{4,0},{5,1},{6,2},{7,3},{8,12},{9,13},{10,... | collective-permute-start | bytes 1572872 | tf_op jit(solution)/shard_map/ppermute | solution.py:460
  68.8 7.1 %collective-permute-start.10 = (f32[192,128]{1,0:T(8,128)S(1)}, f32[192,128]{1,0:T(8,128)S(1)}, u32[]{:S(2)}, u32[]{:S(2)}) collective-permute-start(f32[192,128]{1,0:T(8,128)S(1)} %add_add_fusion.2), channel_id=1, source_target_pairs={{0,64},{1,65},{2,66},{3,67},{4,68},{5,69},{6,70},{7,71},{8,72},{9,... | collective-permute-start | bytes 294920 | tf_op jit(solution)/shard_map/ppermute | solution.py:57
  78.0 13.1 %collective-permute-start.13 = (f32[192,128]{1,0:T(8,128)S(1)}, f32[192,128]{1,0:T(8,128)S(1)}, u32[]{:S(2)}, u32[]{:S(2)}) collective-permute-start(f32[192,128]{1,0:T(8,128)S(1)} %add_add_fusion.1), channel_id=1, source_target_pairs={{0,16},{1,17},{2,18},{3,19},{4,20},{5,21},{6,22},{7,23},{8,24},{9,... | collective-permute-start | bytes 294920 | tf_op jit(solution)/shard_map/ppermute | solution.py:57
  82.0 10.8 %collective-permute-start.14 = (f32[192,128]{1,0:T(8,128)S(1)}, f32[192,128]{1,0:T(8,128)S(1)}, u32[]{:S(2)}, u32[]{:S(2)}) collective-permute-start(f32[192,128]{1,0:T(8,128)S(1)} %add_add_fusion.1), channel_id=1, source_target_pairs={{0,8},{1,9},{2,10},{3,11},{4,12},{5,13},{6,14},{7,15},{8,16},{9,17... | collective-permute-start | bytes 294920 | tf_op jit(solution)/shard_map/ppermute | solution.py:57
  83.0 9.8 %collective-permute-start.15 = (f32[192,128]{1,0:T(8,128)S(1)}, f32[192,128]{1,0:T(8,128)S(1)}, u32[]{:S(2)}, u32[]{:S(2)}) collective-permute-start(f32[192,128]{1,0:T(8,128)S(1)} %add_add_fusion.1), channel_id=1, source_target_pairs={{0,24},{1,25},{2,26},{3,27},{4,28},{5,29},{6,30},{7,31},{8,0},{9,1... | collective-permute-start | bytes 294920 | tf_op jit(solution)/shard_map/ppermute | solution.py:57
  89.0 8.2 %collective-permute-start.21 = (bf16[256,256]{1,0:T(8,128)(2,1)}, bf16[256,256]{1,0:T(8,128)(2,1)S(1)}, u32[]{:S(2)}, u32[]{:S(2)}) collective-permute-start(bf16[256,256]{1,0:T(8,128)(2,1)} %get-tuple-element.42), channel_id=1, source_target_pairs={{0,1},{1,2},{2,3},{3,0},{4,5},{5,6},{6,7},{7,4},{8,9},{9,10},{10,1... | collective-permute-start | bytes 393224 | tf_op jit(solution)/shard_map/ppermute | solution.py:57
  89.0 8.2 %collective-permute-start.22 = (bf16[256,256]{1,0:T(8,128)(2,1)}, bf16[256,256]{1,0:T(8,128)(2,1)S(1)}, u32[]{:S(2)}, u32[]{:S(2)}) collective-permute-start(bf16[256,256]{1,0:T(8,128)(2,1)} %get-tuple-element.43), channel_id=1, source_target_pairs={{0,2},{1,3},{2,0},{3,1},{4,6},{5,7},{6,4},{7,5},{8,10},{9,11},{10,... | collective-permute-start | bytes 393224 | tf_op jit(solution)/shard_map/ppermute | solution.py:57
  91.1 6.7 %collective-permute-start.23 = (bf16[256,256]{1,0:T(8,128)(2,1)}, bf16[256,256]{1,0:T(8,128)(2,1)S(1)}, u32[]{:S(2)}, u32[]{:S(2)}) collective-permute-start(bf16[256,256]{1,0:T(8,128)(2,1)} %get-tuple-element.44), channel_id=1, source_target_pairs={{0,3},{1,0},{2,1},{3,2},{4,7},{5,4},{6,5},{7,6},{8,11},{9,8},{10,9... | collective-permute-start | bytes 393224 | tf_op jit(solution)/shard_map/ppermute | solution.py:57
  92.8 23.1 %collective-permute-start.16 = (f32[192,128]{1,0:T(8,128)S(1)}, f32[192,128]{1,0:T(8,128)S(1)}, u32[]{:S(2)}, u32[]{:S(2)}) collective-permute-start(f32[192,128]{1,0:T(8,128)S(1)} %add_add_fusion.mine_ref), channel_id=1, source_target_pairs={{0,4},{1,5},{2,6},{3,7},{4,0},{5,1},{6,2},{7,3},{8,12},{9,13},{10,... | collective-permute-start | bytes 294920 | tf_op jit(solution)/shard_map/ppermute | solution.py:458
  112.7 25.2 %collective-permute-start.27 = (f32[16,256]{1,0:T(8,128)}, f32[16,256]{1,0:T(8,128)S(1)}, u32[]{:S(2)}, u32[]{:S(2)}) collective-permute-start(f32[16,256]{1,0:T(8,128)} %get-tuple-element.50), channel_id=1, source_target_pairs={{0,8},{1,9},{2,10},{3,11},{4,12},{5,13},{6,14},{7,15},{8,16},{9,17... | collective-permute-start | bytes 49160 | tf_op jit(solution)/shard_map/ppermute | solution.py:57
  112.7 25.2 %collective-permute-start.28 = (f32[16,256]{1,0:T(8,128)}, f32[16,256]{1,0:T(8,128)S(1)}, u32[]{:S(2)}, u32[]{:S(2)}) collective-permute-start(f32[16,256]{1,0:T(8,128)} %get-tuple-element.51), channel_id=1, source_target_pairs={{0,16},{1,17},{2,18},{3,19},{4,20},{5,21},{6,22},{7,23},{8,24},{9,... | collective-permute-start | bytes 49160 | tf_op jit(solution)/shard_map/ppermute | solution.py:57
  114.3 23.6 %collective-permute-start.29 = (f32[16,256]{1,0:T(8,128)}, f32[16,256]{1,0:T(8,128)S(1)}, u32[]{:S(2)}, u32[]{:S(2)}) collective-permute-start(f32[16,256]{1,0:T(8,128)} %get-tuple-element.52), channel_id=1, source_target_pairs={{0,24},{1,25},{2,26},{3,27},{4,28},{5,29},{6,30},{7,31},{8,0},{9,1... | collective-permute-start | bytes 49160 | tf_op jit(solution)/shard_map/ppermute | solution.py:57
  (28 other events, 147.5 us)

commit v2 on v0

v2 whole, which is shorter than its diff:
```python
import functools

import jax
import jax.numpy as jnp
from jax import lax
from jax.experimental import pallas as pl
from jax.experimental.pallas import tpu as pltpu
from jax.sharding import PartitionSpec as P

GROUP = 64
USES = 4
BLOCK_STARS = 128
MODES = 256
STARS = 524288
AXES = ("rows", "units")
F32 = jnp.float32
BF16 = jnp.bfloat16
HIGHEST = lax.Precision.HIGHEST


def split_low(value):
    high = value.astype(BF16)
    return high, (value - high.astype(F32)).astype(BF16)


def dot_rows(a, b):
    return lax.dot_general(a, b, (((0,), (0,)), ((), ())), preferred_element_type=F32)


def dot_last(a, b, precision=None):
    return lax.dot_general(
        a, b, (((1,), (1,)), ((), ())), preferred_element_type=F32, precision=precision
    )


def permutation(move):
    pairs = []
    for x in range(4):
        for z in range(4):
            for c in range(2):
                for y in range(4):
                    u, w, d, v = move(x, z, c, y)
                    pairs.append((((x * 4 + z) * 2 + c) * 4 + y, ((u * 4 + w) * 2 + d) * 4 + v))
    return pairs


SWAP = permutation(lambda x, z, c, y: (x, z, 1 - c, y))
SHIFTS = {
    "x": [permutation(lambda x, z, c, y, k=k: ((x + k) % 4, z, c, y)) for k in (1, 2, 3)],
    "y": [permutation(lambda x, z, c, y, k=k: (x, z, c, (y + k) % 4)) for k in (1, 2, 3)],
    "z": [permutation(lambda x, z, c, y, k=k: (x, (z + k) % 4, c, y)) for k in (1, 2, 3)],
}


def shift_all(axis, pieces):
    return [lax.ppermute(p, AXES, SHIFTS[axis][k]) for k, p in enumerate(pieces)]


def on_chip(shape, kind=F32):
    return pltpu.VMEM(shape, kind)


def resident(kernel, name, scalars, arrays, outs, scratch=(), flops=0, limit=16, out_specs=None):
    vmem = pl.BlockSpec(memory_space=pltpu.VMEM)
    smem = pl.BlockSpec(memory_space=pltpu.SMEM)
    arrays = [pltpu.with_memory_space_constraint(a, pltpu.VMEM) for a in arrays]
    return pl.pallas_call(
        kernel,
        in_specs=[smem] * len(scalars) + [vmem] * len(arrays),
        out_specs=out_specs or [vmem] * len(outs),
        out_shape=list(outs),
        scratch_shapes=list(scratch),
        compiler_params=pltpu.CompilerParams(vmem_limit_bytes=limit << 20),
        cost_estimate=pl.CostEstimate(flops=flops, bytes_accessed=1 << 16, transcendentals=0),
        name=name,
    )(*scalars, *arrays)


def project_kernel(place, zero_ref, sketch_ref, full_ref, half_ref):
    full_ref[...] = jnp.dot(zero_ref[...], sketch_ref[...], preferred_element_type=F32)
    half = full_ref.shape[0] // 2
    half_ref[...] = full_ref[pl.ds(pl.multiple_of(place[2] * half, half), half), :]


def sketch_kernel(tile, res_ref, sketch_ref, out_ref):
    def body(i, carry):
        rows = pl.ds(pl.multiple_of(i * tile, tile), tile)
        out_ref[rows, :] = jnp.dot(res_ref[rows, :], sketch_ref[...], preferred_element_type=F32)
        return carry

    lax.fori_loop(0, res_ref.shape[0] // tile, body, 0)


def correct_kernel(blocks, place, uses, part_ref, load_ref, own_ref, half_ref, other_ref,
                   high_ref, low_ref, gram_keep, gram_send, w_keep, w_send1, w_send2, w_send3,
                   table_high, table_low, gram_hh, gram_hl, weights):
    units = own_ref.shape[0]
    half = units // 2
    tile = blocks * BLOCK_STARS
    y, c = place[3], place[2]
    gram_hh[...] = jnp.zeros_like(gram_hh)
    gram_hl[...] = jnp.zeros_like(gram_hl)
    weights[...] = jnp.zeros_like(weights)

    def put(start, value):
        high, low = split_low(value)
        rows = pl.ds(pl.multiple_of(start, 128), value.shape[0])
        table_high[rows, :] = high
        table_low[rows, :] = low

    put(y * units, own_ref[...])
    for k in range(3):
        base = lax.rem(y + 3 - k, 4) * units
        put(base + c * half, half_ref[k * half:(k + 1) * half, :])
        put(base + (1 - c) * half, other_ref[k * half:(k + 1) * half, :])

    def step(i, carry):
        for block in range(blocks):
            rows = pl.ds(pl.multiple_of(i * tile + block * BLOCK_STARS, BLOCK_STARS), BLOCK_STARS)
            groups = [uses[use, i * blocks + block] for use in range(USES)]
            starts = [pl.multiple_of(g * GROUP, GROUP) for g in groups]
            load = load_ref[rows, :]
            high_table = jnp.concatenate([table_high[pl.ds(s, GROUP), :] for s in starts], axis=0)
            low_table = jnp.concatenate([table_low[pl.ds(s, GROUP), :] for s in starts], axis=0)
            offset = jnp.dot(load, high_table, preferred_element_type=F32)
            offset = offset + jnp.dot(load, low_table, preferred_element_type=F32)
            high, low = split_low(part_ref[rows, :] - offset)
            high_ref[rows, :] = high
            low_ref[rows, :] = low
            product = dot_rows(load, high)
            for use in range(USES):
                weights[pl.ds(starts[use], GROUP), :] += product[use * GROUP:(use + 1) * GROUP, :]
        rows = pl.ds(pl.multiple_of(i * tile, tile), tile)
        gram_hh[...] += dot_rows(high_ref[rows, :], high_ref[rows, :])
        gram_hl[...] += dot_rows(high_ref[rows, :], low_ref[rows, :])
        return carry

    lax.fori_loop(0, part_ref.shape[0] // tile, step, 0)
    cross = gram_hl[...]
    gram = gram_hh[...] + cross + cross.T
    packed = jnp.concatenate([gram[:128, :128], gram[128:, :128], gram[128:, 128:]], axis=0)
    zero = jnp.concatenate([packed[:96], packed[96:192]], axis=1)
    one = jnp.concatenate([packed[192:288], packed[288:]], axis=1)
    first = c == 0
    gram_keep[...] = jnp.where(first, zero, one)
    gram_send[...] = jnp.where(first, one, zero)
    w_keep[...] = weights[pl.ds(pl.multiple_of(y * units, 256), units), :]
    for k, ref in enumerate((w_send1, w_send2, w_send3)):
        base = lax.rem(y + k + 1, 4) * units
        ref[...] = weights[pl.ds(pl.multiple_of(base, 256), units), :].astype(BF16)


def raw_kernel(tile, res_ref, high_ref, out_ref):
    def body(i, carry):
        columns = pl.ds(pl.multiple_of(i * tile, tile), tile)
        out_ref[:, columns] = dot_rows(high_ref[...], res_ref[:, columns])
        return carry

    lax.fori_loop(0, res_ref.shape[1] // tile, body, 0)


def finish_kernel(place, raw_ref, zero_ref, w_keep, w1, w2, w3, keep_ref, send_ref, ordered):
    weights = w_keep[...] + w1[...].astype(F32) + w2[...].astype(F32) + w3[...].astype(F32)
    total = raw_ref[...] - dot_rows(weights.astype(BF16), zero_ref[...])
    bins = total.T
    for chip in range(16):
        for pair in range(8):
            source = (chip * 8 + pair) * 16
            target = (pair * 16 + chip) * 16
            ordered[target:target + 16, :] = bins[source:source + 16, :]
    half = keep_ref.shape[0]
    c = place[2]
    keep_ref[...] = ordered[pl.ds(pl.multiple_of(c * half, half), half), :]
    send_ref[...] = ordered[pl.ds(pl.multiple_of((1 - c) * half, half), half), :].astype(BF16)


def quarters(me, total, kind):
    rows = total.shape[0] // 4
    pieces = [
        lax.dynamic_slice_in_dim(total, lax.rem(me + k, 4) * rows, rows, 0) for k in range(4)
    ]
    return pieces[0], [p.astype(kind) for p in pieces[1:]]


def add_four(own, got):
    return (own + got[1]) + (got[0] + got[2])


def invert_factor(matrix, out_ref, row0):
    lanes = 128
    tiles = 16
    row_in_tile = lax.broadcasted_iota(jnp.int32, (8, lanes), 0)
    rows = lax.broadcasted_iota(jnp.int32, (lanes, lanes), 0)
    cols = lax.broadcasted_iota(jnp.int32, (lanes, lanes), 1)
    unit = (rows == cols).astype(F32)
    work = [matrix[8 * i:8 * i + 8, :] for i in range(tiles)]
    inverse = [unit[8 * i:8 * i + 8, :] for i in range(tiles)]

    def spread(value):
        return jnp.broadcast_to(value, (8, lanes))

    for j in range(0, lanes, 2):
        tile, at = divmod(j, 8)
        r1, r2 = work[tile][at:at + 1, :], work[tile][at + 1:at + 2, :]
        x1, x2 = inverse[tile][at:at + 1, :], inverse[tile][at + 1:at + 2, :]
        a = jnp.broadcast_to(r1[:, j:j + 1], (1, lanes))
        b = jnp.broadcast_to(r1[:, j + 1:j + 2], (1, lanes))
        d = jnp.broadcast_to(r2[:, j + 1:j + 2], (1, lanes))
        det = a * d - b * b
        scale = 1.0 / det
        t1, t2 = spread((d * r1 - b * r2) * scale), spread((a * r2 - b * r1) * scale)
        u1, u2 = spread((d * x1 - b * x2) * scale), spread((a * x2 - b * x1) * scale)
        root = lax.rsqrt(a)
        out_ref[row0 + j:row0 + j + 1, :] = x1 * root
        out_ref[row0 + j + 1:row0 + j + 2, :] = (a * x2 - b * x1) * (root * lax.rsqrt(det))
        for i in range(tile, tiles):
            if i == tile:
                if at == 6:
                    continue
                below = row_in_tile > at + 1
                m1 = jnp.where(below, spread(work[i][:, j:j + 1]), 0.0)
                m2 = jnp.where(below, spread(work[i][:, j + 1:j + 2]), 0.0)
            else:
                m1, m2 = spread(work[i][:, j:j + 1]), spread(work[i][:, j + 1:j + 2])
            work[i] = work[i] - (m1 * t1 + m2 * t2)
            inverse[i] = inverse[i] - (m1 * u1 + m2 * u2)


def dot_plain(a, b):
    return jnp.dot(a, b, preferred_element_type=F32, precision=HIGHEST)

def dot_plain(a, b):
    return jnp.dot(a, b, preferred_element_type=F32, precision=HIGHEST)


def factor_kernel(place, mine_ref, other_ref, inverse_ref, inv_high, inv_low, top, bottom):
    first = place[2] == 0
    mine, other = mine_ref[...] * (1.0 / STARS), other_ref[...] * (1.0 / STARS)
    zero, one = jnp.where(first, mine, other), jnp.where(first, other, mine)
    packed = jnp.concatenate([zero[:, :128], zero[:, 128:], one[:, :128], one[:, 128:]], axis=0)
    invert_factor(packed[:128], top, 0)
    upper = top[...]
    lower = dot_last(packed[128:256], upper, HIGHEST)
    invert_factor(packed[256:] - dot_last(lower, lower, HIGHEST), bottom, 0)
    corner = bottom[...]
    left = -dot_plain(corner, dot_plain(lower, upper))
    inverse_ref[:128, :128] = upper
    inverse_ref[:128, 128:] = jnp.zeros_like(upper)
    inverse_ref[128:, :128] = left
    inverse_ref[128:, 128:] = corner
    high, low = split_low(inverse_ref[...])
    inv_high[...] = high
    inv_low[...] = low


def basis_kernel(tiles, high_ref, low_ref, inv_high, inv_low, out_ref, buffer, sems):
    tile = high_ref.shape[0] // tiles
    copies = []
    for i in range(tiles):
        rows = pl.ds(i * tile, tile)
        buffer[rows, :] = (
            dot_last(high_ref[rows, :], inv_high[...])
            + dot_last(high_ref[rows, :], inv_low[...])
            + dot_last(low_ref[rows, :], inv_high[...])
        )
        copy = pltpu.make_async_copy(buffer.at[rows, :], out_ref.at[rows, :], sems.at[i])
        copy.start()
        copies.append(copy)
    for copy in copies:
        copy.wait()


def modes_kernel(kept, got1, got2, got3, inverse_ref, out_ref):
    raw = (kept[...] + got1[...] + got2[...] + got3[...]) * (1.0 / STARS)
    out_ref[...] = dot_last(raw, inverse_ref[...], HIGHEST)


def on_device(residuals, loadings, zero_points, sketch_matrix, use_lists):
    rows, bins = residuals.shape
    units = zero_points.shape[0]
    r = lax.axis_index("rows")
    x, z, c, y = r // 8, (r // 2) % 4, r % 2, lax.axis_index("units")
    place = jnp.stack([x, z, c, y]).astype(jnp.int32)
    square = (MODES, MODES)
    own, half = resident(
        project_kernel, "project", [place], [zero_points, sketch_matrix],
        [on_chip((units, MODES)), on_chip((units // 2, MODES))], flops=2 * units * bins * MODES,
    )
    halves = jnp.concatenate(shift_all("y", [half] * 3), axis=0)
    others = lax.ppermute(halves, AXES, SWAP)
    part, = resident(
        functools.partial(sketch_kernel, 1024), "sketch", [], [residuals, sketch_matrix],
        [on_chip((rows, MODES))], flops=2 * rows * bins * MODES,
    )
    high, low, gram_keep, gram_send, w_keep, *w_sends = resident(
        functools.partial(correct_kernel, 4), "correct", [place, use_lists.T],
        [part, loadings, own, halves, others],
        [on_chip((rows, MODES), BF16)] * 2 + [on_chip((96, MODES))] * 2 + [on_chip((units, MODES))]
        + [on_chip((units, MODES), BF16)] * 3,
        [
            pltpu.VMEM((4 * units, MODES), BF16),
            pltpu.VMEM((4 * units, MODES), BF16),
            pltpu.VMEM(square, F32),
            pltpu.VMEM(square, F32),
            pltpu.VMEM((4 * units, MODES), F32),
        ],
        flops=2 * rows * bins * MODES,
    )
    gram_high, gram_low = split_low(gram_keep + lax.ppermute(gram_send, AXES, SWAP))
    raw, = resident(
        functools.partial(raw_kernel, 512), "raw_sums", [], [residuals, high],
        [on_chip((MODES, bins))], flops=2 * rows * bins * MODES,
    )
    got = shift_all("y", [jnp.concatenate([w, gram_high, gram_low], axis=0) for w in w_sends])
    join = lambda h, l: h.astype(F32) + l.astype(F32)
    gram = add_four(join(gram_high, gram_low), [join(g[units:units + 96], g[units + 96:]) for g in got])
    for axis in "xz":
        gram = add_four(gram, shift_all(axis, [gram] * 3))
    gram_other = lax.ppermute(gram, AXES, SWAP)
    keep, send = resident(
        finish_kernel, "finish_raw", [place], [raw, zero_points, w_keep] + [g[:units] for g in got],
        [on_chip((bins // 2, MODES)), on_chip((bins // 2, MODES), BF16)],
        [pltpu.VMEM((bins, MODES), F32)], flops=2 * units * bins * MODES,
    )
    total = keep + lax.ppermute(send, AXES, SWAP).astype(F32)
    keep, sends = quarters(y, total, BF16)
    keep, sends = quarters(x, add_four(keep, [g.astype(F32) for g in shift_all("y", sends)]), F32)
    keep, sends = quarters(z, add_four(keep, shift_all("x", sends)), F32)
    raw_got = shift_all("z", sends)
    inverse, inv_high, inv_low = resident(
        factor_kernel, "factor", [place], [gram, gram_other],
        [on_chip(square), on_chip(square, BF16), on_chip(square, BF16)],
        [pltpu.VMEM((128, 128), F32)] * 2, flops=1 << 33,
    )
    star_basis, = resident(
        functools.partial(basis_kernel, 4), "basis", [], [high, low, inv_high, inv_low],
        [jax.ShapeDtypeStruct((rows, MODES), F32)],
        [pltpu.VMEM((rows, MODES), F32), pltpu.SemaphoreType.DMA((4,))],
        flops=6 * rows * MODES * MODES, out_specs=[pl.BlockSpec(memory_space=pl.ANY)],
    )
    bin_modes, = resident(
        modes_kernel, "modes", [], [keep, *raw_got, inverse],
        [jax.ShapeDtypeStruct((keep.shape[0], MODES), F32)], flops=1 << 28,
    )
    return (star_basis, bin_modes)


def solution(mesh):
    in_specs = (
        P(("rows", "units"), None),
        P(("rows", "units"), None),
        P("units", None),
        P(),
        P(("rows", "units"), None),
    )
    out_specs = (P(("rows", "units"), None), P(("rows", "units"), None))
    return jax.shard_map(
        on_device, mesh=mesh, in_specs=in_specs, out_specs=out_specs, check_vma=False
    )
```

time: 369 us -> 109 us (0.30); the launches traced: 364 us -> 108 us
  waiting for transfers between devices: 205 us -> 20 us
  other arithmetic: 59.4 us -> 1.46 us
  matrix products: 57.6 us -> 0 us
  Pallas kernels: 0 us -> 39.4 us
  starting transfers between devices: 0.08 us -> 36.9 us
  local copies, waits for them, and re-layouts: 26.4 us -> 9.72 us
  between operations: 15.9 us -> 1.01 us
    psum x1 -> x0, waiting for transfers between devices: 153 us -> none  [on_device(): lower_factor = jnp.linalg.cholesky(lax.psum(gram_local, ('rows', 'units')))]
    another operation x11 -> x1, other arithmetic: 57 us -> 0.08 us  [on_device(): place = jnp.stack([x, z, c, y]).astype(jnp.int32)]
    all_gather x1 -> x0, waiting for transfers between devices: 51.5 us -> none  [on_device(): gathered = lax.all_gather(zero_points, 'units', axis=0, tiled=True)]
    dot_general x4 -> x0, matrix products: 47.2 us -> none  [the longest x1 23.4 us: on_device(): jnp.einsum('bsk,bkn->bsn', loadings.reshape(block_count, BLOCK_STARS, USE...]
    pallas_call x0 -> x8, Pallas kernels: none -> 39.4 us  [resident(): pl.pallas_call(kernel, in_specs=[smem] * len(scalars) + [vmem] * len(arra...]
    ppermute x0 -> x25, starting transfers between devices: none -> 36.9 us  [the longest x21 36.2 us: shift_all(): lax.ppermute(p, AXES, SHIFTS[axis][k])]
    ppermute x0 -> x25, waiting for transfers between devices: none -> 20 us  [the longest x21 19.1 us: shift_all(): lax.ppermute(p, AXES, SHIFTS[axis][k])]
    gather x1 -> x0, local copies, waits for them, and re-layouts: 14.9 us -> none  [on_device(): chosen = tables[use_lists].reshape(block_count, USES * GROUP, width_bins)]
  transfers between devices with their start and end apart: 2 -> 25, of which waited for: 2 -> 10; matrix products, arithmetic and copies ran while one was open for 0% -> 1% of each run, Pallas kernels for 0% -> 25%
where the time goes in v2:
time: 109 us; the launch traced here: 108 us
  Pallas kernels  39.4 us (36%)
  starting transfers between devices  36.9 us (34%)
  waiting for transfers between devices  20 us (18%)
  local copies, waits for them, and re-layouts  9.72 us (9%)
  other arithmetic  1.46 us (1%)
    pallas_call x8, Pallas kernels, resident(): pl.pallas_call(kernel, in_specs=[smem] * len(scalars) + [vmem] * len(arra...  39.4 us
    ppermute x21, starting transfers between devices, shift_all(): lax.ppermute(p, AXES, SHIFTS[axis][k])  36.2 us
    ppermute x21, waiting for transfers between devices, shift_all(): lax.ppermute(p, AXES, SHIFTS[axis][k])  19.1 us
    unnamed x28, local copies, waits for them, and re-layouts  9.59 us
  transfers between devices with their start and end apart: 25, of which 10 were waited for; matrix products, arithmetic and copies ran while one was open for 1% of the time, Pallas kernels for 25%

profile of v2, /device:TPU:0, one launch (start us, length us, event | category | flops | bytes accessed | tf_op | source)
XLA Modules:
  0.0 108.5 jit_solution(7597817871040326688)
XLA Ops:
  4.2 1.8 %collective-permute-start = (f32[128,256]{1,0:T(8,128)S(1)}, f32[128,256]{1,0:T(8,128)S(1)}, u32[]{:S(2)}, u32[]{:S(2)}) collective-permute-start(f32[128,256]{1,0:T(8,128)S(1)} %get-tuple-element.18), channel_id=1, source_target_pairs={{0,1},{1,2},{2,3},{3,0},{4,5},{5,6},{6,7},{7,4},{8,9},{9,10},{10,1... | collective-permute-start | bytes 393224 | tf_op jit(solution)/shard_map/ppermute | solution.py:56
  6.0 2.9 %collective-permute-start.1 = (f32[128,256]{1,0:T(8,128)S(1)}, f32[128,256]{1,0:T(8,128)S(1)}, u32[]{:S(2)}, u32[]{:S(2)}) collective-permute-start(f32[128,256]{1,0:T(8,128)S(1)} %get-tuple-element.18), channel_id=1, source_target_pairs={{0,2},{1,3},{2,0},{3,1},{4,6},{5,7},{6,4},{7,5},{8,10},{9,11},{10,... | collective-permute-start | bytes 393224 | tf_op jit(solution)/shard_map/ppermute | solution.py:56
  10.9 4.0 %collective-permute-done.1 = f32[128,256]{1,0:T(8,128)S(1)} collective-permute-done((f32[128,256]{1,0:T(8,128)S(1)}, f32[128,256]{1,0:T(8,128)S(1)}, u32[]{:S(2)}, u32[]{:S(2)}) %collective-permute-start.1) | collective-permute-done | bytes 131104 | tf_op jit(solution)/shard_map/ppermute | solution.py:56
  15.0 5.8 %copy-done = bf16[4096,2048]{1,0:T(8,128)(2,1)S(1)} copy-done((bf16[4096,2048]{1,0:T(8,128)(2,1)S(1)}, bf16[4096,2048]{1,0:T(8,128)(2,1)}, u32[]{:S(2)}) %copy-start) | copy-done | bytes 16777240
  20.8 5.0 %sketch.1.part_ref = f32[4096,256]{1,0:T(8,128)S(1)} custom-call(bf16[4096,2048]{1,0:T(8,128)(2,1)S(1)} %copy-done, bf16[2048,256]{1,0:T(8,128)(2,1)S(1)} %copy-done.4), custom_call_target="tpu_custom_call" | custom-call | flops 4294967296 | bytes 65536 | tf_op jit(solution)/shard_map/sketch/pallas_call | solution.py:67
  25.9 8.4 %correct.1 = (bf16[4096,256]{1,0:T(8,128)(2,1)S(1)}, bf16[4096,256]{1,0:T(8,128)(2,1)S(1)}, f32[96,256]{1,0:T(8,128)S(1)}, f32[96,256]{1,0:T(8,128)S(1)}, f32[25...) custom-call(s32[4]{0:T(128)S(1)} %pad_add_fusion.place, ...), custom_call_target="tpu_custom_call" | custom-call | flops 4294967296 | bytes 65536 | tf_op jit(solution)/shard_map/correct/pallas_call | solution.py:67
  38.4 2.4 %collective-permute-start.5 = (bf16[448,256]{1,0:T(8,128)(2,1)S(1)}, bf16[448,256]{1,0:T(8,128)(2,1)S(1)}, u32[]{:S(2)}, u32[]{:S(2)}) collective-permute-start(bf16[448,256]{1,0:T(8,128)(2,1)S(1)} %get-tuple-element.40), channel_id=1, source_target_pairs={{0,2},{1,3},{2,0},{3,1},{4,6},{5,7},{6,4},{7,5},{8,10},{9,11},{10,... | collective-permute-start | bytes 688136 | tf_op jit(solution)/shard_map/ppermute | solution.py:56
  40.8 1.6 %collective-permute-start.7 = (bf16[448,256]{1,0:T(8,128)(2,1)S(1)}, bf16[448,256]{1,0:T(8,128)(2,1)S(1)}, u32[]{:S(2)}, u32[]{:S(2)}) collective-permute-start(bf16[448,256]{1,0:T(8,128)(2,1)S(1)} %get-tuple-element.42), channel_id=1, source_target_pairs={{0,3},{1,0},{2,1},{3,2},{4,7},{5,4},{6,5},{7,6},{8,11},{9,8},{10,9... | collective-permute-start | bytes 688136 | tf_op jit(solution)/shard_map/ppermute | solution.py:56
  42.4 5.2 %raw_sums.1.raw_ref = f32[256,2048]{1,0:T(8,128)S(1)} custom-call(bf16[4096,2048]{1,0:T(8,128)(2,1)S(1)} %bitcast.6, bf16[4096,256]{1,0:T(8,128)(2,1)S(1)} %get-tuple-element.19.high_ref), custom_call_target="tpu_custom_call" | custom-call | flops 4294967296 | bytes 65536 | tf_op jit(solution)/shard_map/raw_sums/pallas_call | solution.py:67
  47.6 3.9 %collective-permute-done.5 = bf16[448,256]{1,0:T(8,128)(2,1)S(1)} collective-permute-done((bf16[448,256]{1,0:T(8,128)(2,1)S(1)}, bf16[448,256]{1,0:T(8,128)(2,1)S(1)}, u32[]{:S(2)}, u32[]{:S(2)}) %collective-permute-start.5) | collective-permute-done | bytes 229408 | tf_op jit(solution)/shard_map/ppermute | solution.py:56
  51.8 2.3 %finish_raw.1 = (f32[1024,256]{1,0:T(8,128)S(1)}, bf16[1024,256]{1,0:T(8,128)(2,1)}) custom-call(s32[4]{0:T(128)S(1)} %pad_add_fusion.place, f32[256,2048]{1,0:T(8,128)S(1)} %raw_sums.1.raw_ref, bf16[256,2048]{1,0:T(8,128)(2,1)S(1)} %copy-done.2, f32[256,256]{1,0:T(8,128)S(1)} %get-tuple-element.28.w_keep, bf16[256,256]{1,0:T(8,128)(2,1)S(1)} %slice.42.w1, ...), custom_call_target="tpu_custom_call" | custom-call | flops 268435456 | bytes 65536 | tf_op jit(solution)/shard_map/finish_raw/pallas_call | solution.py:67
  54.2 2.8 %collective-permute-start.10 = (f32[96,256]{1,0:T(8,128)S(1)}, f32[96,256]{1,0:T(8,128)S(1)}, u32[]{:S(2)}, u32[]{:S(2)}) collective-permute-start(f32[96,256]{1,0:T(8,128)S(1)} %fusion.2), channel_id=1, source_target_pairs={{0,96},{1,97},{2,98},{3,99},{4,100},{5,101},{6,102},{7,103},{8,104... | collective-permute-start | bytes 294920 | tf_op jit(solution)/shard_map/ppermute | solution.py:56
  58.7 3.2 %collective-permute-done.10 = f32[96,256]{1,0:T(8,128)S(1)} collective-permute-done((f32[96,256]{1,0:T(8,128)S(1)}, f32[96,256]{1,0:T(8,128)S(1)}, u32[]{:S(2)}, u32[]{:S(2)}) %collective-permute-start.10) | collective-permute-done | bytes 98336 | tf_op jit(solution)/shard_map/ppermute | solution.py:56
  61.9 2.3 %collective-permute-done.8 = f32[96,256]{1,0:T(8,128)S(1)} collective-permute-done((f32[96,256]{1,0:T(8,128)S(1)}, f32[96,256]{1,0:T(8,128)S(1)}, u32[]{:S(2)}, u32[]{:S(2)}) %collective-permute-start.8) | collective-permute-done | bytes 98336 | tf_op jit(solution)/shard_map/ppermute | solution.py:56
  65.6 4.0 %collective-permute-start.11 = (f32[96,256]{1,0:T(8,128)S(1)}, f32[96,256]{1,0:T(8,128)S(1)}, u32[]{:S(2)}, u32[]{:S(2)}) collective-permute-start(f32[96,256]{1,0:T(8,128)S(1)} %add_add_fusion.2), channel_id=1, source_target_pairs={{0,16},{1,17},{2,18},{3,19},{4,20},{5,21},{6,22},{7,23},{8,24},{9,... | collective-permute-start | bytes 294920 | tf_op jit(solution)/shard_map/ppermute | solution.py:56
  70.6 2.2 %collective-permute-start.13 = (f32[96,256]{1,0:T(8,128)S(1)}, f32[96,256]{1,0:T(8,128)S(1)}, u32[]{:S(2)}, u32[]{:S(2)}) collective-permute-start(f32[96,256]{1,0:T(8,128)S(1)} %add_add_fusion.2), channel_id=1, source_target_pairs={{0,24},{1,25},{2,26},{3,27},{4,28},{5,29},{6,30},{7,31},{8,0},{9,1... | collective-permute-start | bytes 294920 | tf_op jit(solution)/shard_map/ppermute | solution.py:56
  74.0 2.6 %collective-permute-start.16 = (bf16[256,256]{1,0:T(8,128)(2,1)S(1)}, bf16[256,256]{1,0:T(8,128)(2,1)S(1)}, u32[]{:S(2)}, u32[]{:S(2)}) collective-permute-start(bf16[256,256]{1,0:T(8,128)(2,1)S(1)} %get-tuple-element.34), channel_id=1, source_target_pairs={{0,2},{1,3},{2,0},{3,1},{4,6},{5,7},{6,4},{7,5},{8,10},{9,11},{10,... | collective-permute-start | bytes 393224 | tf_op jit(solution)/shard_map/ppermute | solution.py:56
  77.6 2.3 %collective-permute-start.18 = (bf16[256,256]{1,0:T(8,128)(2,1)S(1)}, bf16[256,256]{1,0:T(8,128)(2,1)S(1)}, u32[]{:S(2)}, u32[]{:S(2)}) collective-permute-start(bf16[256,256]{1,0:T(8,128)(2,1)S(1)} %get-tuple-element.35), channel_id=1, source_target_pairs={{0,3},{1,0},{2,1},{3,2},{4,7},{5,4},{6,5},{7,6},{8,11},{9,8},{10,9... | collective-permute-start | bytes 393224 | tf_op jit(solution)/shard_map/ppermute | solution.py:56
  80.0 1.7 %collective-permute-done.16 = bf16[256,256]{1,0:T(8,128)(2,1)S(1)} collective-permute-done((bf16[256,256]{1,0:T(8,128)(2,1)S(1)}, bf16[256,256]{1,0:T(8,128)(2,1)S(1)}, u32[]{:S(2)}, u32[]{:S(2)}) %collective-permute-start.16) | collective-permute-done | bytes 131104 | tf_op jit(solution)/shard_map/ppermute | solution.py:56
  81.7 1.6 %collective-permute-done.17 = bf16[256,256]{1,0:T(8,128)(2,1)S(1)} collective-permute-done((bf16[256,256]{1,0:T(8,128)(2,1)S(1)}, bf16[256,256]{1,0:T(8,128)(2,1)S(1)}, u32[]{:S(2)}, u32[]{:S(2)}) %collective-permute-start.17) | collective-permute-done | bytes 131104 | tf_op jit(solution)/shard_map/ppermute | solution.py:56
  84.6 3.0 %collective-permute-start.21 = (f32[64,256]{1,0:T(8,128)S(1)}, f32[64,256]{1,0:T(8,128)S(1)}, u32[]{:S(2)}, u32[]{:S(2)}) collective-permute-start(f32[64,256]{1,0:T(8,128)S(1)} %get-tuple-element.38), channel_id=1, source_target_pairs={{0,96},{1,97},{2,98},{3,99},{4,100},{5,101},{6,102},{7,103},{8,104... | collective-permute-start | bytes 196616 | tf_op jit(solution)/shard_map/ppermute | solution.py:56
  87.6 13.3 %factor.1 = (f32[256,256]{1,0:T(8,128)S(1)}, bf16[256,256]{1,0:T(8,128)(2,1)S(1)}, bf16[256,256]{1,0:T(8,128)(2,1)S(1)}) custom-call(s32[4]{0:T(128)S(1)} %pad_add_fusion.place, f32[96,256]{1,0:T(8,128)S(1)} %add_add_fusion.1.mine_ref, f32[96,256]{1,0:T(8,128)S(1)} %collective-permute-done.14.other_ref), custom_call_target="tpu_custom_call" | custom-call | flops 8589934592 | bytes 65536 | tf_op jit(solution)/shard_map/factor/pallas_call | solution.py:67
  102.5 1.8 %collective-permute-start.24 = (f32[16,256]{1,0:T(8,128)S(1)}, f32[16,256]{1,0:T(8,128)S(1)}, u32[]{:S(2)}, u32[]{:S(2)}) collective-permute-start(f32[16,256]{1,0:T(8,128)S(1)} %get-tuple-element.43), channel_id=1, source_target_pairs={{0,24},{1,25},{2,26},{3,27},{4,28},{5,29},{6,30},{7,31},{8,0},{9,1... | collective-permute-start | bytes 49160 | tf_op jit(solution)/shard_map/ppermute | solution.py:56
  104.3 3.2 %basis.1 = f32[4096,256]{1,0:T(8,128)} custom-call(bf16[4096,256]{1,0:T(8,128)(2,1)S(1)} %get-tuple-element.19.high_ref, bf16[4096,256]{1,0:T(8,128)(2,1)S(1)} %copy-done.6, bf16[256,256]{1,0:T(8,128)(2,1)S(1)} %get-tuple-element.26.inv_high, bf16[256,256]{1,0:T(8,128)(2,1)S(1)} %get-tuple-element.27.inv_low), custom_call_target="tpu_custom_call" | custom-call | flops 1610612736 | bytes 65536 | tf_op jit(solution)/shard_map/basis/pallas_call | solution.py:67
  (79 shorter events, 20.2 us)
Async XLA Ops:
  4.2 6.7 %collective-permute-start = (f32[128,256]{1,0:T(8,128)S(1)}, f32[128,256]{1,0:T(8,128)S(1)}, u32[]{:S(2)}, u32[]{:S(2)}) collective-permute-start(f32[128,256]{1,0:T(8,128)S(1)} %get-tuple-element.18), channel_id=1, source_target_pairs={{0,1},{1,2},{2,3},{3,0},{4,5},{5,6},{6,7},{7,4},{8,9},{9,10},{10,1... | collective-permute-start | bytes 393224 | tf_op jit(solution)/shard_map/ppermute | solution.py:56
  6.0 8.9 %collective-permute-start.1 = (f32[128,256]{1,0:T(8,128)S(1)}, f32[128,256]{1,0:T(8,128)S(1)}, u32[]{:S(2)}, u32[]{:S(2)}) collective-permute-start(f32[128,256]{1,0:T(8,128)S(1)} %get-tuple-element.18), channel_id=1, source_target_pairs={{0,2},{1,3},{2,0},{3,1},{4,6},{5,7},{6,4},{7,5},{8,10},{9,11},{10,... | collective-permute-start | bytes 393224 | tf_op jit(solution)/shard_map/ppermute | solution.py:56
  8.9 6.0 %collective-permute-start.2 = (f32[128,256]{1,0:T(8,128)S(1)}, f32[128,256]{1,0:T(8,128)S(1)}, u32[]{:S(2)}, u32[]{:S(2)}) collective-permute-start(f32[128,256]{1,0:T(8,128)S(1)} %get-tuple-element.18), channel_id=1, source_target_pairs={{0,3},{1,0},{2,1},{3,2},{4,7},{5,4},{6,5},{7,6},{8,11},{9,8},{10,9... | collective-permute-start | bytes 393224 | tf_op jit(solution)/shard_map/ppermute | solution.py:56
  14.9 10.9 %collective-permute-start.3 = (f32[384,256]{1,0:T(8,128)S(1)}, f32[384,256]{1,0:T(8,128)S(1)}, u32[]{:S(2)}, u32[]{:S(2)}) collective-permute-start(f32[384,256]{1,0:T(8,128)S(1)} %constant_dynamic-update-slice_fusion.half_ref), channel_id=1, source_target_pairs={{0,4},{1,5},{2,6},{3,7},{4,0},{5,1},{6,2},{7,3},{8,12},{9,13},{10,... | collective-permute-start | bytes 1179656 | tf_op jit(solution)/shard_map/ppermute | solution.py:290
  37.1 10.5 %collective-permute-start.6 = (bf16[448,256]{1,0:T(8,128)(2,1)S(1)}, bf16[448,256]{1,0:T(8,128)(2,1)S(1)}, u32[]{:S(2)}, u32[]{:S(2)}) collective-permute-start(bf16[448,256]{1,0:T(8,128)(2,1)S(1)} %get-tuple-element.41), channel_id=1, source_target_pairs={{0,1},{1,2},{2,3},{3,0},{4,5},{5,6},{6,7},{7,4},{8,9},{9,10},{10,1... | collective-permute-start | bytes 688136 | tf_op jit(solution)/shard_map/ppermute | solution.py:56
  38.4 13.1 %collective-permute-start.5 = (bf16[448,256]{1,0:T(8,128)(2,1)S(1)}, bf16[448,256]{1,0:T(8,128)(2,1)S(1)}, u32[]{:S(2)}, u32[]{:S(2)}) collective-permute-start(bf16[448,256]{1,0:T(8,128)(2,1)S(1)} %get-tuple-element.40), channel_id=1, source_target_pairs={{0,2},{1,3},{2,0},{3,1},{4,6},{5,7},{6,4},{7,5},{8,10},{9,11},{10,... | collective-permute-start | bytes 688136 | tf_op jit(solution)/shard_map/ppermute | solution.py:56
  40.8 11.0 %collective-permute-start.7 = (bf16[448,256]{1,0:T(8,128)(2,1)S(1)}, bf16[448,256]{1,0:T(8,128)(2,1)S(1)}, u32[]{:S(2)}, u32[]{:S(2)}) collective-permute-start(bf16[448,256]{1,0:T(8,128)(2,1)S(1)} %get-tuple-element.42), channel_id=1, source_target_pairs={{0,3},{1,0},{2,1},{3,2},{4,7},{5,4},{6,5},{7,6},{8,11},{9,8},{10,9... | collective-permute-start | bytes 688136 | tf_op jit(solution)/shard_map/ppermute | solution.py:56
  54.2 18.6 %collective-permute-start.15 = (bf16[1024,256]{1,0:T(8,128)(2,1)}, bf16[1024,256]{1,0:T(8,128)(2,1)}, u32[]{:S(2)}, u32[]{:S(2)}) collective-permute-start(bf16[1024,256]{1,0:T(8,128)(2,1)} %get-tuple-element.30), channel_id=1, source_target_pairs={{0,4},{1,5},{2,6},{3,7},{4,0},{5,1},{6,2},{7,3},{8,12},{9,13},{10,... | collective-permute-start | bytes 1572872 | tf_op jit(solution)/shard_map/ppermute | solution.py:325
  54.2 7.7 %collective-permute-start.10 = (f32[96,256]{1,0:T(8,128)S(1)}, f32[96,256]{1,0:T(8,128)S(1)}, u32[]{:S(2)}, u32[]{:S(2)}) collective-permute-start(f32[96,256]{1,0:T(8,128)S(1)} %fusion.2), channel_id=1, source_target_pairs={{0,96},{1,97},{2,98},{3,99},{4,100},{5,101},{6,102},{7,103},{8,104... | collective-permute-start | bytes 294920 | tf_op jit(solution)/shard_map/ppermute | solution.py:56
  57.0 7.2 %collective-permute-start.8 = (f32[96,256]{1,0:T(8,128)S(1)}, f32[96,256]{1,0:T(8,128)S(1)}, u32[]{:S(2)}, u32[]{:S(2)}) collective-permute-start(f32[96,256]{1,0:T(8,128)S(1)} %fusion.2), channel_id=1, source_target_pairs={{0,64},{1,65},{2,66},{3,67},{4,68},{5,69},{6,70},{7,71},{8,72},{9,... | collective-permute-start | bytes 294920 | tf_op jit(solution)/shard_map/ppermute | solution.py:56
  57.8 7.7 %collective-permute-start.9 = (f32[96,256]{1,0:T(8,128)S(1)}, f32[96,256]{1,0:T(8,128)S(1)}, u32[]{:S(2)}, u32[]{:S(2)}) collective-permute-start(f32[96,256]{1,0:T(8,128)S(1)} %fusion.2), channel_id=1, source_target_pairs={{0,32},{1,33},{2,34},{3,35},{4,36},{5,37},{6,38},{7,39},{8,40},{9,... | collective-permute-start | bytes 294920 | tf_op jit(solution)/shard_map/ppermute | solution.py:56
  65.6 12.0 %collective-permute-start.11 = (f32[96,256]{1,0:T(8,128)S(1)}, f32[96,256]{1,0:T(8,128)S(1)}, u32[]{:S(2)}, u32[]{:S(2)}) collective-permute-start(f32[96,256]{1,0:T(8,128)S(1)} %add_add_fusion.2), channel_id=1, source_target_pairs={{0,16},{1,17},{2,18},{3,19},{4,20},{5,21},{6,22},{7,23},{8,24},{9,... | collective-permute-start | bytes 294920 | tf_op jit(solution)/shard_map/ppermute | solution.py:56
  69.6 10.3 %collective-permute-start.12 = (f32[96,256]{1,0:T(8,128)S(1)}, f32[96,256]{1,0:T(8,128)S(1)}, u32[]{:S(2)}, u32[]{:S(2)}) collective-permute-start(f32[96,256]{1,0:T(8,128)S(1)} %add_add_fusion.2), channel_id=1, source_target_pairs={{0,8},{1,9},{2,10},{3,11},{4,12},{5,13},{6,14},{7,15},{8,16},{9,17... | collective-permute-start | bytes 294920 | tf_op jit(solution)/shard_map/ppermute | solution.py:56
  70.6 9.3 %collective-permute-start.13 = (f32[96,256]{1,0:T(8,128)S(1)}, f32[96,256]{1,0:T(8,128)S(1)}, u32[]{:S(2)}, u32[]{:S(2)}) collective-permute-start(f32[96,256]{1,0:T(8,128)S(1)} %add_add_fusion.2), channel_id=1, source_target_pairs={{0,24},{1,25},{2,26},{3,27},{4,28},{5,29},{6,30},{7,31},{8,0},{9,1... | collective-permute-start | bytes 294920 | tf_op jit(solution)/shard_map/ppermute | solution.py:56
  74.0 7.7 %collective-permute-start.16 = (bf16[256,256]{1,0:T(8,128)(2,1)S(1)}, bf16[256,256]{1,0:T(8,128)(2,1)S(1)}, u32[]{:S(2)}, u32[]{:S(2)}) collective-permute-start(bf16[256,256]{1,0:T(8,128)(2,1)S(1)} %get-tuple-element.34), channel_id=1, source_target_pairs={{0,2},{1,3},{2,0},{3,1},{4,6},{5,7},{6,4},{7,5},{8,10},{9,11},{10,... | collective-permute-start | bytes 393224 | tf_op jit(solution)/shard_map/ppermute | solution.py:56
  76.6 6.7 %collective-permute-start.17 = (bf16[256,256]{1,0:T(8,128)(2,1)S(1)}, bf16[256,256]{1,0:T(8,128)(2,1)S(1)}, u32[]{:S(2)}, u32[]{:S(2)}) collective-permute-start(bf16[256,256]{1,0:T(8,128)(2,1)S(1)} %get-tuple-element.36), channel_id=1, source_target_pairs={{0,1},{1,2},{2,3},{3,0},{4,5},{5,6},{6,7},{7,4},{8,9},{9,10},{10,1... | collective-permute-start | bytes 393224 | tf_op jit(solution)/shard_map/ppermute | solution.py:56
  77.6 5.8 %collective-permute-start.18 = (bf16[256,256]{1,0:T(8,128)(2,1)S(1)}, bf16[256,256]{1,0:T(8,128)(2,1)S(1)}, u32[]{:S(2)}, u32[]{:S(2)}) collective-permute-start(bf16[256,256]{1,0:T(8,128)(2,1)S(1)} %get-tuple-element.35), channel_id=1, source_target_pairs={{0,3},{1,0},{2,1},{3,2},{4,7},{5,4},{6,5},{7,6},{8,11},{9,8},{10,9... | collective-permute-start | bytes 393224 | tf_op jit(solution)/shard_map/ppermute | solution.py:56
  79.9 7.7 %collective-permute-start.14 = (f32[96,256]{1,0:T(8,128)S(1)}, f32[96,256]{1,0:T(8,128)S(1)}, u32[]{:S(2)}, u32[]{:S(2)}) collective-permute-start(f32[96,256]{1,0:T(8,128)S(1)} %add_add_fusion.1.mine_ref), channel_id=1, source_target_pairs={{0,4},{1,5},{2,6},{3,7},{4,0},{5,1},{6,2},{7,3},{8,12},{9,13},{10,... | collective-permute-start | bytes 294920 | tf_op jit(solution)/shard_map/ppermute | solution.py:319
  83.5 17.4 %collective-permute-start.19 = (f32[64,256]{1,0:T(8,128)S(1)}, f32[64,256]{1,0:T(8,128)S(1)}, u32[]{:S(2)}, u32[]{:S(2)}) collective-permute-start(f32[64,256]{1,0:T(8,128)S(1)} %get-tuple-element.37), channel_id=1, source_target_pairs={{0,64},{1,65},{2,66},{3,67},{4,68},{5,69},{6,70},{7,71},{8,72},{9,... | collective-permute-start | bytes 196616 | tf_op jit(solution)/shard_map/ppermute | solution.py:56
  84.3 16.6 %collective-permute-start.20 = (f32[64,256]{1,0:T(8,128)S(1)}, f32[64,256]{1,0:T(8,128)S(1)}, u32[]{:S(2)}, u32[]{:S(2)}) collective-permute-start(f32[64,256]{1,0:T(8,128)S(1)} %get-tuple-element.39), channel_id=1, source_target_pairs={{0,32},{1,33},{2,34},{3,35},{4,36},{5,37},{6,38},{7,39},{8,40},{9,... | collective-permute-start | bytes 196616 | tf_op jit(solution)/shard_map/ppermute | solution.py:56
  84.6 16.3 %collective-permute-start.21 = (f32[64,256]{1,0:T(8,128)S(1)}, f32[64,256]{1,0:T(8,128)S(1)}, u32[]{:S(2)}, u32[]{:S(2)}) collective-permute-start(f32[64,256]{1,0:T(8,128)S(1)} %get-tuple-element.38), channel_id=1, source_target_pairs={{0,96},{1,97},{2,98},{3,99},{4,100},{5,101},{6,102},{7,103},{8,104... | collective-permute-start | bytes 196616 | tf_op jit(solution)/shard_map/ppermute | solution.py:56
  101.0 6.6 %collective-permute-start.22 = (f32[16,256]{1,0:T(8,128)S(1)}, f32[16,256]{1,0:T(8,128)S(1)}, u32[]{:S(2)}, u32[]{:S(2)}) collective-permute-start(f32[16,256]{1,0:T(8,128)S(1)} %get-tuple-element.45), channel_id=1, source_target_pairs={{0,8},{1,9},{2,10},{3,11},{4,12},{5,13},{6,14},{7,15},{8,16},{9,17... | collective-permute-start | bytes 49160 | tf_op jit(solution)/shard_map/ppermute | solution.py:56
  101.0 6.5 %collective-permute-start.23 = (f32[16,256]{1,0:T(8,128)S(1)}, f32[16,256]{1,0:T(8,128)S(1)}, u32[]{:S(2)}, u32[]{:S(2)}) collective-permute-start(f32[16,256]{1,0:T(8,128)S(1)} %get-tuple-element.44), channel_id=1, source_target_pairs={{0,16},{1,17},{2,18},{3,19},{4,20},{5,21},{6,22},{7,23},{8,24},{9,... | collective-permute-start | bytes 49160 | tf_op jit(solution)/shard_map/ppermute | solution.py:56
  102.5 5.0 %collective-permute-start.24 = (f32[16,256]{1,0:T(8,128)S(1)}, f32[16,256]{1,0:T(8,128)S(1)}, u32[]{:S(2)}, u32[]{:S(2)}) collective-permute-start(f32[16,256]{1,0:T(8,128)S(1)} %get-tuple-element.43), channel_id=1, source_target_pairs={{0,24},{1,25},{2,26},{3,27},{4,28},{5,29},{6,30},{7,31},{8,0},{9,1... | collective-permute-start | bytes 49160 | tf_op jit(solution)/shard_map/ppermute | solution.py:56
  (14 other events, 143.3 us)

commit v3 on v2

--- a/solution.py
+++ b/solution.py
@@ -60,35 +60,49 @@
     return pltpu.VMEM(shape, kind)
 
 
-def resident(kernel, name, scalars, arrays, outs, scratch=(), flops=0, limit=16, out_specs=None):
+def resident(kernel, name, scalars, arrays, outs, scratch=(), flops=0, limit=16, out_specs=None, far=()):
     vmem = pl.BlockSpec(memory_space=pltpu.VMEM)
     smem = pl.BlockSpec(memory_space=pltpu.SMEM)
     arrays = [pltpu.with_memory_space_constraint(a, pltpu.VMEM) for a in arrays]
+    far = [pltpu.with_memory_space_constraint(a, pltpu.HBM) for a in far]
     return pl.pallas_call(
         kernel,
-        in_specs=[smem] * len(scalars) + [vmem] * len(arrays),
+        in_specs=[smem] * len(scalars) + [vmem] * len(arrays) + [pl.BlockSpec(memory_space=pltpu.HBM)] * len(far),
         out_specs=out_specs or [vmem] * len(outs),
         out_shape=list(outs),
         scratch_shapes=list(scratch),
         compiler_params=pltpu.CompilerParams(vmem_limit_bytes=limit << 20),
         cost_estimate=pl.CostEstimate(flops=flops, bytes_accessed=1 << 16, transcendentals=0),
         name=name,
-    )(*scalars, *arrays)
-
-
-def project_kernel(place, zero_ref, sketch_ref, full_ref, half_ref):
-    full_ref[...] = jnp.dot(zero_ref[...], sketch_ref[...], preferred_element_type=F32)
+    )(*scalars, *arrays, *far)
+
+
+def project_kernel(place, zero_hbm, sketch_hbm, full_ref, half_ref, zero, sketch, sems):
+    copies = [
+        pltpu.make_async_copy(zero_hbm, zero, sems.at[0]),
+        pltpu.make_async_copy(sketch_hbm, sketch, sems.at[1]),
+    ]
+    for copy in copies:
+        copy.start()
+    for copy in copies:
+        copy.wait()
+    full_ref[...] = jnp.dot(zero[...], sketch[...], preferred_element_type=F32)
     half = full_ref.shape[0] // 2
     half_ref[...] = full_ref[pl.ds(pl.multiple_of(place[2] * half, half), half), :]
 
 
-def sketch_kernel(tile, res_ref, sketch_ref, out_ref):
-    def body(i, carry):
-        rows = pl.ds(pl.multiple_of(i * tile, tile), tile)
+def sketch_kernel(tiles, sketch_ref, res_hbm, out_ref, res_ref, flag_ref, sems):
+    tile = res_ref.shape[0] // tiles
+    copies = []
+    for i in range(tiles):
+        rows = pl.ds(i * tile, tile)
+        copies.append(pltpu.make_async_copy(res_hbm.at[rows, :], res_ref.at[rows, :], sems.at[i]))
+        copies[i].start()
+    for i in range(tiles):
+        copies[i].wait()
+        rows = pl.ds(i * tile, tile)
         out_ref[rows, :] = jnp.dot(res_ref[rows, :], sketch_ref[...], preferred_element_type=F32)
-        return carry
-
-    lax.fori_loop(0, res_ref.shape[0] // tile, body, 0)
+    flag_ref[...] = jnp.zeros_like(flag_ref)
 
 
 def correct_kernel(blocks, place, uses, part_ref, load_ref, own_ref, half_ref, other_ref,
@@ -164,10 +178,10 @@
     total = raw_ref[...] - dot_rows(weights.astype(BF16), zero_ref[...])
     bins = total.T
     for chip in range(16):
-        for pair in range(8):
-            source = (chip * 8 + pair) * 16
-            target = (pair * 16 + chip) * 16
-            ordered[target:target + 16, :] = bins[source:source + 16, :]
+        for core in range(2):
+            source = (chip * 2 + core) * 64
+            target = (core * 16 + chip) * 64
+            ordered[target:target + 64, :] = bins[source:source + 64, :]
     half = keep_ref.shape[0]
     c = place[2]
     keep_ref[...] = ordered[pl.ds(pl.multiple_of(c * half, half), half), :]
@@ -186,44 +200,67 @@
     return (own + got[1]) + (got[0] + got[2])
 
 
-def invert_factor(matrix, out_ref, row0):
-    lanes = 128
-    tiles = 16
+def invert_factor(matrix, out_ref, panel=8):
+    lanes, tiles = 128, 16
     row_in_tile = lax.broadcasted_iota(jnp.int32, (8, lanes), 0)
     rows = lax.broadcasted_iota(jnp.int32, (lanes, lanes), 0)
-    cols = lax.broadcasted_iota(jnp.int32, (lanes, lanes), 1)
-    unit = (rows == cols).astype(F32)
+    unit = (rows == lax.broadcasted_iota(jnp.int32, (lanes, lanes), 1)).astype(F32)
     work = [matrix[8 * i:8 * i + 8, :] for i in range(tiles)]
     inverse = [unit[8 * i:8 * i + 8, :] for i in range(tiles)]
 
     def spread(value):
         return jnp.broadcast_to(value, (8, lanes))
 
-    for j in range(0, lanes, 2):
+    for j in range(0, lanes, panel):
         tile, at = divmod(j, 8)
-        r1, r2 = work[tile][at:at + 1, :], work[tile][at + 1:at + 2, :]
-        x1, x2 = inverse[tile][at:at + 1, :], inverse[tile][at + 1:at + 2, :]
-        a = jnp.broadcast_to(r1[:, j:j + 1], (1, lanes))
-        b = jnp.broadcast_to(r1[:, j + 1:j + 2], (1, lanes))
-        d = jnp.broadcast_to(r2[:, j + 1:j + 2], (1, lanes))
-        det = a * d - b * b
-        scale = 1.0 / det
-        t1, t2 = spread((d * r1 - b * r2) * scale), spread((a * r2 - b * r1) * scale)
-        u1, u2 = spread((d * x1 - b * x2) * scale), spread((a * x2 - b * x1) * scale)
-        root = lax.rsqrt(a)
-        out_ref[row0 + j:row0 + j + 1, :] = x1 * root
-        out_ref[row0 + j + 1:row0 + j + 2, :] = (a * x2 - b * x1) * (root * lax.rsqrt(det))
+        top = [spread(work[tile][at + k:at + k + 1, :]) for k in range(panel)]
+        low = [spread(inverse[tile][at + k:at + k + 1, :]) for k in range(panel)]
+        entry = {
+            (p, q): spread(top[p][:, j + q:j + q + 1])
+            for p in range(panel) for q in range(p, panel)
+        }
+        top_solved, low_solved, factors = {}, {}, {}
+        for k in range(0, panel, 2):
+            a, b, d = entry[k, k], entry[k, k + 1], entry[k + 1, k + 1]
+            det = a * d - b * b
+            scale = 1.0 / det
+            i00, i01, i11 = d * scale, b * scale, a * scale
+            root = lax.rsqrt(a)
+            r = at + k
+            out_ref[j + k:j + k + 1, :] = (low[k] * root)[r:r + 1, :]
+            under = (a * low[k + 1] - b * low[k]) * (root * lax.rsqrt(det))
+            out_ref[j + k + 1:j + k + 2, :] = under[r + 1:r + 2, :]
+            for rows_of, solved in ((top, top_solved), (low, low_solved)):
+                solved[k] = i00 * rows_of[k] - i01 * rows_of[k + 1]
+                solved[k + 1] = i11 * rows_of[k + 1] - i01 * rows_of[k]
+            for q in range(k + 2, panel):
+                u, v = entry[k, q], entry[k + 1, q]
+                factors[k, q], factors[k + 1, q] = i00 * u - i01 * v, i11 * v - i01 * u
+            for p in range(k + 2, panel):
+                for q in range(p, panel):
+                    entry[p, q] = entry[p, q] - (entry[k, p] * factors[k, q] + entry[k + 1, p] * factors[k + 1, q])
+                for rows_of in (top, low):
+                    rows_of[p] = rows_of[p] - (factors[k, p] * rows_of[k] + factors[k + 1, p] * rows_of[k + 1])
+        for solved in (top_solved, low_solved):
+            for k in range(panel - 3, -1, -1):
+                for q in range(panel - 1, k // 2 * 2 + 1, -1):
+                    solved[k] = solved[k] - factors[k, q] * solved[q]
+        top_rows = [top_solved[k] for k in range(panel)]
+        low_rows = [low_solved[k] for k in range(panel)]
         for i in range(tile, tiles):
+            if i == tile and at + panel == 8:
+                continue
+            columns = [spread(work[i][:, j + k:j + k + 1]) for k in range(panel)]
             if i == tile:
-                if at == 6:
-                    continue
-                below = row_in_tile > at + 1
-                m1 = jnp.where(below, spread(work[i][:, j:j + 1]), 0.0)
-                m2 = jnp.where(below, spread(work[i][:, j + 1:j + 2]), 0.0)
-            else:
-                m1, m2 = spread(work[i][:, j:j + 1]), spread(work[i][:, j + 1:j + 2])
-            work[i] = work[i] - (m1 * t1 + m2 * t2)
-            inverse[i] = inverse[i] - (m1 * u1 + m2 * u2)
+                columns = [jnp.where(row_in_tile >= at + panel, m, 0.0) for m in columns]
+            work[i] = work[i] - sum_pairs([m * t for m, t in zip(columns, top_rows)])
+            inverse[i] = inverse[i] - sum_pairs([m * t for m, t in zip(columns, low_rows)])
+
+
+def sum_pairs(terms):
+    while len(terms) > 1:
+        terms = [a + b for a, b in zip(terms[::2], terms[1::2])]
+    return terms[0]
 
 
 def dot_plain(a, b):
@@ -238,10 +275,10 @@
     mine, other = mine_ref[...] * (1.0 / STARS), other_ref[...] * (1.0 / STARS)
     zero, one = jnp.where(first, mine, other), jnp.where(first, other, mine)
     packed = jnp.concatenate([zero[:, :128], zero[:, 128:], one[:, :128], one[:, 128:]], axis=0)
-    invert_factor(packed[:128], top, 0)
+    invert_factor(packed[:128], top)
     upper = top[...]
     lower = dot_last(packed[128:256], upper, HIGHEST)
-    invert_factor(packed[256:] - dot_last(lower, lower, HIGHEST), bottom, 0)
+    invert_factor(packed[256:] - dot_last(lower, lower, HIGHEST), bottom)
     corner = bottom[...]
     left = -dot_plain(corner, dot_plain(lower, upper))
     inverse_ref[:128, :128] = upper
@@ -283,15 +320,23 @@
     place = jnp.stack([x, z, c, y]).astype(jnp.int32)
     square = (MODES, MODES)
     own, half = resident(
-        project_kernel, "project", [place], [zero_points, sketch_matrix],
-        [on_chip((units, MODES)), on_chip((units // 2, MODES))], flops=2 * units * bins * MODES,
-    )
-    halves = jnp.concatenate(shift_all("y", [half] * 3), axis=0)
+        project_kernel, "project", [place], [],
+        [on_chip((units, MODES)), on_chip((units // 2, MODES))],
+        [
+            pltpu.VMEM((units, bins), BF16),
+            pltpu.VMEM((bins, MODES), BF16),
+            pltpu.SemaphoreType.DMA((2,)),
+        ],
+        flops=2 * units * bins * MODES, far=[zero_points, sketch_matrix],
+    )
+    shifted = shift_all("y", [half] * 3)
+    part, residuals, flag = resident(
+        functools.partial(sketch_kernel, 8), "sketch", [], [sketch_matrix],
+        [on_chip((rows, MODES)), on_chip((rows, bins), BF16), jax.ShapeDtypeStruct((8, 128), F32)],
+        [pltpu.SemaphoreType.DMA((8,))], flops=2 * rows * bins * MODES, far=[residuals],
+    )
+    halves = jnp.concatenate(shifted, axis=0) + flag[0, 0]
     others = lax.ppermute(halves, AXES, SWAP)
-    part, = resident(
-        functools.partial(sketch_kernel, 1024), "sketch", [], [residuals, sketch_matrix],
-        [on_chip((rows, MODES))], flops=2 * rows * bins * MODES,
-    )
     high, low, gram_keep, gram_send, w_keep, *w_sends = resident(
         functools.partial(correct_kernel, 4), "correct", [place, use_lists.T],
         [part, loadings, own, halves, others],
@@ -306,27 +351,25 @@
         ],
         flops=2 * rows * bins * MODES,
     )
-    gram_high, gram_low = split_low(gram_keep + lax.ppermute(gram_send, AXES, SWAP))
+    w_got = shift_all("y", w_sends)
+    gram = gram_keep + lax.ppermute(gram_send, AXES, SWAP)
     raw, = resident(
         functools.partial(raw_kernel, 512), "raw_sums", [], [residuals, high],
         [on_chip((MODES, bins))], flops=2 * rows * bins * MODES,
     )
-    got = shift_all("y", [jnp.concatenate([w, gram_high, gram_low], axis=0) for w in w_sends])
-    join = lambda h, l: h.astype(F32) + l.astype(F32)
-    gram = add_four(join(gram_high, gram_low), [join(g[units:units + 96], g[units + 96:]) for g in got])
-    for axis in "xz":
+    for axis in "xzy":
         gram = add_four(gram, shift_all(axis, [gram] * 3))
     gram_other = lax.ppermute(gram, AXES, SWAP)
     keep, send = resident(
-        finish_kernel, "finish_raw", [place], [raw, zero_points, w_keep] + [g[:units] for g in got],
+        finish_kernel, "finish_raw", [place], [raw, zero_points, w_keep, *w_got],
         [on_chip((bins // 2, MODES)), on_chip((bins // 2, MODES), BF16)],
         [pltpu.VMEM((bins, MODES), F32)], flops=2 * units * bins * MODES,
     )
     total = keep + lax.ppermute(send, AXES, SWAP).astype(F32)
-    keep, sends = quarters(y, total, BF16)
-    keep, sends = quarters(x, add_four(keep, [g.astype(F32) for g in shift_all("y", sends)]), F32)
-    keep, sends = quarters(z, add_four(keep, shift_all("x", sends)), F32)
-    raw_got = shift_all("z", sends)
+    keep, sends = quarters(x, total, BF16)
+    keep, sends = quarters(z, add_four(keep, [g.astype(F32) for g in shift_all("x", sends)]), F32)
+    keep, sends = quarters(y, add_four(keep, shift_all("z", sends)), F32)
+    raw_got = shift_all("y", sends)
     inverse, inv_high, inv_low = resident(
         factor_kernel, "factor", [place], [gram, gram_other],
         [on_chip(square), on_chip(square, BF16), on_chip(square, BF16)],
@@ -336,7 +379,7 @@
         functools.partial(basis_kernel, 4), "basis", [], [high, low, inv_high, inv_low],
         [jax.ShapeDtypeStruct((rows, MODES), F32)],
         [pltpu.VMEM((rows, MODES), F32), pltpu.SemaphoreType.DMA((4,))],
-        flops=6 * rows * MODES * MODES, out_specs=[pl.BlockSpec(memory_space=pl.ANY)],
+        flops=6 * rows * MODES * MODES, out_specs=[pl.BlockSpec(memory_space=pltpu.HBM)],
     )
     bin_modes, = resident(
         modes_kernel, "modes", [], [keep, *raw_got, inverse],

time: 109 us -> 104 us (0.954)
  local copies, waits for them, and re-layouts: 9.72 us -> 1.85 us
  Pallas kernels: 39.4 us -> 45.2 us
  waiting for transfers between devices: 20 us -> 16.4 us
    unnamed x28 -> x12, local copies, waits for them, and re-layouts: 9.59 us -> 1.25 us
    pallas_call x8, Pallas kernels: 39.4 us -> 45.2 us  [resident(): pl.pallas_call(kernel, in_specs=[smem] * len(scalars) + [vmem] * len(arra...]
    ppermute x21 -> x24, waiting for transfers between devices: 19.1 us -> 14.7 us  [shift_all(): lax.ppermute(p, AXES, SHIFTS[axis][k])]
    ppermute x1, waiting for transfers between devices: 0.01 us -> 1.71 us  [on_device(): others = lax.ppermute(halves, AXES, SWAP)]
    ppermute x21 -> x24, starting transfers between devices: 36.2 us -> 37 us  [shift_all(): lax.ppermute(p, AXES, SHIFTS[axis][k])]
  transfers between devices with their start and end apart: 25 -> 28, of which waited for: 10 -> 8; matrix products, arithmetic and copies ran while one was open for 1% -> 2% of each run, Pallas kernels for 25% -> 32%
where the time goes in v3:
time: 104 us
  Pallas kernels  45.2 us (43%)
  starting transfers between devices  37.1 us (36%)
  waiting for transfers between devices  16.4 us (16%)
  other arithmetic  2.06 us (2%)
  local copies, waits for them, and re-layouts  1.85 us (2%)
    pallas_call x8, Pallas kernels, resident(): pl.pallas_call(kernel, in_specs=[smem] * len(scalars) + [vmem] * len(arra...  45.2 us
    ppermute x24, starting transfers between devices, shift_all(): lax.ppermute(p, AXES, SHIFTS[axis][k])  37 us
    ppermute x24, waiting for transfers between devices, shift_all(): lax.ppermute(p, AXES, SHIFTS[axis][k])  14.7 us
  transfers between devices with their start and end apart: 28, of which 8 were waited for; matrix products, arithmetic and copies ran while one was open for 2% of the time, Pallas kernels for 32%

profile of v3, /device:TPU:0, one launch (start us, length us, event | category | flops | bytes accessed | tf_op | source)
XLA Modules:
  0.0 103.6 jit_solution(7326702257990399309)
XLA Ops:
  0.8 2.7 %project.1 = (f32[256,256]{1,0:T(8,128)S(1)}, f32[128,256]{1,0:T(8,128)S(1)}) custom-call(s32[4]{0:T(128)S(1)} %pad_add_fusion.place, bf16[256,2048]{1,0:T(8,128)(2,1)} %zero_ref.1, bf16[2048,256]{1,0:T(8,128)(2,1)} %sketch_hbm.1), custom_call_target="tpu_custom_call" | custom-call | flops 268435456 | bytes 65536 | tf_op jit(solution)/shard_map/project/pallas_call | solution.py:68
  3.4 1.8 %collective-permute-start = (f32[128,256]{1,0:T(8,128)S(1)}, f32[128,256]{1,0:T(8,128)S(1)}, u32[]{:S(2)}, u32[]{:S(2)}) collective-permute-start(f32[128,256]{1,0:T(8,128)S(1)} %get-tuple-element.22), channel_id=1, source_target_pairs={{0,1},{1,2},{2,3},{3,0},{4,5},{5,6},{6,7},{7,4},{8,9},{9,10},{10,1... | collective-permute-start | bytes 393224 | tf_op jit(solution)/shard_map/ppermute | solution.py:56
  5.2 2.9 %collective-permute-start.1 = (f32[128,256]{1,0:T(8,128)S(1)}, f32[128,256]{1,0:T(8,128)S(1)}, u32[]{:S(2)}, u32[]{:S(2)}) collective-permute-start(f32[128,256]{1,0:T(8,128)S(1)} %get-tuple-element.22), channel_id=1, source_target_pairs={{0,2},{1,3},{2,0},{3,1},{4,6},{5,7},{6,4},{7,5},{8,10},{9,11},{10,... | collective-permute-start | bytes 393224 | tf_op jit(solution)/shard_map/ppermute | solution.py:56
  10.6 11.5 %sketch.1 = (f32[4096,256]{1,0:T(8,128)S(1)}, bf16[4096,2048]{1,0:T(8,128)(2,1)S(1)}, f32[8,128]{1,0:T(8,128)S(1)}) custom-call(bf16[2048,256]{1,0:T(8,128)(2,1)S(1)} %copy-done, bf16[4096,2048]{1,0:T(8,128)(2,1)} %res_hbm.1), custom_call_target="tpu_custom_call" | custom-call | flops 4294967296 | bytes 65536 | tf_op jit(solution)/shard_map/sketch/pallas_call | solution.py:68
  23.5 1.7 %collective-permute-done.3.other_ref = f32[384,256]{1,0:T(8,128)S(1)} collective-permute-done((f32[384,256]{1,0:T(8,128)S(1)}, f32[384,256]{1,0:T(8,128)S(1)}, u32[]{:S(2)}, u32[]{:S(2)}) %collective-permute-start.3) | collective-permute-done | bytes 393248 | tf_op jit(solution)/shard_map/ppermute | solution.py:339
  25.2 8.6 %correct.1 = (bf16[4096,256]{1,0:T(8,128)(2,1)S(1)}, bf16[4096,256]{1,0:T(8,128)(2,1)S(1)}, f32[96,256]{1,0:T(8,128)S(1)}, f32[96,256]{1,0:T(8,128)S(1)}, f32[25...) custom-call(s32[4]{0:T(128)S(1)} %pad_add_fusion.place, ...), custom_call_target="tpu_custom_call" | custom-call | flops 4294967296 | bytes 65536 | tf_op jit(solution)/shard_map/correct/pallas_call | solution.py:68
  35.3 2.1 %collective-permute-start.17 = (bf16[256,256]{1,0:T(8,128)(2,1)S(1)}, bf16[256,256]{1,0:T(8,128)(2,1)S(1)}, u32[]{:S(2)}, u32[]{:S(2)}) collective-permute-start(bf16[256,256]{1,0:T(8,128)(2,1)S(1)} %get-tuple-element.34), channel_id=1, source_target_pairs={{0,3},{1,0},{2,1},{3,2},{4,7},{5,4},{6,5},{7,6},{8,11},{9,8},{10,9... | collective-permute-start | bytes 393224 | tf_op jit(solution)/shard_map/ppermute | solution.py:56
  37.4 3.1 %collective-permute-start.5 = (f32[96,256]{1,0:T(8,128)S(1)}, f32[96,256]{1,0:T(8,128)S(1)}, u32[]{:S(2)}, u32[]{:S(2)}) collective-permute-start(f32[96,256]{1,0:T(8,128)S(1)} %add.133), channel_id=1, source_target_pairs={{0,64},{1,65},{2,66},{3,67},{4,68},{5,69},{6,70},{7,71},{8,72},{9,... | collective-permute-start | bytes 294920 | tf_op jit(solution)/shard_map/ppermute | solution.py:56
  41.1 2.3 %collective-permute-done.15.w1 = bf16[256,256]{1,0:T(8,128)(2,1)S(1)} collective-permute-done((bf16[256,256]{1,0:T(8,128)(2,1)S(1)}, bf16[256,256]{1,0:T(8,128)(2,1)S(1)}, u32[]{:S(2)}, u32[]{:S(2)}) %collective-permute-start.15) | collective-permute-done | bytes 131104 | tf_op jit(solution)/shard_map/ppermute | solution.py:56
  43.4 2.8 %collective-permute-start.7 = (f32[96,256]{1,0:T(8,128)S(1)}, f32[96,256]{1,0:T(8,128)S(1)}, u32[]{:S(2)}, u32[]{:S(2)}) collective-permute-start(f32[96,256]{1,0:T(8,128)S(1)} %add.133), channel_id=1, source_target_pairs={{0,96},{1,97},{2,98},{3,99},{4,100},{5,101},{6,102},{7,103},{8,104... | collective-permute-start | bytes 294920 | tf_op jit(solution)/shard_map/ppermute | solution.py:56
  46.2 5.2 %raw_sums.1.raw_ref = f32[256,2048]{1,0:T(8,128)S(1)} custom-call(bf16[4096,2048]{1,0:T(8,128)(2,1)S(1)} %get-tuple-element.30.res_ref, bf16[4096,256]{1,0:T(8,128)(2,1)S(1)} %get-tuple-element.24.high_ref), custom_call_target="tpu_custom_call" | custom-call | flops 4294967296 | bytes 65536 | tf_op jit(solution)/shard_map/raw_sums/pallas_call | solution.py:68
  51.4 2.3 %finish_raw.1 = (f32[1024,256]{1,0:T(8,128)S(1)}, bf16[1024,256]{1,0:T(8,128)(2,1)}) custom-call(s32[4]{0:T(128)S(1)} %pad_add_fusion.place, f32[256,2048]{1,0:T(8,128)S(1)} %raw_sums.1.raw_ref, bf16[256,2048]{1,0:T(8,128)(2,1)S(1)} %copy-done.1, f32[256,256]{1,0:T(8,128)S(1)} %get-tuple-element.31.w_keep, bf16[256,256]{1,0:T(8,128)(2,1)S(1)} %collective-permute-done.15.w1, ...), custom_call_target="tpu_custom_call" | custom-call | flops 268435456 | bytes 65536 | tf_op jit(solution)/shard_map/finish_raw/pallas_call | solution.py:68
  53.7 4.3 %collective-permute-start.10 = (f32[96,256]{1,0:T(8,128)S(1)}, f32[96,256]{1,0:T(8,128)S(1)}, u32[]{:S(2)}, u32[]{:S(2)}) collective-permute-start(f32[96,256]{1,0:T(8,128)S(1)} %add_add_fusion.3), channel_id=1, source_target_pairs={{0,24},{1,25},{2,26},{3,27},{4,28},{5,29},{6,30},{7,31},{8,0},{9,1... | collective-permute-start | bytes 294920 | tf_op jit(solution)/shard_map/ppermute | solution.py:56
  59.3 3.6 %collective-permute-done.10 = f32[96,256]{1,0:T(8,128)S(1)} collective-permute-done((f32[96,256]{1,0:T(8,128)S(1)}, f32[96,256]{1,0:T(8,128)S(1)}, u32[]{:S(2)}, u32[]{:S(2)}) %collective-permute-start.10) | collective-permute-done | bytes 98336 | tf_op jit(solution)/shard_map/ppermute | solution.py:56
  62.9 2.4 %collective-permute-done.8 = f32[96,256]{1,0:T(8,128)S(1)} collective-permute-done((f32[96,256]{1,0:T(8,128)S(1)}, f32[96,256]{1,0:T(8,128)S(1)}, u32[]{:S(2)}, u32[]{:S(2)}) %collective-permute-start.8) | collective-permute-done | bytes 98336 | tf_op jit(solution)/shard_map/ppermute | solution.py:56
  66.8 3.1 %collective-permute-start.13 = (f32[96,256]{1,0:T(8,128)S(1)}, f32[96,256]{1,0:T(8,128)S(1)}, u32[]{:S(2)}, u32[]{:S(2)}) collective-permute-start(f32[96,256]{1,0:T(8,128)S(1)} %add_add_fusion.2), channel_id=1, source_target_pairs={{0,3},{1,0},{2,1},{3,2},{4,7},{5,4},{6,5},{7,6},{8,11},{9,8},{10,9... | collective-permute-start | bytes 294920 | tf_op jit(solution)/shard_map/ppermute | solution.py:56
  73.4 1.6 %collective-permute-start.21 = (bf16[256,256]{1,0:T(8,128)(2,1)S(1)}, bf16[256,256]{1,0:T(8,128)(2,1)S(1)}, u32[]{:S(2)}, u32[]{:S(2)}) collective-permute-start(bf16[256,256]{1,0:T(8,128)(2,1)S(1)} %get-tuple-element.39), channel_id=1, source_target_pairs={{0,96},{1,97},{2,98},{3,99},{4,100},{5,101},{6,102},{7,103},{8,104... | collective-permute-start | bytes 393224 | tf_op jit(solution)/shard_map/ppermute | solution.py:56
  75.2 3.3 %collective-permute-done.19 = bf16[256,256]{1,0:T(8,128)(2,1)S(1)} collective-permute-done((bf16[256,256]{1,0:T(8,128)(2,1)S(1)}, bf16[256,256]{1,0:T(8,128)(2,1)S(1)}, u32[]{:S(2)}, u32[]{:S(2)}) %collective-permute-start.19) | collective-permute-done | bytes 131104 | tf_op jit(solution)/shard_map/ppermute | solution.py:56
  78.5 1.4 %collective-permute-done.20 = bf16[256,256]{1,0:T(8,128)(2,1)S(1)} collective-permute-done((bf16[256,256]{1,0:T(8,128)(2,1)S(1)}, bf16[256,256]{1,0:T(8,128)(2,1)S(1)}, u32[]{:S(2)}, u32[]{:S(2)}) %collective-permute-start.20) | collective-permute-done | bytes 131104 | tf_op jit(solution)/shard_map/ppermute | solution.py:56
  81.4 2.4 %collective-permute-start.24 = (f32[64,256]{1,0:T(8,128)S(1)}, f32[64,256]{1,0:T(8,128)S(1)}, u32[]{:S(2)}, u32[]{:S(2)}) collective-permute-start(f32[64,256]{1,0:T(8,128)S(1)} %get-tuple-element.42), channel_id=1, source_target_pairs={{0,24},{1,25},{2,26},{3,27},{4,28},{5,29},{6,30},{7,31},{8,0},{9,1... | collective-permute-start | bytes 196616 | tf_op jit(solution)/shard_map/ppermute | solution.py:56
  83.8 10.8 %factor.1 = (f32[256,256]{1,0:T(8,128)S(1)}, bf16[256,256]{1,0:T(8,128)(2,1)S(1)}, bf16[256,256]{1,0:T(8,128)(2,1)S(1)}) custom-call(s32[4]{0:T(128)S(1)} %pad_add_fusion.place, f32[96,256]{1,0:T(8,128)S(1)} %add_add_fusion.1.mine_ref, f32[96,256]{1,0:T(8,128)S(1)} %collective-permute-done.14.other_ref), custom_call_target="tpu_custom_call" | custom-call | flops 8589934592 | bytes 65536 | tf_op jit(solution)/shard_map/factor/pallas_call | solution.py:68
  94.9 2.1 %collective-permute-start.26 = (f32[16,256]{1,0:T(8,128)S(1)}, f32[16,256]{1,0:T(8,128)S(1)}, u32[]{:S(2)}, u32[]{:S(2)}) collective-permute-start(f32[16,256]{1,0:T(8,128)S(1)} %get-tuple-element.45), channel_id=1, source_target_pairs={{0,2},{1,3},{2,0},{3,1},{4,6},{5,7},{6,4},{7,5},{8,10},{9,11},{10,... | collective-permute-start | bytes 49160 | tf_op jit(solution)/shard_map/ppermute | solution.py:56
  97.0 2.4 %collective-permute-start.27 = (f32[16,256]{1,0:T(8,128)S(1)}, f32[16,256]{1,0:T(8,128)S(1)}, u32[]{:S(2)}, u32[]{:S(2)}) collective-permute-start(f32[16,256]{1,0:T(8,128)S(1)} %get-tuple-element.44), channel_id=1, source_target_pairs={{0,3},{1,0},{2,1},{3,2},{4,7},{5,4},{6,5},{7,6},{8,11},{9,8},{10,9... | collective-permute-start | bytes 49160 | tf_op jit(solution)/shard_map/ppermute | solution.py:56
  99.3 3.2 %basis.1 = f32[4096,256]{1,0:T(8,128)} custom-call(bf16[4096,256]{1,0:T(8,128)(2,1)S(1)} %get-tuple-element.24.high_ref, bf16[4096,256]{1,0:T(8,128)(2,1)S(1)} %copy-done.3, bf16[256,256]{1,0:T(8,128)(2,1)S(1)} %get-tuple-element.28.inv_high, bf16[256,256]{1,0:T(8,128)(2,1)S(1)} %get-tuple-element.29.inv_low), custom_call_target="tpu_custom_call" | custom-call | flops 1610612736 | bytes 65536 | tf_op jit(solution)/shard_map/basis/pallas_call | solution.py:68
  (65 shorter events, 15.4 us)
Async XLA Ops:
  3.4 19.3 %collective-permute-start = (f32[128,256]{1,0:T(8,128)S(1)}, f32[128,256]{1,0:T(8,128)S(1)}, u32[]{:S(2)}, u32[]{:S(2)}) collective-permute-start(f32[128,256]{1,0:T(8,128)S(1)} %get-tuple-element.22), channel_id=1, source_target_pairs={{0,1},{1,2},{2,3},{3,0},{4,5},{5,6},{6,7},{7,4},{8,9},{9,10},{10,1... | collective-permute-start | bytes 393224 | tf_op jit(solution)/shard_map/ppermute | solution.py:56
  5.2 17.5 %collective-permute-start.1 = (f32[128,256]{1,0:T(8,128)S(1)}, f32[128,256]{1,0:T(8,128)S(1)}, u32[]{:S(2)}, u32[]{:S(2)}) collective-permute-start(f32[128,256]{1,0:T(8,128)S(1)} %get-tuple-element.22), channel_id=1, source_target_pairs={{0,2},{1,3},{2,0},{3,1},{4,6},{5,7},{6,4},{7,5},{8,10},{9,11},{10,... | collective-permute-start | bytes 393224 | tf_op jit(solution)/shard_map/ppermute | solution.py:56
  8.1 14.6 %collective-permute-start.2 = (f32[128,256]{1,0:T(8,128)S(1)}, f32[128,256]{1,0:T(8,128)S(1)}, u32[]{:S(2)}, u32[]{:S(2)}) collective-permute-start(f32[128,256]{1,0:T(8,128)S(1)} %get-tuple-element.22), channel_id=1, source_target_pairs={{0,3},{1,0},{2,1},{3,2},{4,7},{5,4},{6,5},{7,6},{8,11},{9,8},{10,9... | collective-permute-start | bytes 393224 | tf_op jit(solution)/shard_map/ppermute | solution.py:56
  33.8 9.6 %collective-permute-start.15 = (bf16[256,256]{1,0:T(8,128)(2,1)S(1)}, bf16[256,256]{1,0:T(8,128)(2,1)S(1)}, u32[]{:S(2)}, u32[]{:S(2)}) collective-permute-start(bf16[256,256]{1,0:T(8,128)(2,1)S(1)} %get-tuple-element.32), channel_id=1, source_target_pairs={{0,1},{1,2},{2,3},{3,0},{4,5},{5,6},{6,7},{7,4},{8,9},{9,10},{10,1... | collective-permute-start | bytes 393224 | tf_op jit(solution)/shard_map/ppermute | solution.py:56
  34.5 16.8 %collective-permute-start.16 = (bf16[256,256]{1,0:T(8,128)(2,1)S(1)}, bf16[256,256]{1,0:T(8,128)(2,1)S(1)}, u32[]{:S(2)}, u32[]{:S(2)}) collective-permute-start(bf16[256,256]{1,0:T(8,128)(2,1)S(1)} %get-tuple-element.33), channel_id=1, source_target_pairs={{0,2},{1,3},{2,0},{3,1},{4,6},{5,7},{6,4},{7,5},{8,10},{9,11},{10,... | collective-permute-start | bytes 393224 | tf_op jit(solution)/shard_map/ppermute | solution.py:56
  35.3 16.1 %collective-permute-start.17 = (bf16[256,256]{1,0:T(8,128)(2,1)S(1)}, bf16[256,256]{1,0:T(8,128)(2,1)S(1)}, u32[]{:S(2)}, u32[]{:S(2)}) collective-permute-start(bf16[256,256]{1,0:T(8,128)(2,1)S(1)} %get-tuple-element.34), channel_id=1, source_target_pairs={{0,3},{1,0},{2,1},{3,2},{4,7},{5,4},{6,5},{7,6},{8,11},{9,8},{10,9... | collective-permute-start | bytes 393224 | tf_op jit(solution)/shard_map/ppermute | solution.py:56
  37.4 16.3 %collective-permute-start.5 = (f32[96,256]{1,0:T(8,128)S(1)}, f32[96,256]{1,0:T(8,128)S(1)}, u32[]{:S(2)}, u32[]{:S(2)}) collective-permute-start(f32[96,256]{1,0:T(8,128)S(1)} %add.133), channel_id=1, source_target_pairs={{0,64},{1,65},{2,66},{3,67},{4,68},{5,69},{6,70},{7,71},{8,72},{9,... | collective-permute-start | bytes 294920 | tf_op jit(solution)/shard_map/ppermute | solution.py:56
  40.5 13.2 %collective-permute-start.6 = (f32[96,256]{1,0:T(8,128)S(1)}, f32[96,256]{1,0:T(8,128)S(1)}, u32[]{:S(2)}, u32[]{:S(2)}) collective-permute-start(f32[96,256]{1,0:T(8,128)S(1)} %add.133), channel_id=1, source_target_pairs={{0,32},{1,33},{2,34},{3,35},{4,36},{5,37},{6,38},{7,39},{8,40},{9,... | collective-permute-start | bytes 294920 | tf_op jit(solution)/shard_map/ppermute | solution.py:56
  43.4 10.3 %collective-permute-start.7 = (f32[96,256]{1,0:T(8,128)S(1)}, f32[96,256]{1,0:T(8,128)S(1)}, u32[]{:S(2)}, u32[]{:S(2)}) collective-permute-start(f32[96,256]{1,0:T(8,128)S(1)} %add.133), channel_id=1, source_target_pairs={{0,96},{1,97},{2,98},{3,99},{4,100},{5,101},{6,102},{7,103},{8,104... | collective-permute-start | bytes 294920 | tf_op jit(solution)/shard_map/ppermute | solution.py:56
  53.7 16.1 %collective-permute-start.18 = (bf16[1024,256]{1,0:T(8,128)(2,1)}, bf16[1024,256]{1,0:T(8,128)(2,1)}, u32[]{:S(2)}, u32[]{:S(2)}) collective-permute-start(bf16[1024,256]{1,0:T(8,128)(2,1)} %get-tuple-element.36), channel_id=1, source_target_pairs={{0,4},{1,5},{2,6},{3,7},{4,0},{5,1},{6,2},{7,3},{8,12},{9,13},{10,... | collective-permute-start | bytes 1572872 | tf_op jit(solution)/shard_map/ppermute | solution.py:368
  53.7 9.1 %collective-permute-start.10 = (f32[96,256]{1,0:T(8,128)S(1)}, f32[96,256]{1,0:T(8,128)S(1)}, u32[]{:S(2)}, u32[]{:S(2)}) collective-permute-start(f32[96,256]{1,0:T(8,128)S(1)} %add_add_fusion.3), channel_id=1, source_target_pairs={{0,24},{1,25},{2,26},{3,27},{4,28},{5,29},{6,30},{7,31},{8,0},{9,1... | collective-permute-start | bytes 294920 | tf_op jit(solution)/shard_map/ppermute | solution.py:56
  58.0 7.2 %collective-permute-start.8 = (f32[96,256]{1,0:T(8,128)S(1)}, f32[96,256]{1,0:T(8,128)S(1)}, u32[]{:S(2)}, u32[]{:S(2)}) collective-permute-start(f32[96,256]{1,0:T(8,128)S(1)} %add_add_fusion.3), channel_id=1, source_target_pairs={{0,16},{1,17},{2,18},{3,19},{4,20},{5,21},{6,22},{7,23},{8,24},{9,... | collective-permute-start | bytes 294920 | tf_op jit(solution)/shard_map/ppermute | solution.py:56
  58.0 8.2 %collective-permute-start.9 = (f32[96,256]{1,0:T(8,128)S(1)}, f32[96,256]{1,0:T(8,128)S(1)}, u32[]{:S(2)}, u32[]{:S(2)}) collective-permute-start(f32[96,256]{1,0:T(8,128)S(1)} %add_add_fusion.3), channel_id=1, source_target_pairs={{0,8},{1,9},{2,10},{3,11},{4,12},{5,13},{6,14},{7,15},{8,16},{9,17... | collective-permute-start | bytes 294920 | tf_op jit(solution)/shard_map/ppermute | solution.py:56
  66.3 7.1 %collective-permute-start.11 = (f32[96,256]{1,0:T(8,128)S(1)}, f32[96,256]{1,0:T(8,128)S(1)}, u32[]{:S(2)}, u32[]{:S(2)}) collective-permute-start(f32[96,256]{1,0:T(8,128)S(1)} %add_add_fusion.2), channel_id=1, source_target_pairs={{0,2},{1,3},{2,0},{3,1},{4,6},{5,7},{6,4},{7,5},{8,10},{9,11},{10,... | collective-permute-start | bytes 294920 | tf_op jit(solution)/shard_map/ppermute | solution.py:56
  66.6 8.4 %collective-permute-start.12 = (f32[96,256]{1,0:T(8,128)S(1)}, f32[96,256]{1,0:T(8,128)S(1)}, u32[]{:S(2)}, u32[]{:S(2)}) collective-permute-start(f32[96,256]{1,0:T(8,128)S(1)} %add_add_fusion.2), channel_id=1, source_target_pairs={{0,1},{1,2},{2,3},{3,0},{4,5},{5,6},{6,7},{7,4},{8,9},{9,10},{10,1... | collective-permute-start | bytes 294920 | tf_op jit(solution)/shard_map/ppermute | solution.py:56
  66.8 8.3 %collective-permute-start.13 = (f32[96,256]{1,0:T(8,128)S(1)}, f32[96,256]{1,0:T(8,128)S(1)}, u32[]{:S(2)}, u32[]{:S(2)}) collective-permute-start(f32[96,256]{1,0:T(8,128)S(1)} %add_add_fusion.2), channel_id=1, source_target_pairs={{0,3},{1,0},{2,1},{3,2},{4,7},{5,4},{6,5},{7,6},{8,11},{9,8},{10,9... | collective-permute-start | bytes 294920 | tf_op jit(solution)/shard_map/ppermute | solution.py:56
  71.0 7.4 %collective-permute-start.19 = (bf16[256,256]{1,0:T(8,128)(2,1)S(1)}, bf16[256,256]{1,0:T(8,128)(2,1)S(1)}, u32[]{:S(2)}, u32[]{:S(2)}) collective-permute-start(bf16[256,256]{1,0:T(8,128)(2,1)S(1)} %get-tuple-element.38), channel_id=1, source_target_pairs={{0,64},{1,65},{2,66},{3,67},{4,68},{5,69},{6,70},{7,71},{8,72},{9,... | collective-permute-start | bytes 393224 | tf_op jit(solution)/shard_map/ppermute | solution.py:56
  71.8 8.1 %collective-permute-start.20 = (bf16[256,256]{1,0:T(8,128)(2,1)S(1)}, bf16[256,256]{1,0:T(8,128)(2,1)S(1)}, u32[]{:S(2)}, u32[]{:S(2)}) collective-permute-start(bf16[256,256]{1,0:T(8,128)(2,1)S(1)} %get-tuple-element.40), channel_id=1, source_target_pairs={{0,32},{1,33},{2,34},{3,35},{4,36},{5,37},{6,38},{7,39},{8,40},{9,... | collective-permute-start | bytes 393224 | tf_op jit(solution)/shard_map/ppermute | solution.py:56
  75.1 8.7 %collective-permute-start.14 = (f32[96,256]{1,0:T(8,128)S(1)}, f32[96,256]{1,0:T(8,128)S(1)}, u32[]{:S(2)}, u32[]{:S(2)}) collective-permute-start(f32[96,256]{1,0:T(8,128)S(1)} %add_add_fusion.1.mine_ref), channel_id=1, source_target_pairs={{0,4},{1,5},{2,6},{3,7},{4,0},{5,1},{6,2},{7,3},{8,12},{9,13},{10,... | collective-permute-start | bytes 294920 | tf_op jit(solution)/shard_map/ppermute | solution.py:362
  80.0 14.6 %collective-permute-start.22 = (f32[64,256]{1,0:T(8,128)S(1)}, f32[64,256]{1,0:T(8,128)S(1)}, u32[]{:S(2)}, u32[]{:S(2)}) collective-permute-start(f32[64,256]{1,0:T(8,128)S(1)} %get-tuple-element.41), channel_id=1, source_target_pairs={{0,16},{1,17},{2,18},{3,19},{4,20},{5,21},{6,22},{7,23},{8,24},{9,... | collective-permute-start | bytes 196616 | tf_op jit(solution)/shard_map/ppermute | solution.py:56
  80.6 14.0 %collective-permute-start.23 = (f32[64,256]{1,0:T(8,128)S(1)}, f32[64,256]{1,0:T(8,128)S(1)}, u32[]{:S(2)}, u32[]{:S(2)}) collective-permute-start(f32[64,256]{1,0:T(8,128)S(1)} %get-tuple-element.43), channel_id=1, source_target_pairs={{0,8},{1,9},{2,10},{3,11},{4,12},{5,13},{6,14},{7,15},{8,16},{9,17... | collective-permute-start | bytes 196616 | tf_op jit(solution)/shard_map/ppermute | solution.py:56
  81.4 13.2 %collective-permute-start.24 = (f32[64,256]{1,0:T(8,128)S(1)}, f32[64,256]{1,0:T(8,128)S(1)}, u32[]{:S(2)}, u32[]{:S(2)}) collective-permute-start(f32[64,256]{1,0:T(8,128)S(1)} %get-tuple-element.42), channel_id=1, source_target_pairs={{0,24},{1,25},{2,26},{3,27},{4,28},{5,29},{6,30},{7,31},{8,0},{9,1... | collective-permute-start | bytes 196616 | tf_op jit(solution)/shard_map/ppermute | solution.py:56
  94.7 7.9 %collective-permute-start.25 = (f32[16,256]{1,0:T(8,128)S(1)}, f32[16,256]{1,0:T(8,128)S(1)}, u32[]{:S(2)}, u32[]{:S(2)}) collective-permute-start(f32[16,256]{1,0:T(8,128)S(1)} %get-tuple-element.46), channel_id=1, source_target_pairs={{0,1},{1,2},{2,3},{3,0},{4,5},{5,6},{6,7},{7,4},{8,9},{9,10},{10,1... | collective-permute-start | bytes 49160 | tf_op jit(solution)/shard_map/ppermute | solution.py:56
  94.9 7.7 %collective-permute-start.26 = (f32[16,256]{1,0:T(8,128)S(1)}, f32[16,256]{1,0:T(8,128)S(1)}, u32[]{:S(2)}, u32[]{:S(2)}) collective-permute-start(f32[16,256]{1,0:T(8,128)S(1)} %get-tuple-element.45), channel_id=1, source_target_pairs={{0,2},{1,3},{2,0},{3,1},{4,6},{5,7},{6,4},{7,5},{8,10},{9,11},{10,... | collective-permute-start | bytes 49160 | tf_op jit(solution)/shard_map/ppermute | solution.py:56
  (10 other events, 107.6 us)

commit v4 on v3

--- a/solution.py
+++ b/solution.py
@@ -7,12 +7,14 @@
 from jax.experimental.pallas import tpu as pltpu
 from jax.sharding import PartitionSpec as P
 
+
 GROUP = 64
 USES = 4
 BLOCK_STARS = 128
 MODES = 256
 STARS = 524288
 AXES = ("rows", "units")
+DEPTH = 2
 F32 = jnp.float32
 BF16 = jnp.bfloat16
 HIGHEST = lax.Precision.HIGHEST
@@ -51,16 +53,26 @@
     "z": [permutation(lambda x, z, c, y, k=k: (x, (z + k) % 4, c, y)) for k in (1, 2, 3)],
 }
 
+PAIRS = {
+    "x": [permutation(lambda x, z, c, y: (x ^ 1, z, c, y)), permutation(lambda x, z, c, y: (3 - x, z, c, y))],
+    "y": [permutation(lambda x, z, c, y: (x, z, c, y ^ 1)), permutation(lambda x, z, c, y: (x, z, c, 3 - y))],
+    "z": [permutation(lambda x, z, c, y: (x, z ^ 1, c, y)), permutation(lambda x, z, c, y: (x, 3 - z, c, y))],
+}
+
+
+def send(value, pairs):
+    return lax.ppermute(value, AXES, pairs)
+
 
 def shift_all(axis, pieces):
-    return [lax.ppermute(p, AXES, SHIFTS[axis][k]) for k, p in enumerate(pieces)]
+    return [send(p, SHIFTS[axis][k]) for k, p in enumerate(pieces)]
 
 
 def on_chip(shape, kind=F32):
     return pltpu.VMEM(shape, kind)
 
 
-def resident(kernel, name, scalars, arrays, outs, scratch=(), flops=0, limit=16, out_specs=None, far=()):
+def resident(kernel, scalars, arrays, outs, scratch=(), flops=0, limit=16, out_specs=None, far=()):
     vmem = pl.BlockSpec(memory_space=pltpu.VMEM)
     smem = pl.BlockSpec(memory_space=pltpu.SMEM)
     arrays = [pltpu.with_memory_space_constraint(a, pltpu.VMEM) for a in arrays]
@@ -73,11 +85,10 @@
         scratch_shapes=list(scratch),
         compiler_params=pltpu.CompilerParams(vmem_limit_bytes=limit << 20),
         cost_estimate=pl.CostEstimate(flops=flops, bytes_accessed=1 << 16, transcendentals=0),
-        name=name,
     )(*scalars, *arrays, *far)
 
 
-def project_kernel(place, zero_hbm, sketch_hbm, full_ref, half_ref, zero, sketch, sems):
+def project_kernel(place, zero_hbm, sketch_hbm, full_ref, half_ref, sketch, zero, sems):
     copies = [
         pltpu.make_async_copy(zero_hbm, zero, sems.at[0]),
         pltpu.make_async_copy(sketch_hbm, sketch, sems.at[1]),
@@ -97,9 +108,12 @@
     for i in range(tiles):
         rows = pl.ds(i * tile, tile)
         copies.append(pltpu.make_async_copy(res_hbm.at[rows, :], res_ref.at[rows, :], sems.at[i]))
+    for i in range(DEPTH):
         copies[i].start()
     for i in range(tiles):
         copies[i].wait()
+        if i + DEPTH < tiles:
+            copies[i + DEPTH].start()
         rows = pl.ds(i * tile, tile)
         out_ref[rows, :] = jnp.dot(res_ref[rows, :], sketch_ref[...], preferred_element_type=F32)
     flag_ref[...] = jnp.zeros_like(flag_ref)
@@ -266,6 +280,7 @@
 def dot_plain(a, b):
     return jnp.dot(a, b, preferred_element_type=F32, precision=HIGHEST)
 
+
 def dot_plain(a, b):
     return jnp.dot(a, b, preferred_element_type=F32, precision=HIGHEST)
 
@@ -319,26 +334,22 @@
     x, z, c, y = r // 8, (r // 2) % 4, r % 2, lax.axis_index("units")
     place = jnp.stack([x, z, c, y]).astype(jnp.int32)
     square = (MODES, MODES)
-    own, half = resident(
-        project_kernel, "project", [place], [],
-        [on_chip((units, MODES)), on_chip((units // 2, MODES))],
-        [
-            pltpu.VMEM((units, bins), BF16),
-            pltpu.VMEM((bins, MODES), BF16),
-            pltpu.SemaphoreType.DMA((2,)),
-        ],
+    own, half, sketch_near = resident(
+        project_kernel, [place], [],
+        [on_chip((units, MODES)), on_chip((units // 2, MODES)), on_chip((bins, MODES), BF16)],
+        [pltpu.VMEM((units, bins), BF16), pltpu.SemaphoreType.DMA((2,))],
         flops=2 * units * bins * MODES, far=[zero_points, sketch_matrix],
     )
     shifted = shift_all("y", [half] * 3)
     part, residuals, flag = resident(
-        functools.partial(sketch_kernel, 8), "sketch", [], [sketch_matrix],
-        [on_chip((rows, MODES)), on_chip((rows, bins), BF16), jax.ShapeDtypeStruct((8, 128), F32)],
+        functools.partial(sketch_kernel, 8), [], [sketch_near],
+        [on_chip((rows, MODES)), on_chip((rows, bins), BF16), on_chip((8, 128))],
         [pltpu.SemaphoreType.DMA((8,))], flops=2 * rows * bins * MODES, far=[residuals],
     )
     halves = jnp.concatenate(shifted, axis=0) + flag[0, 0]
-    others = lax.ppermute(halves, AXES, SWAP)
+    others = send(halves, SWAP)
     high, low, gram_keep, gram_send, w_keep, *w_sends = resident(
-        functools.partial(correct_kernel, 4), "correct", [place, use_lists.T],
+        functools.partial(correct_kernel, 4), [place, use_lists.T],
         [part, loadings, own, halves, others],
         [on_chip((rows, MODES), BF16)] * 2 + [on_chip((96, MODES))] * 2 + [on_chip((units, MODES))]
         + [on_chip((units, MODES), BF16)] * 3,
@@ -352,37 +363,38 @@
         flops=2 * rows * bins * MODES,
     )
     w_got = shift_all("y", w_sends)
-    gram = gram_keep + lax.ppermute(gram_send, AXES, SWAP)
+    gram = gram_keep + send(gram_send, SWAP)
     raw, = resident(
-        functools.partial(raw_kernel, 512), "raw_sums", [], [residuals, high],
+        functools.partial(raw_kernel, 512), [], [residuals, high],
         [on_chip((MODES, bins))], flops=2 * rows * bins * MODES,
     )
     for axis in "xzy":
-        gram = add_four(gram, shift_all(axis, [gram] * 3))
-    gram_other = lax.ppermute(gram, AXES, SWAP)
-    keep, send = resident(
-        finish_kernel, "finish_raw", [place], [raw, zero_points, w_keep, *w_got],
+        for pairs in PAIRS[axis]:
+            gram = gram + send(gram, pairs)
+    gram_other = send(gram, SWAP)
+    keep, sent = resident(
+        finish_kernel, [place], [raw, zero_points, w_keep, *w_got],
         [on_chip((bins // 2, MODES)), on_chip((bins // 2, MODES), BF16)],
         [pltpu.VMEM((bins, MODES), F32)], flops=2 * units * bins * MODES,
     )
-    total = keep + lax.ppermute(send, AXES, SWAP).astype(F32)
-    keep, sends = quarters(x, total, BF16)
+    arrived = send(sent, SWAP)
+    keep, sends = quarters(x, keep + arrived.astype(F32), BF16)
     keep, sends = quarters(z, add_four(keep, [g.astype(F32) for g in shift_all("x", sends)]), F32)
     keep, sends = quarters(y, add_four(keep, shift_all("z", sends)), F32)
     raw_got = shift_all("y", sends)
     inverse, inv_high, inv_low = resident(
-        factor_kernel, "factor", [place], [gram, gram_other],
+        factor_kernel, [place], [gram, gram_other],
         [on_chip(square), on_chip(square, BF16), on_chip(square, BF16)],
         [pltpu.VMEM((128, 128), F32)] * 2, flops=1 << 33,
     )
     star_basis, = resident(
-        functools.partial(basis_kernel, 4), "basis", [], [high, low, inv_high, inv_low],
+        functools.partial(basis_kernel, 4), [], [high, low, inv_high, inv_low],
         [jax.ShapeDtypeStruct((rows, MODES), F32)],
         [pltpu.VMEM((rows, MODES), F32), pltpu.SemaphoreType.DMA((4,))],
         flops=6 * rows * MODES * MODES, out_specs=[pl.BlockSpec(memory_space=pltpu.HBM)],
     )
     bin_modes, = resident(
-        modes_kernel, "modes", [], [keep, *raw_got, inverse],
+        modes_kernel, [], [keep, *raw_got, inverse],
         [jax.ShapeDtypeStruct((keep.shape[0], MODES), F32)], flops=1 << 28,
     )
     return (star_basis, bin_modes)
@@ -397,6 +409,4 @@
         P(("rows", "units"), None),
     )
     out_specs = (P(("rows", "units"), None), P(("rows", "units"), None))
-    return jax.shard_map(
-        on_device, mesh=mesh, in_specs=in_specs, out_specs=out_specs, check_vma=False
-    )
+    return jax.shard_map(on_device, mesh=mesh, in_specs=in_specs, out_specs=out_specs, check_vma=False)

time: 104 us -> 110 us (1.058)
  waiting for transfers between devices: 16.4 us -> 20.5 us
  starting transfers between devices: 37.1 us -> 39 us
    ppermute x28 -> x25, waiting for transfers between devices: 16.4 us -> 20.5 us  [send(): return lax.ppermute(value, AXES, pairs)]
    ppermute x28 -> x25, starting transfers between devices: 37.1 us -> 39 us  [send(): return lax.ppermute(value, AXES, pairs)]
  transfers between devices with their start and end apart: 28 -> 25, of which waited for: 8 -> 9; matrix products, arithmetic and copies ran while one was open for 2% -> 3% of each run, Pallas kernels for 32% -> 28%
where the time goes in v4:
time: 110 us
  Pallas kernels  45.1 us (41%)
  starting transfers between devices  39 us (35%)
  waiting for transfers between devices  20.5 us (19%)
  other arithmetic  3.07 us (3%)
  local copies, waits for them, and re-layouts  1.58 us (1%)
    pallas_call x8, Pallas kernels, resident(): pl.pallas_call(kernel, in_specs=[smem] * len(scalars) + [vmem] * len(arra...  45.1 us
    ppermute x25, starting transfers between devices, send(): return lax.ppermute(value, AXES, pairs)  39 us
    ppermute x25, waiting for transfers between devices, send(): return lax.ppermute(value, AXES, pairs)  20.5 us
  transfers between devices with their start and end apart: 25, of which 9 were waited for; matrix products, arithmetic and copies ran while one was open for 3% of the time, Pallas kernels for 28%

profile of v4, /device:TPU:0, one launch (start us, length us, event | category | flops | bytes accessed | tf_op | source)
XLA Modules:
  0.0 110.1 jit_solution(10601551660399871195)
XLA Ops:
  0.8 2.6 %shard_map.68 = (f32[256,256]{1,0:T(8,128)S(1)}, f32[128,256]{1,0:T(8,128)S(1)}, bf16[2048,256]{1,0:T(8,128)(2,1)S(1)}) custom-call(s32[4]{0:T(128)S(1)} %pad_add_fusion.place, bf16[256,2048]{1,0:T(8,128)(2,1)} %zero_ref.1, bf16[2048,256]{1,0:T(8,128)(2,1)} %sketch_hbm.1), custom_call_target="tpu_custom_call" | custom-call | flops 268435456 | bytes 65536 | tf_op jit(solution)/shard_map/pallas_call | solution.py:80
  3.3 1.8 %collective-permute-start = (f32[128,256]{1,0:T(8,128)S(1)}, f32[128,256]{1,0:T(8,128)S(1)}, u32[]{:S(2)}, u32[]{:S(2)}) collective-permute-start(f32[128,256]{1,0:T(8,128)S(1)} %get-tuple-element.24), channel_id=1, source_target_pairs={{0,1},{1,2},{2,3},{3,0},{4,5},{5,6},{6,7},{7,4},{8,9},{9,10},{10,1... | collective-permute-start | bytes 393224 | tf_op jit(solution)/shard_map/ppermute | solution.py:64
  5.1 2.9 %collective-permute-start.1 = (f32[128,256]{1,0:T(8,128)S(1)}, f32[128,256]{1,0:T(8,128)S(1)}, u32[]{:S(2)}, u32[]{:S(2)}) collective-permute-start(f32[128,256]{1,0:T(8,128)S(1)} %get-tuple-element.24), channel_id=1, source_target_pairs={{0,2},{1,3},{2,0},{3,1},{4,6},{5,7},{6,4},{7,5},{8,10},{9,11},{10,... | collective-permute-start | bytes 393224 | tf_op jit(solution)/shard_map/ppermute | solution.py:64
  9.3 11.6 %shard_map.69 = (f32[4096,256]{1,0:T(8,128)S(1)}, bf16[4096,2048]{1,0:T(8,128)(2,1)S(1)}, f32[8,128]{1,0:T(8,128)S(1)}) custom-call(bf16[2048,256]{1,0:T(8,128)(2,1)S(1)} %get-tuple-element.21.sketch_ref, bf16[4096,2048]{1,0:T(8,128)(2,1)} %res_hbm.1), custom_call_target="tpu_custom_call" | custom-call | flops 4294967296 | bytes 65536 | tf_op jit(solution)/shard_map/pallas_call | solution.py:80
  24.0 8.5 %shard_map.70 = (bf16[4096,256]{1,0:T(8,128)(2,1)S(1)}, bf16[4096,256]{1,0:T(8,128)(2,1)S(1)}, f32[96,256]{1,0:T(8,128)S(1)}, f32[96,256]{1,0:T(8,128)S(1)}, f32...) custom-call(s32[4]{0:T(128)S(1)} %pad_add_fusion.place, ...), custom_call_target="tpu_custom_call" | custom-call | flops 4294967296 | bytes 65536 | tf_op jit(solution)/shard_map/pallas_call | solution.py:80
  34.0 2.0 %collective-permute-start.14 = (bf16[256,256]{1,0:T(8,128)(2,1)S(1)}, bf16[256,256]{1,0:T(8,128)(2,1)S(1)}, u32[]{:S(2)}, u32[]{:S(2)}) collective-permute-start(bf16[256,256]{1,0:T(8,128)(2,1)S(1)} %get-tuple-element.36), channel_id=1, source_target_pairs={{0,3},{1,0},{2,1},{3,2},{4,7},{5,4},{6,5},{7,6},{8,11},{9,8},{10,9... | collective-permute-start | bytes 393224 | tf_op jit(solution)/shard_map/ppermute | solution.py:64
  36.0 5.2 %shard_map.73.raw_ref = f32[256,2048]{1,0:T(8,128)S(1)} custom-call(bf16[4096,2048]{1,0:T(8,128)(2,1)S(1)} %get-tuple-element.32.res_ref, bf16[4096,256]{1,0:T(8,128)(2,1)S(1)} %get-tuple-element.26.high_ref), custom_call_target="tpu_custom_call" | custom-call | flops 4294967296 | bytes 65536 | tf_op jit(solution)/shard_map/pallas_call | solution.py:80
  42.8 2.3 %shard_map.74 = (f32[1024,256]{1,0:T(8,128)S(1)}, bf16[1024,256]{1,0:T(8,128)(2,1)}) custom-call(s32[4]{0:T(128)S(1)} %pad_add_fusion.place, f32[256,2048]{1,0:T(8,128)S(1)} %shard_map.73.raw_ref, bf16[256,2048]{1,0:T(8,128)(2,1)S(1)} %copy-done, f32[256,256]{1,0:T(8,128)S(1)} %get-tuple-element.33.w_keep, bf16[256,256]{1,0:T(8,128)(2,1)S(1)} %collective-permute-done.12.w1, ...), custom_call_target="tpu_custom_call" | custom-call | flops 268435456 | bytes 65536 | tf_op jit(solution)/shard_map/pallas_call | solution.py:80
  48.9 3.3 %collective-permute-done.5 = f32[96,256]{1,0:T(8,128)S(1)} collective-permute-done((f32[96,256]{1,0:T(8,128)S(1)}, f32[96,256]{1,0:T(8,128)S(1)}, u32[]{:S(2)}, u32[]{:S(2)}) %collective-permute-start.5) | collective-permute-done | bytes 98336 | tf_op jit(solution)/shard_map/ppermute | solution.py:64
  52.3 2.8 %collective-permute-start.6 = (f32[96,256]{1,0:T(8,128)S(1)}, f32[96,256]{1,0:T(8,128)S(1)}, u32[]{:S(2)}, u32[]{:S(2)}) collective-permute-start(f32[96,256]{1,0:T(8,128)S(1)} %add.125), channel_id=1, source_target_pairs={{0,96},{1,97},{2,98},{3,99},{4,100},{5,101},{6,102},{7,103},{8,104... | collective-permute-start | bytes 294920 | tf_op jit(solution)/shard_map/ppermute | solution.py:64
  55.1 3.1 %collective-permute-done.6 = f32[96,256]{1,0:T(8,128)S(1)} collective-permute-done((f32[96,256]{1,0:T(8,128)S(1)}, f32[96,256]{1,0:T(8,128)S(1)}, u32[]{:S(2)}, u32[]{:S(2)}) %collective-permute-start.6) | collective-permute-done | bytes 98336 | tf_op jit(solution)/shard_map/ppermute | solution.py:64
  58.2 2.0 %collective-permute-start.7 = (f32[96,256]{1,0:T(8,128)S(1)}, f32[96,256]{1,0:T(8,128)S(1)}, u32[]{:S(2)}, u32[]{:S(2)}) collective-permute-start(f32[96,256]{1,0:T(8,128)S(1)} %add.126), channel_id=1, source_target_pairs={{0,8},{1,9},{2,10},{3,11},{4,12},{5,13},{6,14},{7,15},{8,0},{9,1},... | collective-permute-start | bytes 294920 | tf_op jit(solution)/shard_map/ppermute | solution.py:64
  60.2 2.7 %collective-permute-done.7 = f32[96,256]{1,0:T(8,128)S(1)} collective-permute-done((f32[96,256]{1,0:T(8,128)S(1)}, f32[96,256]{1,0:T(8,128)S(1)}, u32[]{:S(2)}, u32[]{:S(2)}) %collective-permute-start.7) | collective-permute-done | bytes 98336 | tf_op jit(solution)/shard_map/ppermute | solution.py:64
  62.9 4.3 %collective-permute-start.8 = (f32[96,256]{1,0:T(8,128)S(1)}, f32[96,256]{1,0:T(8,128)S(1)}, u32[]{:S(2)}, u32[]{:S(2)}) collective-permute-start(f32[96,256]{1,0:T(8,128)S(1)} %add.127), channel_id=1, source_target_pairs={{0,24},{1,25},{2,26},{3,27},{4,28},{5,29},{6,30},{7,31},{8,16},{9,... | collective-permute-start | bytes 294920 | tf_op jit(solution)/shard_map/ppermute | solution.py:64
  67.2 2.6 %collective-permute-done.8 = f32[96,256]{1,0:T(8,128)S(1)} collective-permute-done((f32[96,256]{1,0:T(8,128)S(1)}, f32[96,256]{1,0:T(8,128)S(1)}, u32[]{:S(2)}, u32[]{:S(2)}) %collective-permute-start.8) | collective-permute-done | bytes 98336 | tf_op jit(solution)/shard_map/ppermute | solution.py:64
  72.5 1.9 %collective-permute-start.16 = (bf16[256,256]{1,0:T(8,128)(2,1)S(1)}, bf16[256,256]{1,0:T(8,128)(2,1)S(1)}, u32[]{:S(2)}, u32[]{:S(2)}) collective-permute-start(bf16[256,256]{1,0:T(8,128)(2,1)S(1)} %get-tuple-element.40), channel_id=1, source_target_pairs={{0,64},{1,65},{2,66},{3,67},{4,68},{5,69},{6,70},{7,71},{8,72},{9,... | collective-permute-start | bytes 393224 | tf_op jit(solution)/shard_map/ppermute | solution.py:64
  74.4 1.8 %collective-permute-start.17 = (bf16[256,256]{1,0:T(8,128)(2,1)S(1)}, bf16[256,256]{1,0:T(8,128)(2,1)S(1)}, u32[]{:S(2)}, u32[]{:S(2)}) collective-permute-start(bf16[256,256]{1,0:T(8,128)(2,1)S(1)} %get-tuple-element.42), channel_id=1, source_target_pairs={{0,32},{1,33},{2,34},{3,35},{4,36},{5,37},{6,38},{7,39},{8,40},{9,... | collective-permute-start | bytes 393224 | tf_op jit(solution)/shard_map/ppermute | solution.py:64
  77.7 2.2 %collective-permute-start.10 = (f32[96,256]{1,0:T(8,128)S(1)}, f32[96,256]{1,0:T(8,128)S(1)}, u32[]{:S(2)}, u32[]{:S(2)}) collective-permute-start(f32[96,256]{1,0:T(8,128)S(1)} %add.129), channel_id=1, source_target_pairs={{0,3},{1,2},{2,1},{3,0},{4,7},{5,6},{6,5},{7,4},{8,11},{9,10},{10,... | collective-permute-start | bytes 294920 | tf_op jit(solution)/shard_map/ppermute | solution.py:64
  79.9 3.7 %collective-permute-done.10 = f32[96,256]{1,0:T(8,128)S(1)} collective-permute-done((f32[96,256]{1,0:T(8,128)S(1)}, f32[96,256]{1,0:T(8,128)S(1)}, u32[]{:S(2)}, u32[]{:S(2)}) %collective-permute-start.10) | collective-permute-done | bytes 98336 | tf_op jit(solution)/shard_map/ppermute | solution.py:64
  84.8 1.9 %collective-permute-start.19 = (f32[64,256]{1,0:T(8,128)S(1)}, f32[64,256]{1,0:T(8,128)S(1)}, u32[]{:S(2)}, u32[]{:S(2)}) collective-permute-start(f32[64,256]{1,0:T(8,128)S(1)} %get-tuple-element.43), channel_id=1, source_target_pairs={{0,16},{1,17},{2,18},{3,19},{4,20},{5,21},{6,22},{7,23},{8,24},{9,... | collective-permute-start | bytes 196616 | tf_op jit(solution)/shard_map/ppermute | solution.py:64
  86.7 2.2 %collective-permute-start.20 = (f32[64,256]{1,0:T(8,128)S(1)}, f32[64,256]{1,0:T(8,128)S(1)}, u32[]{:S(2)}, u32[]{:S(2)}) collective-permute-start(f32[64,256]{1,0:T(8,128)S(1)} %get-tuple-element.45), channel_id=1, source_target_pairs={{0,8},{1,9},{2,10},{3,11},{4,12},{5,13},{6,14},{7,15},{8,16},{9,17... | collective-permute-start | bytes 196616 | tf_op jit(solution)/shard_map/ppermute | solution.py:64
  90.0 10.8 %shard_map.71 = (f32[256,256]{1,0:T(8,128)S(1)}, bf16[256,256]{1,0:T(8,128)(2,1)S(1)}, bf16[256,256]{1,0:T(8,128)(2,1)S(1)}) custom-call(s32[4]{0:T(128)S(1)} %pad_add_fusion.place, f32[96,256]{1,0:T(8,128)S(1)} %add.130.mine_ref, f32[96,256]{1,0:T(8,128)S(1)} %collective-permute-done.11.other_ref), custom_call_target="tpu_custom_call" | custom-call | flops 8589934592 | bytes 65536 | tf_op jit(solution)/shard_map/pallas_call | solution.py:80
  101.3 3.2 %collective-permute-start.23 = (f32[16,256]{1,0:T(8,128)S(1)}, f32[16,256]{1,0:T(8,128)S(1)}, u32[]{:S(2)}, u32[]{:S(2)}) collective-permute-start(f32[16,256]{1,0:T(8,128)S(1)} %get-tuple-element.47), channel_id=1, source_target_pairs={{0,2},{1,3},{2,0},{3,1},{4,6},{5,7},{6,4},{7,5},{8,10},{9,11},{10,... | collective-permute-start | bytes 49160 | tf_op jit(solution)/shard_map/ppermute | solution.py:64
  105.9 3.3 %shard_map.72 = f32[4096,256]{1,0:T(8,128)} custom-call(bf16[4096,256]{1,0:T(8,128)(2,1)S(1)} %get-tuple-element.26.high_ref, bf16[4096,256]{1,0:T(8,128)(2,1)S(1)} %copy-done.2, bf16[256,256]{1,0:T(8,128)(2,1)S(1)} %get-tuple-element.30.inv_high, bf16[256,256]{1,0:T(8,128)(2,1)S(1)} %get-tuple-element.31.inv_low), custom_call_target="tpu_custom_call" | custom-call | flops 1610612736 | bytes 65536 | tf_op jit(solution)/shard_map/pallas_call | solution.py:80
  (62 shorter events, 20.6 us)
Async XLA Ops:
  3.3 18.2 %collective-permute-start = (f32[128,256]{1,0:T(8,128)S(1)}, f32[128,256]{1,0:T(8,128)S(1)}, u32[]{:S(2)}, u32[]{:S(2)}) collective-permute-start(f32[128,256]{1,0:T(8,128)S(1)} %get-tuple-element.24), channel_id=1, source_target_pairs={{0,1},{1,2},{2,3},{3,0},{4,5},{5,6},{6,7},{7,4},{8,9},{9,10},{10,1... | collective-permute-start | bytes 393224 | tf_op jit(solution)/shard_map/ppermute | solution.py:64
  5.1 16.4 %collective-permute-start.1 = (f32[128,256]{1,0:T(8,128)S(1)}, f32[128,256]{1,0:T(8,128)S(1)}, u32[]{:S(2)}, u32[]{:S(2)}) collective-permute-start(f32[128,256]{1,0:T(8,128)S(1)} %get-tuple-element.24), channel_id=1, source_target_pairs={{0,2},{1,3},{2,0},{3,1},{4,6},{5,7},{6,4},{7,5},{8,10},{9,11},{10,... | collective-permute-start | bytes 393224 | tf_op jit(solution)/shard_map/ppermute | solution.py:64
  8.0 13.5 %collective-permute-start.2 = (f32[128,256]{1,0:T(8,128)S(1)}, f32[128,256]{1,0:T(8,128)S(1)}, u32[]{:S(2)}, u32[]{:S(2)}) collective-permute-start(f32[128,256]{1,0:T(8,128)S(1)} %get-tuple-element.24), channel_id=1, source_target_pairs={{0,3},{1,0},{2,1},{3,2},{4,7},{5,4},{6,5},{7,6},{8,11},{9,8},{10,9... | collective-permute-start | bytes 393224 | tf_op jit(solution)/shard_map/ppermute | solution.py:64
  32.5 9.6 %collective-permute-start.12 = (bf16[256,256]{1,0:T(8,128)(2,1)S(1)}, bf16[256,256]{1,0:T(8,128)(2,1)S(1)}, u32[]{:S(2)}, u32[]{:S(2)}) collective-permute-start(bf16[256,256]{1,0:T(8,128)(2,1)S(1)} %get-tuple-element.34), channel_id=1, source_target_pairs={{0,1},{1,2},{2,3},{3,0},{4,5},{5,6},{6,7},{7,4},{8,9},{9,10},{10,1... | collective-permute-start | bytes 393224 | tf_op jit(solution)/shard_map/ppermute | solution.py:64
  33.2 8.9 %collective-permute-start.13 = (bf16[256,256]{1,0:T(8,128)(2,1)S(1)}, bf16[256,256]{1,0:T(8,128)(2,1)S(1)}, u32[]{:S(2)}, u32[]{:S(2)}) collective-permute-start(bf16[256,256]{1,0:T(8,128)(2,1)S(1)} %get-tuple-element.35), channel_id=1, source_target_pairs={{0,2},{1,3},{2,0},{3,1},{4,6},{5,7},{6,4},{7,5},{8,10},{9,11},{10,... | collective-permute-start | bytes 393224 | tf_op jit(solution)/shard_map/ppermute | solution.py:64
  34.0 8.7 %collective-permute-start.14 = (bf16[256,256]{1,0:T(8,128)(2,1)S(1)}, bf16[256,256]{1,0:T(8,128)(2,1)S(1)}, u32[]{:S(2)}, u32[]{:S(2)}) collective-permute-start(bf16[256,256]{1,0:T(8,128)(2,1)S(1)} %get-tuple-element.36), channel_id=1, source_target_pairs={{0,3},{1,0},{2,1},{3,2},{4,7},{5,4},{6,5},{7,6},{8,11},{9,8},{10,9... | collective-permute-start | bytes 393224 | tf_op jit(solution)/shard_map/ppermute | solution.py:64
  45.1 25.3 %collective-permute-start.15 = (bf16[1024,256]{1,0:T(8,128)(2,1)}, bf16[1024,256]{1,0:T(8,128)(2,1)}, u32[]{:S(2)}, u32[]{:S(2)}) collective-permute-start(bf16[1024,256]{1,0:T(8,128)(2,1)} %get-tuple-element.38), channel_id=1, source_target_pairs={{0,4},{1,5},{2,6},{3,7},{4,0},{5,1},{6,2},{7,3},{8,12},{9,13},{10,... | collective-permute-start | bytes 1572872 | tf_op jit(solution)/shard_map/ppermute | solution.py:64
  45.1 2.3 %collective-permute-start.4 = (f32[96,256]{1,0:T(8,128)S(1)}, f32[96,256]{1,0:T(8,128)S(1)}, u32[]{:S(2)}, u32[]{:S(2)}) collective-permute-start(f32[96,256]{1,0:T(8,128)S(1)} %get-tuple-element.29), channel_id=1, source_target_pairs={{0,4},{1,5},{2,6},{3,7},{4,0},{5,1},{6,2},{7,3},{8,12},{9,13},{10,... | collective-permute-start | bytes 294920 | tf_op jit(solution)/shard_map/ppermute | solution.py:64
  47.3 4.9 %collective-permute-start.5 = (f32[96,256]{1,0:T(8,128)S(1)}, f32[96,256]{1,0:T(8,128)S(1)}, u32[]{:S(2)}, u32[]{:S(2)}) collective-permute-start(f32[96,256]{1,0:T(8,128)S(1)} %add.124), channel_id=1, source_target_pairs={{0,32},{1,33},{2,34},{3,35},{4,36},{5,37},{6,38},{7,39},{8,40},{9,... | collective-permute-start | bytes 294920 | tf_op jit(solution)/shard_map/ppermute | solution.py:64
  52.3 5.9 %collective-permute-start.6 = (f32[96,256]{1,0:T(8,128)S(1)}, f32[96,256]{1,0:T(8,128)S(1)}, u32[]{:S(2)}, u32[]{:S(2)}) collective-permute-start(f32[96,256]{1,0:T(8,128)S(1)} %add.125), channel_id=1, source_target_pairs={{0,96},{1,97},{2,98},{3,99},{4,100},{5,101},{6,102},{7,103},{8,104... | collective-permute-start | bytes 294920 | tf_op jit(solution)/shard_map/ppermute | solution.py:64
  58.2 4.7 %collective-permute-start.7 = (f32[96,256]{1,0:T(8,128)S(1)}, f32[96,256]{1,0:T(8,128)S(1)}, u32[]{:S(2)}, u32[]{:S(2)}) collective-permute-start(f32[96,256]{1,0:T(8,128)S(1)} %add.126), channel_id=1, source_target_pairs={{0,8},{1,9},{2,10},{3,11},{4,12},{5,13},{6,14},{7,15},{8,0},{9,1},... | collective-permute-start | bytes 294920 | tf_op jit(solution)/shard_map/ppermute | solution.py:64
  62.9 6.9 %collective-permute-start.8 = (f32[96,256]{1,0:T(8,128)S(1)}, f32[96,256]{1,0:T(8,128)S(1)}, u32[]{:S(2)}, u32[]{:S(2)}) collective-permute-start(f32[96,256]{1,0:T(8,128)S(1)} %add.127), channel_id=1, source_target_pairs={{0,24},{1,25},{2,26},{3,27},{4,28},{5,29},{6,30},{7,31},{8,16},{9,... | collective-permute-start | bytes 294920 | tf_op jit(solution)/shard_map/ppermute | solution.py:64
  69.8 7.8 %collective-permute-start.9 = (f32[96,256]{1,0:T(8,128)S(1)}, f32[96,256]{1,0:T(8,128)S(1)}, u32[]{:S(2)}, u32[]{:S(2)}) collective-permute-start(f32[96,256]{1,0:T(8,128)S(1)} %add.128), channel_id=1, source_target_pairs={{0,1},{1,0},{2,3},{3,2},{4,5},{5,4},{6,7},{7,6},{8,9},{9,8},{10,11... | collective-permute-start | bytes 294920 | tf_op jit(solution)/shard_map/ppermute | solution.py:64
  72.5 11.2 %collective-permute-start.16 = (bf16[256,256]{1,0:T(8,128)(2,1)S(1)}, bf16[256,256]{1,0:T(8,128)(2,1)S(1)}, u32[]{:S(2)}, u32[]{:S(2)}) collective-permute-start(bf16[256,256]{1,0:T(8,128)(2,1)S(1)} %get-tuple-element.40), channel_id=1, source_target_pairs={{0,64},{1,65},{2,66},{3,67},{4,68},{5,69},{6,70},{7,71},{8,72},{9,... | collective-permute-start | bytes 393224 | tf_op jit(solution)/shard_map/ppermute | solution.py:64
  74.4 9.3 %collective-permute-start.17 = (bf16[256,256]{1,0:T(8,128)(2,1)S(1)}, bf16[256,256]{1,0:T(8,128)(2,1)S(1)}, u32[]{:S(2)}, u32[]{:S(2)}) collective-permute-start(bf16[256,256]{1,0:T(8,128)(2,1)S(1)} %get-tuple-element.42), channel_id=1, source_target_pairs={{0,32},{1,33},{2,34},{3,35},{4,36},{5,37},{6,38},{7,39},{8,40},{9,... | collective-permute-start | bytes 393224 | tf_op jit(solution)/shard_map/ppermute | solution.py:64
  76.2 7.5 %collective-permute-start.18 = (bf16[256,256]{1,0:T(8,128)(2,1)S(1)}, bf16[256,256]{1,0:T(8,128)(2,1)S(1)}, u32[]{:S(2)}, u32[]{:S(2)}) collective-permute-start(bf16[256,256]{1,0:T(8,128)(2,1)S(1)} %get-tuple-element.41), channel_id=1, source_target_pairs={{0,96},{1,97},{2,98},{3,99},{4,100},{5,101},{6,102},{7,103},{8,104... | collective-permute-start | bytes 393224 | tf_op jit(solution)/shard_map/ppermute | solution.py:64
  77.7 5.9 %collective-permute-start.10 = (f32[96,256]{1,0:T(8,128)S(1)}, f32[96,256]{1,0:T(8,128)S(1)}, u32[]{:S(2)}, u32[]{:S(2)}) collective-permute-start(f32[96,256]{1,0:T(8,128)S(1)} %add.129), channel_id=1, source_target_pairs={{0,3},{1,2},{2,1},{3,0},{4,7},{5,6},{6,5},{7,4},{8,11},{9,10},{10,... | collective-permute-start | bytes 294920 | tf_op jit(solution)/shard_map/ppermute | solution.py:64
  83.6 6.4 %collective-permute-start.11 = (f32[96,256]{1,0:T(8,128)S(1)}, f32[96,256]{1,0:T(8,128)S(1)}, u32[]{:S(2)}, u32[]{:S(2)}) collective-permute-start(f32[96,256]{1,0:T(8,128)S(1)} %add.130.mine_ref), channel_id=1, source_target_pairs={{0,4},{1,5},{2,6},{3,7},{4,0},{5,1},{6,2},{7,3},{8,12},{9,13},{10,... | collective-permute-start | bytes 294920 | tf_op jit(solution)/shard_map/ppermute | solution.py:64
  84.8 16.0 %collective-permute-start.19 = (f32[64,256]{1,0:T(8,128)S(1)}, f32[64,256]{1,0:T(8,128)S(1)}, u32[]{:S(2)}, u32[]{:S(2)}) collective-permute-start(f32[64,256]{1,0:T(8,128)S(1)} %get-tuple-element.43), channel_id=1, source_target_pairs={{0,16},{1,17},{2,18},{3,19},{4,20},{5,21},{6,22},{7,23},{8,24},{9,... | collective-permute-start | bytes 196616 | tf_op jit(solution)/shard_map/ppermute | solution.py:64
  86.7 14.0 %collective-permute-start.20 = (f32[64,256]{1,0:T(8,128)S(1)}, f32[64,256]{1,0:T(8,128)S(1)}, u32[]{:S(2)}, u32[]{:S(2)}) collective-permute-start(f32[64,256]{1,0:T(8,128)S(1)} %get-tuple-element.45), channel_id=1, source_target_pairs={{0,8},{1,9},{2,10},{3,11},{4,12},{5,13},{6,14},{7,15},{8,16},{9,17... | collective-permute-start | bytes 196616 | tf_op jit(solution)/shard_map/ppermute | solution.py:64
  89.0 11.8 %collective-permute-start.21 = (f32[64,256]{1,0:T(8,128)S(1)}, f32[64,256]{1,0:T(8,128)S(1)}, u32[]{:S(2)}, u32[]{:S(2)}) collective-permute-start(f32[64,256]{1,0:T(8,128)S(1)} %get-tuple-element.44), channel_id=1, source_target_pairs={{0,24},{1,25},{2,26},{3,27},{4,28},{5,29},{6,30},{7,31},{8,0},{9,1... | collective-permute-start | bytes 196616 | tf_op jit(solution)/shard_map/ppermute | solution.py:64
  100.9 8.3 %collective-permute-start.22 = (f32[16,256]{1,0:T(8,128)S(1)}, f32[16,256]{1,0:T(8,128)S(1)}, u32[]{:S(2)}, u32[]{:S(2)}) collective-permute-start(f32[16,256]{1,0:T(8,128)S(1)} %get-tuple-element.48), channel_id=1, source_target_pairs={{0,1},{1,2},{2,3},{3,0},{4,5},{5,6},{6,7},{7,4},{8,9},{9,10},{10,1... | collective-permute-start | bytes 49160 | tf_op jit(solution)/shard_map/ppermute | solution.py:64
  101.3 7.9 %collective-permute-start.23 = (f32[16,256]{1,0:T(8,128)S(1)}, f32[16,256]{1,0:T(8,128)S(1)}, u32[]{:S(2)}, u32[]{:S(2)}) collective-permute-start(f32[16,256]{1,0:T(8,128)S(1)} %get-tuple-element.47), channel_id=1, source_target_pairs={{0,2},{1,3},{2,0},{3,1},{4,6},{5,7},{6,4},{7,5},{8,10},{9,11},{10,... | collective-permute-start | bytes 49160 | tf_op jit(solution)/shard_map/ppermute | solution.py:64
  104.5 4.7 %collective-permute-start.24 = (f32[16,256]{1,0:T(8,128)S(1)}, f32[16,256]{1,0:T(8,128)S(1)}, u32[]{:S(2)}, u32[]{:S(2)}) collective-permute-start(f32[16,256]{1,0:T(8,128)S(1)} %get-tuple-element.46), channel_id=1, source_target_pairs={{0,3},{1,0},{2,1},{3,2},{4,7},{5,4},{6,5},{7,6},{8,11},{9,8},{10,9... | collective-permute-start | bytes 49160 | tf_op jit(solution)/shard_map/ppermute | solution.py:64
  (7 other events, 64.5 us)

commit v5 on v4

--- a/solution.py
+++ b/solution.py
@@ -14,7 +14,6 @@
 MODES = 256
 STARS = 524288
 AXES = ("rows", "units")
-DEPTH = 2
 F32 = jnp.float32
 BF16 = jnp.bfloat16
 HIGHEST = lax.Precision.HIGHEST
@@ -102,29 +101,38 @@
     half_ref[...] = full_ref[pl.ds(pl.multiple_of(place[2] * half, half), half), :]
 
 
-def sketch_kernel(tiles, sketch_ref, res_hbm, out_ref, res_ref, flag_ref, sems):
-    tile = res_ref.shape[0] // tiles
+def fetch_kernel(sketch_ref, res_hbm, out_ref, res_ref, sems):
+    half = out_ref.shape[0]
     copies = []
-    for i in range(tiles):
+    for i in range(2):
+        rows = pl.ds(i * half, half)
+        copies.append(pltpu.make_async_copy(res_hbm.at[rows, :], res_ref.at[rows, :], sems.at[i]))
+        copies[i].start()
+    copies[0].wait()
+    sketch_kernel(sketch_ref, res_ref, out_ref, 0)
+    copies[1].wait()
+
+
+def sketch_kernel(sketch_ref, res_ref, out_ref, first):
+    tile = out_ref.shape[0] // 2
+    for i in range(2):
         rows = pl.ds(i * tile, tile)
-        copies.append(pltpu.make_async_copy(res_hbm.at[rows, :], res_ref.at[rows, :], sems.at[i]))
-    for i in range(DEPTH):
-        copies[i].start()
-    for i in range(tiles):
-        copies[i].wait()
-        if i + DEPTH < tiles:
-            copies[i + DEPTH].start()
-        rows = pl.ds(i * tile, tile)
-        out_ref[rows, :] = jnp.dot(res_ref[rows, :], sketch_ref[...], preferred_element_type=F32)
-    flag_ref[...] = jnp.zeros_like(flag_ref)
-
-
-def correct_kernel(blocks, place, uses, part_ref, load_ref, own_ref, half_ref, other_ref,
+        out_ref[rows, :] = jnp.dot(
+            res_ref[pl.ds(first + i * tile, tile), :], sketch_ref[...], preferred_element_type=F32
+        )
+
+
+def sketch_rest_kernel(sketch_ref, res_ref, out_ref):
+    sketch_kernel(sketch_ref, res_ref, out_ref, res_ref.shape[0] // 2)
+
+
+def correct_kernel(place, uses, part_a, part_b, load_ref, own_ref, half_ref, other_ref,
                    high_ref, low_ref, gram_keep, gram_send, w_keep, w_send1, w_send2, w_send3,
                    table_high, table_low, gram_hh, gram_hl, weights):
     units = own_ref.shape[0]
     half = units // 2
-    tile = blocks * BLOCK_STARS
+    tile = part_a.shape[0]
+    blocks = tile // BLOCK_STARS
     y, c = place[3], place[2]
     gram_hh[...] = jnp.zeros_like(gram_hh)
     gram_hl[...] = jnp.zeros_like(gram_hl)
@@ -142,9 +150,9 @@
         put(base + c * half, half_ref[k * half:(k + 1) * half, :])
         put(base + (1 - c) * half, other_ref[k * half:(k + 1) * half, :])
 
-    def step(i, carry):
+    for i, part_ref in enumerate((part_a, part_b)):
         for block in range(blocks):
-            rows = pl.ds(pl.multiple_of(i * tile + block * BLOCK_STARS, BLOCK_STARS), BLOCK_STARS)
+            rows = pl.ds(i * tile + block * BLOCK_STARS, BLOCK_STARS)
             groups = [uses[use, i * blocks + block] for use in range(USES)]
             starts = [pl.multiple_of(g * GROUP, GROUP) for g in groups]
             load = load_ref[rows, :]
@@ -152,18 +160,15 @@
             low_table = jnp.concatenate([table_low[pl.ds(s, GROUP), :] for s in starts], axis=0)
             offset = jnp.dot(load, high_table, preferred_element_type=F32)
             offset = offset + jnp.dot(load, low_table, preferred_element_type=F32)
-            high, low = split_low(part_ref[rows, :] - offset)
+            high, low = split_low(part_ref[pl.ds(block * BLOCK_STARS, BLOCK_STARS), :] - offset)
             high_ref[rows, :] = high
             low_ref[rows, :] = low
             product = dot_rows(load, high)
             for use in range(USES):
                 weights[pl.ds(starts[use], GROUP), :] += product[use * GROUP:(use + 1) * GROUP, :]
-        rows = pl.ds(pl.multiple_of(i * tile, tile), tile)
+        rows = pl.ds(i * tile, tile)
         gram_hh[...] += dot_rows(high_ref[rows, :], high_ref[rows, :])
         gram_hl[...] += dot_rows(high_ref[rows, :], low_ref[rows, :])
-        return carry
-
-    lax.fori_loop(0, part_ref.shape[0] // tile, step, 0)
     cross = gram_hl[...]
     gram = gram_hh[...] + cross + cross.T
     packed = jnp.concatenate([gram[:128, :128], gram[128:, :128], gram[128:, 128:]], axis=0)
@@ -341,16 +346,20 @@
         flops=2 * units * bins * MODES, far=[zero_points, sketch_matrix],
     )
     shifted = shift_all("y", [half] * 3)
-    part, residuals, flag = resident(
-        functools.partial(sketch_kernel, 8), [], [sketch_near],
-        [on_chip((rows, MODES)), on_chip((rows, bins), BF16), on_chip((8, 128))],
-        [pltpu.SemaphoreType.DMA((8,))], flops=2 * rows * bins * MODES, far=[residuals],
-    )
-    halves = jnp.concatenate(shifted, axis=0) + flag[0, 0]
+    part_a, near = resident(
+        fetch_kernel, [], [sketch_near],
+        [on_chip((rows // 2, MODES)), on_chip((rows, bins), BF16)],
+        [pltpu.SemaphoreType.DMA((2,))], flops=rows * bins * MODES, far=[residuals],
+    )
+    halves = jnp.concatenate(shifted, axis=0)
     others = send(halves, SWAP)
+    part_b, = resident(
+        sketch_rest_kernel, [], [sketch_near, near],
+        [on_chip((rows // 2, MODES))], flops=rows * bins * MODES,
+    )
     high, low, gram_keep, gram_send, w_keep, *w_sends = resident(
-        functools.partial(correct_kernel, 4), [place, use_lists.T],
-        [part, loadings, own, halves, others],
+        correct_kernel, [place, use_lists.T],
+        [part_a, part_b, loadings, own, halves, others],
         [on_chip((rows, MODES), BF16)] * 2 + [on_chip((96, MODES))] * 2 + [on_chip((units, MODES))]
         + [on_chip((units, MODES), BF16)] * 3,
         [
@@ -365,7 +374,7 @@
     w_got = shift_all("y", w_sends)
     gram = gram_keep + send(gram_send, SWAP)
     raw, = resident(
-        functools.partial(raw_kernel, 512), [], [residuals, high],
+        functools.partial(raw_kernel, 512), [], [near, high],
         [on_chip((MODES, bins))], flops=2 * rows * bins * MODES,
     )
     for axis in "xzy":
@@ -379,6 +388,7 @@
     )
     arrived = send(sent, SWAP)
     keep, sends = quarters(x, keep + arrived.astype(F32), BF16)
+    keep, *sends = lax.optimization_barrier((keep, *sends))
     keep, sends = quarters(z, add_four(keep, [g.astype(F32) for g in shift_all("x", sends)]), F32)
     keep, sends = quarters(y, add_four(keep, shift_all("z", sends)), F32)
     raw_got = shift_all("y", sends)

time: 110 us -> 104 us (0.945)
  Pallas kernels: 45.1 us -> 38.1 us
  waiting for transfers between devices: 20.5 us -> 22.7 us
  other arithmetic: 3.07 us -> 1.39 us
  local copies, waits for them, and re-layouts: 1.58 us -> 0.18 us
    pallas_call x8 -> x9, Pallas kernels: 45.1 us -> 38.1 us  [resident(): pl.pallas_call(kernel, in_specs=[smem] * len(scalars) + [vmem] * len(arra...]
    ppermute x25, waiting for transfers between devices: 20.5 us -> 22.7 us  [send(): return lax.ppermute(value, AXES, pairs)]
  transfers between devices with their start and end apart: 25 -> 25, of which waited for: 9 -> 9; matrix products, arithmetic and copies ran while one was open for 3% -> 1% of each run, Pallas kernels for 28% -> 26%
where the time goes in v5:
time: 104 us; the launch traced here: 103 us
  starting transfers between devices  39.9 us (38%)
  Pallas kernels  38.1 us (37%)
  waiting for transfers between devices  22.7 us (22%)
  other arithmetic  1.39 us (1%)
    ppermute x25, starting transfers between devices, send(): return lax.ppermute(value, AXES, pairs)  39.9 us
    pallas_call x9, Pallas kernels, resident(): pl.pallas_call(kernel, in_specs=[smem] * len(scalars) + [vmem] * len(arra...  38.1 us
    ppermute x25, waiting for transfers between devices, send(): return lax.ppermute(value, AXES, pairs)  22.7 us
  transfers between devices with their start and end apart: 25, of which 9 were waited for; matrix products, arithmetic and copies ran while one was open for 1% of the time, Pallas kernels for 26%

profile of v5, /device:TPU:0, one launch (start us, length us, event | category | flops | bytes accessed | tf_op | source)
XLA Modules:
  0.0 103.3 jit_solution(2508087123939167530)
XLA Ops:
  0.8 2.5 %shard_map.68 = (f32[256,256]{1,0:T(8,128)S(1)}, f32[128,256]{1,0:T(8,128)S(1)}, bf16[2048,256]{1,0:T(8,128)(2,1)S(1)}) custom-call(s32[4]{0:T(128)S(1)} %pad_add_fusion.place, bf16[256,2048]{1,0:T(8,128)(2,1)} %zero_ref.1, bf16[2048,256]{1,0:T(8,128)(2,1)} %sketch_hbm.1), custom_call_target="tpu_custom_call" | custom-call | flops 268435456 | bytes 65536 | tf_op jit(solution)/shard_map/pallas_call | solution.py:79
  5.1 2.9 %collective-permute-start.1 = (f32[128,256]{1,0:T(8,128)S(1)}, f32[128,256]{1,0:T(8,128)S(1)}, u32[]{:S(2)}, u32[]{:S(2)}) collective-permute-start(f32[128,256]{1,0:T(8,128)S(1)} %get-tuple-element.28), channel_id=1, source_target_pairs={{0,2},{1,3},{2,0},{3,1},{4,6},{5,7},{6,4},{7,5},{8,10},{9,11},{10,... | collective-permute-start | bytes 393224 | tf_op jit(solution)/shard_map/ppermute | solution.py:63
  10.0 4.0 %collective-permute-done.1 = f32[128,256]{1,0:T(8,128)S(1)} collective-permute-done((f32[128,256]{1,0:T(8,128)S(1)}, f32[128,256]{1,0:T(8,128)S(1)}, u32[]{:S(2)}, u32[]{:S(2)}) %collective-permute-start.1) | collective-permute-done | bytes 131104 | tf_op jit(solution)/shard_map/ppermute | solution.py:63
  14.1 5.8 %shard_map.69 = (f32[2048,256]{1,0:T(8,128)S(1)}, bf16[4096,2048]{1,0:T(8,128)(2,1)S(1)}) custom-call(bf16[2048,256]{1,0:T(8,128)(2,1)S(1)} %get-tuple-element.24.sketch_ref, bf16[4096,2048]{1,0:T(8,128)(2,1)} %res_hbm.1), custom_call_target="tpu_custom_call" | custom-call | flops 2147483648 | bytes 65536 | tf_op jit(solution)/shard_map/pallas_call | solution.py:79
  19.9 2.3 %shard_map.70.part_b = f32[2048,256]{1,0:T(8,128)S(1)} custom-call(bf16[2048,256]{1,0:T(8,128)(2,1)S(1)} %get-tuple-element.24.sketch_ref, bf16[4096,2048]{1,0:T(8,128)(2,1)S(1)} %get-tuple-element.26.res_ref), custom_call_target="tpu_custom_call" | custom-call | flops 2147483648 | bytes 65536 | tf_op jit(solution)/shard_map/pallas_call | solution.py:79
  22.3 5.0 %shard_map.71 = (bf16[4096,256]{1,0:T(8,128)(2,1)S(1)}, bf16[4096,256]{1,0:T(8,128)(2,1)S(1)}, f32[96,256]{1,0:T(8,128)S(1)}, f32[96,256]{1,0:T(8,128)S(1)}, f32...) custom-call(s32[4]{0:T(128)S(1)} %pad_add_fusion.place, ...), custom_call_target="tpu_custom_call" | custom-call | flops 4294967296 | bytes 65536 | tf_op jit(solution)/shard_map/pallas_call | solution.py:79
  28.6 2.4 %collective-permute-start.13 = (bf16[256,256]{1,0:T(8,128)(2,1)S(1)}, bf16[256,256]{1,0:T(8,128)(2,1)S(1)}, u32[]{:S(2)}, u32[]{:S(2)}) collective-permute-start(bf16[256,256]{1,0:T(8,128)(2,1)S(1)} %get-tuple-element.37), channel_id=1, source_target_pairs={{0,2},{1,3},{2,0},{3,1},{4,6},{5,7},{6,4},{7,5},{8,10},{9,11},{10,... | collective-permute-start | bytes 393224 | tf_op jit(solution)/shard_map/ppermute | solution.py:63
  32.6 5.2 %shard_map.74.raw_ref = f32[256,2048]{1,0:T(8,128)S(1)} custom-call(bf16[4096,2048]{1,0:T(8,128)(2,1)S(1)} %get-tuple-element.26.res_ref, bf16[4096,256]{1,0:T(8,128)(2,1)S(1)} %get-tuple-element.29.high_ref), custom_call_target="tpu_custom_call" | custom-call | flops 4294967296 | bytes 65536 | tf_op jit(solution)/shard_map/pallas_call | solution.py:79
  37.9 2.3 %shard_map.75 = (f32[1024,256]{1,0:T(8,128)S(1)}, bf16[1024,256]{1,0:T(8,128)(2,1)}) custom-call(s32[4]{0:T(128)S(1)} %pad_add_fusion.place, f32[256,2048]{1,0:T(8,128)S(1)} %shard_map.74.raw_ref, bf16[256,2048]{1,0:T(8,128)(2,1)S(1)} %copy-done, f32[256,256]{1,0:T(8,128)S(1)} %get-tuple-element.35.w_keep, bf16[256,256]{1,0:T(8,128)(2,1)S(1)} %collective-permute-done.12.w1, ...), custom_call_target="tpu_custom_call" | custom-call | flops 268435456 | bytes 65536 | tf_op jit(solution)/shard_map/pallas_call | solution.py:79
  44.1 3.3 %collective-permute-done.5 = f32[96,256]{1,0:T(8,128)S(1)} collective-permute-done((f32[96,256]{1,0:T(8,128)S(1)}, f32[96,256]{1,0:T(8,128)S(1)}, u32[]{:S(2)}, u32[]{:S(2)}) %collective-permute-start.5) | collective-permute-done | bytes 98336 | tf_op jit(solution)/shard_map/ppermute | solution.py:63
  47.4 2.8 %collective-permute-start.6 = (f32[96,256]{1,0:T(8,128)S(1)}, f32[96,256]{1,0:T(8,128)S(1)}, u32[]{:S(2)}, u32[]{:S(2)}) collective-permute-start(f32[96,256]{1,0:T(8,128)S(1)} %add.117), channel_id=1, source_target_pairs={{0,96},{1,97},{2,98},{3,99},{4,100},{5,101},{6,102},{7,103},{8,104... | collective-permute-start | bytes 294920 | tf_op jit(solution)/shard_map/ppermute | solution.py:63
  50.3 3.1 %collective-permute-done.6 = f32[96,256]{1,0:T(8,128)S(1)} collective-permute-done((f32[96,256]{1,0:T(8,128)S(1)}, f32[96,256]{1,0:T(8,128)S(1)}, u32[]{:S(2)}, u32[]{:S(2)}) %collective-permute-start.6) | collective-permute-done | bytes 98336 | tf_op jit(solution)/shard_map/ppermute | solution.py:63
  53.4 2.0 %collective-permute-start.7 = (f32[96,256]{1,0:T(8,128)S(1)}, f32[96,256]{1,0:T(8,128)S(1)}, u32[]{:S(2)}, u32[]{:S(2)}) collective-permute-start(f32[96,256]{1,0:T(8,128)S(1)} %add.118), channel_id=1, source_target_pairs={{0,8},{1,9},{2,10},{3,11},{4,12},{5,13},{6,14},{7,15},{8,0},{9,1},... | collective-permute-start | bytes 294920 | tf_op jit(solution)/shard_map/ppermute | solution.py:63
  55.3 2.7 %collective-permute-done.7 = f32[96,256]{1,0:T(8,128)S(1)} collective-permute-done((f32[96,256]{1,0:T(8,128)S(1)}, f32[96,256]{1,0:T(8,128)S(1)}, u32[]{:S(2)}, u32[]{:S(2)}) %collective-permute-start.7) | collective-permute-done | bytes 98336 | tf_op jit(solution)/shard_map/ppermute | solution.py:63
  58.1 4.1 %collective-permute-start.8 = (f32[96,256]{1,0:T(8,128)S(1)}, f32[96,256]{1,0:T(8,128)S(1)}, u32[]{:S(2)}, u32[]{:S(2)}) collective-permute-start(f32[96,256]{1,0:T(8,128)S(1)} %add.119), channel_id=1, source_target_pairs={{0,24},{1,25},{2,26},{3,27},{4,28},{5,29},{6,30},{7,31},{8,16},{9,... | collective-permute-start | bytes 294920 | tf_op jit(solution)/shard_map/ppermute | solution.py:63
  62.2 2.6 %collective-permute-done.8 = f32[96,256]{1,0:T(8,128)S(1)} collective-permute-done((f32[96,256]{1,0:T(8,128)S(1)}, f32[96,256]{1,0:T(8,128)S(1)}, u32[]{:S(2)}, u32[]{:S(2)}) %collective-permute-start.8) | collective-permute-done | bytes 98336 | tf_op jit(solution)/shard_map/ppermute | solution.py:63
  64.8 1.8 %collective-permute-start.9 = (f32[96,256]{1,0:T(8,128)S(1)}, f32[96,256]{1,0:T(8,128)S(1)}, u32[]{:S(2)}, u32[]{:S(2)}) collective-permute-start(f32[96,256]{1,0:T(8,128)S(1)} %add.120), channel_id=1, source_target_pairs={{0,1},{1,0},{2,3},{3,2},{4,5},{5,4},{6,7},{7,6},{8,9},{9,8},{10,11... | collective-permute-start | bytes 294920 | tf_op jit(solution)/shard_map/ppermute | solution.py:63
  67.9 1.9 %collective-permute-start.16 = (bf16[256,256]{1,0:T(8,128)(2,1)S(1)}, bf16[256,256]{1,0:T(8,128)(2,1)S(1)}, u32[]{:S(2)}, u32[]{:S(2)}) collective-permute-start(bf16[256,256]{1,0:T(8,128)(2,1)S(1)} %get-tuple-element.42), channel_id=1, source_target_pairs={{0,64},{1,65},{2,66},{3,67},{4,68},{5,69},{6,70},{7,71},{8,72},{9,... | collective-permute-start | bytes 393224 | tf_op jit(solution)/shard_map/ppermute | solution.py:63
  74.5 4.4 %collective-permute-done.10 = f32[96,256]{1,0:T(8,128)S(1)} collective-permute-done((f32[96,256]{1,0:T(8,128)S(1)}, f32[96,256]{1,0:T(8,128)S(1)}, u32[]{:S(2)}, u32[]{:S(2)}) %collective-permute-start.10) | collective-permute-done | bytes 98336 | tf_op jit(solution)/shard_map/ppermute | solution.py:63
  79.2 1.9 %collective-permute-start.19 = (f32[64,256]{1,0:T(8,128)S(1)}, f32[64,256]{1,0:T(8,128)S(1)}, u32[]{:S(2)}, u32[]{:S(2)}) collective-permute-start(f32[64,256]{1,0:T(8,128)S(1)} %get-tuple-element.49), channel_id=1, source_target_pairs={{0,16},{1,17},{2,18},{3,19},{4,20},{5,21},{6,22},{7,23},{8,24},{9,... | collective-permute-start | bytes 196616 | tf_op jit(solution)/shard_map/ppermute | solution.py:63
  81.1 2.2 %collective-permute-start.20 = (f32[64,256]{1,0:T(8,128)S(1)}, f32[64,256]{1,0:T(8,128)S(1)}, u32[]{:S(2)}, u32[]{:S(2)}) collective-permute-start(f32[64,256]{1,0:T(8,128)S(1)} %get-tuple-element.51), channel_id=1, source_target_pairs={{0,8},{1,9},{2,10},{3,11},{4,12},{5,13},{6,14},{7,15},{8,16},{9,17... | collective-permute-start | bytes 196616 | tf_op jit(solution)/shard_map/ppermute | solution.py:63
  84.3 10.8 %shard_map.72 = (f32[256,256]{1,0:T(8,128)S(1)}, bf16[256,256]{1,0:T(8,128)(2,1)S(1)}, bf16[256,256]{1,0:T(8,128)(2,1)S(1)}) custom-call(s32[4]{0:T(128)S(1)} %pad_add_fusion.place, f32[96,256]{1,0:T(8,128)S(1)} %add.122.mine_ref, f32[96,256]{1,0:T(8,128)S(1)} %collective-permute-done.11.other_ref), custom_call_target="tpu_custom_call" | custom-call | flops 8589934592 | bytes 65536 | tf_op jit(solution)/shard_map/pallas_call | solution.py:79
  95.3 2.8 %collective-permute-start.23 = (f32[16,256]{1,0:T(8,128)S(1)}, f32[16,256]{1,0:T(8,128)S(1)}, u32[]{:S(2)}, u32[]{:S(2)}) collective-permute-start(f32[16,256]{1,0:T(8,128)S(1)} %get-tuple-element.53), channel_id=1, source_target_pairs={{0,2},{1,3},{2,0},{3,1},{4,6},{5,7},{6,4},{7,5},{8,10},{9,11},{10,... | collective-permute-start | bytes 49160 | tf_op jit(solution)/shard_map/ppermute | solution.py:63
  99.1 3.2 %shard_map.73 = f32[4096,256]{1,0:T(8,128)} custom-call(bf16[4096,256]{1,0:T(8,128)(2,1)S(1)} %get-tuple-element.29.high_ref, bf16[4096,256]{1,0:T(8,128)(2,1)S(1)} %copy-done.2, bf16[256,256]{1,0:T(8,128)(2,1)S(1)} %get-tuple-element.33.inv_high, bf16[256,256]{1,0:T(8,128)(2,1)S(1)} %get-tuple-element.34.inv_low), custom_call_target="tpu_custom_call" | custom-call | flops 1610612736 | bytes 65536 | tf_op jit(solution)/shard_map/pallas_call | solution.py:79
  (63 shorter events, 20.1 us)
Async XLA Ops:
  3.3 6.7 %collective-permute-start = (f32[128,256]{1,0:T(8,128)S(1)}, f32[128,256]{1,0:T(8,128)S(1)}, u32[]{:S(2)}, u32[]{:S(2)}) collective-permute-start(f32[128,256]{1,0:T(8,128)S(1)} %get-tuple-element.28), channel_id=1, source_target_pairs={{0,1},{1,2},{2,3},{3,0},{4,5},{5,6},{6,7},{7,4},{8,9},{9,10},{10,1... | collective-permute-start | bytes 393224 | tf_op jit(solution)/shard_map/ppermute | solution.py:63
  5.1 8.9 %collective-permute-start.1 = (f32[128,256]{1,0:T(8,128)S(1)}, f32[128,256]{1,0:T(8,128)S(1)}, u32[]{:S(2)}, u32[]{:S(2)}) collective-permute-start(f32[128,256]{1,0:T(8,128)S(1)} %get-tuple-element.28), channel_id=1, source_target_pairs={{0,2},{1,3},{2,0},{3,1},{4,6},{5,7},{6,4},{7,5},{8,10},{9,11},{10,... | collective-permute-start | bytes 393224 | tf_op jit(solution)/shard_map/ppermute | solution.py:63
  8.0 6.0 %collective-permute-start.2 = (f32[128,256]{1,0:T(8,128)S(1)}, f32[128,256]{1,0:T(8,128)S(1)}, u32[]{:S(2)}, u32[]{:S(2)}) collective-permute-start(f32[128,256]{1,0:T(8,128)S(1)} %get-tuple-element.28), channel_id=1, source_target_pairs={{0,3},{1,0},{2,1},{3,2},{4,7},{5,4},{6,5},{7,6},{8,11},{9,8},{10,9... | collective-permute-start | bytes 393224 | tf_op jit(solution)/shard_map/ppermute | solution.py:63
  14.0 8.2 %collective-permute-start.3 = (f32[384,256]{1,0:T(8,128)S(1)}, f32[384,256]{1,0:T(8,128)S(1)}, u32[]{:S(2)}, u32[]{:S(2)}) collective-permute-start(f32[384,256]{1,0:T(8,128)S(1)} %constant_dynamic-update-slice_fusion.half_ref), channel_id=1, source_target_pairs={{0,4},{1,5},{2,6},{3,7},{4,0},{5,1},{6,2},{7,3},{8,12},{9,13},{10,... | collective-permute-start | bytes 1179656 | tf_op jit(solution)/shard_map/ppermute | solution.py:63
  27.3 10.4 %collective-permute-start.12 = (bf16[256,256]{1,0:T(8,128)(2,1)S(1)}, bf16[256,256]{1,0:T(8,128)(2,1)S(1)}, u32[]{:S(2)}, u32[]{:S(2)}) collective-permute-start(bf16[256,256]{1,0:T(8,128)(2,1)S(1)} %get-tuple-element.36), channel_id=1, source_target_pairs={{0,1},{1,2},{2,3},{3,0},{4,5},{5,6},{6,7},{7,4},{8,9},{9,10},{10,1... | collective-permute-start | bytes 393224 | tf_op jit(solution)/shard_map/ppermute | solution.py:63
  28.6 9.2 %collective-permute-start.13 = (bf16[256,256]{1,0:T(8,128)(2,1)S(1)}, bf16[256,256]{1,0:T(8,128)(2,1)S(1)}, u32[]{:S(2)}, u32[]{:S(2)}) collective-permute-start(bf16[256,256]{1,0:T(8,128)(2,1)S(1)} %get-tuple-element.37), channel_id=1, source_target_pairs={{0,2},{1,3},{2,0},{3,1},{4,6},{5,7},{6,4},{7,5},{8,10},{9,11},{10,... | collective-permute-start | bytes 393224 | tf_op jit(solution)/shard_map/ppermute | solution.py:63
  31.0 6.9 %collective-permute-start.14 = (bf16[256,256]{1,0:T(8,128)(2,1)S(1)}, bf16[256,256]{1,0:T(8,128)(2,1)S(1)}, u32[]{:S(2)}, u32[]{:S(2)}) collective-permute-start(bf16[256,256]{1,0:T(8,128)(2,1)S(1)} %get-tuple-element.38), channel_id=1, source_target_pairs={{0,3},{1,0},{2,1},{3,2},{4,7},{5,4},{6,5},{7,6},{8,11},{9,8},{10,9... | collective-permute-start | bytes 393224 | tf_op jit(solution)/shard_map/ppermute | solution.py:63
  40.2 26.4 %collective-permute-start.15 = (bf16[1024,256]{1,0:T(8,128)(2,1)}, bf16[1024,256]{1,0:T(8,128)(2,1)}, u32[]{:S(2)}, u32[]{:S(2)}) collective-permute-start(bf16[1024,256]{1,0:T(8,128)(2,1)} %get-tuple-element.40), channel_id=1, source_target_pairs={{0,4},{1,5},{2,6},{3,7},{4,0},{5,1},{6,2},{7,3},{8,12},{9,13},{10,... | collective-permute-start | bytes 1572872 | tf_op jit(solution)/shard_map/ppermute | solution.py:63
  42.5 4.9 %collective-permute-start.5 = (f32[96,256]{1,0:T(8,128)S(1)}, f32[96,256]{1,0:T(8,128)S(1)}, u32[]{:S(2)}, u32[]{:S(2)}) collective-permute-start(f32[96,256]{1,0:T(8,128)S(1)} %add.116), channel_id=1, source_target_pairs={{0,32},{1,33},{2,34},{3,35},{4,36},{5,37},{6,38},{7,39},{8,40},{9,... | collective-permute-start | bytes 294920 | tf_op jit(solution)/shard_map/ppermute | solution.py:63
  47.4 5.9 %collective-permute-start.6 = (f32[96,256]{1,0:T(8,128)S(1)}, f32[96,256]{1,0:T(8,128)S(1)}, u32[]{:S(2)}, u32[]{:S(2)}) collective-permute-start(f32[96,256]{1,0:T(8,128)S(1)} %add.117), channel_id=1, source_target_pairs={{0,96},{1,97},{2,98},{3,99},{4,100},{5,101},{6,102},{7,103},{8,104... | collective-permute-start | bytes 294920 | tf_op jit(solution)/shard_map/ppermute | solution.py:63
  53.4 4.7 %collective-permute-start.7 = (f32[96,256]{1,0:T(8,128)S(1)}, f32[96,256]{1,0:T(8,128)S(1)}, u32[]{:S(2)}, u32[]{:S(2)}) collective-permute-start(f32[96,256]{1,0:T(8,128)S(1)} %add.118), channel_id=1, source_target_pairs={{0,8},{1,9},{2,10},{3,11},{4,12},{5,13},{6,14},{7,15},{8,0},{9,1},... | collective-permute-start | bytes 294920 | tf_op jit(solution)/shard_map/ppermute | solution.py:63
  58.1 6.7 %collective-permute-start.8 = (f32[96,256]{1,0:T(8,128)S(1)}, f32[96,256]{1,0:T(8,128)S(1)}, u32[]{:S(2)}, u32[]{:S(2)}) collective-permute-start(f32[96,256]{1,0:T(8,128)S(1)} %add.119), channel_id=1, source_target_pairs={{0,24},{1,25},{2,26},{3,27},{4,28},{5,29},{6,30},{7,31},{8,16},{9,... | collective-permute-start | bytes 294920 | tf_op jit(solution)/shard_map/ppermute | solution.py:63
  64.8 8.2 %collective-permute-start.9 = (f32[96,256]{1,0:T(8,128)S(1)}, f32[96,256]{1,0:T(8,128)S(1)}, u32[]{:S(2)}, u32[]{:S(2)}) collective-permute-start(f32[96,256]{1,0:T(8,128)S(1)} %add.120), channel_id=1, source_target_pairs={{0,1},{1,0},{2,3},{3,2},{4,5},{5,4},{6,7},{7,6},{8,9},{9,8},{10,11... | collective-permute-start | bytes 294920 | tf_op jit(solution)/shard_map/ppermute | solution.py:63
  67.9 11.2 %collective-permute-start.16 = (bf16[256,256]{1,0:T(8,128)(2,1)S(1)}, bf16[256,256]{1,0:T(8,128)(2,1)S(1)}, u32[]{:S(2)}, u32[]{:S(2)}) collective-permute-start(bf16[256,256]{1,0:T(8,128)(2,1)S(1)} %get-tuple-element.42), channel_id=1, source_target_pairs={{0,64},{1,65},{2,66},{3,67},{4,68},{5,69},{6,70},{7,71},{8,72},{9,... | collective-permute-start | bytes 393224 | tf_op jit(solution)/shard_map/ppermute | solution.py:63
  69.8 9.3 %collective-permute-start.17 = (bf16[256,256]{1,0:T(8,128)(2,1)S(1)}, bf16[256,256]{1,0:T(8,128)(2,1)S(1)}, u32[]{:S(2)}, u32[]{:S(2)}) collective-permute-start(bf16[256,256]{1,0:T(8,128)(2,1)S(1)} %get-tuple-element.43), channel_id=1, source_target_pairs={{0,32},{1,33},{2,34},{3,35},{4,36},{5,37},{6,38},{7,39},{8,40},{9,... | collective-permute-start | bytes 393224 | tf_op jit(solution)/shard_map/ppermute | solution.py:63
  71.6 7.5 %collective-permute-start.18 = (bf16[256,256]{1,0:T(8,128)(2,1)S(1)}, bf16[256,256]{1,0:T(8,128)(2,1)S(1)}, u32[]{:S(2)}, u32[]{:S(2)}) collective-permute-start(bf16[256,256]{1,0:T(8,128)(2,1)S(1)} %get-tuple-element.44), channel_id=1, source_target_pairs={{0,96},{1,97},{2,98},{3,99},{4,100},{5,101},{6,102},{7,103},{8,104... | collective-permute-start | bytes 393224 | tf_op jit(solution)/shard_map/ppermute | solution.py:63
  73.0 5.9 %collective-permute-start.10 = (f32[96,256]{1,0:T(8,128)S(1)}, f32[96,256]{1,0:T(8,128)S(1)}, u32[]{:S(2)}, u32[]{:S(2)}) collective-permute-start(f32[96,256]{1,0:T(8,128)S(1)} %add.121), channel_id=1, source_target_pairs={{0,3},{1,2},{2,1},{3,0},{4,7},{5,6},{6,5},{7,4},{8,11},{9,10},{10,... | collective-permute-start | bytes 294920 | tf_op jit(solution)/shard_map/ppermute | solution.py:63
  78.9 5.4 %collective-permute-start.11 = (f32[96,256]{1,0:T(8,128)S(1)}, f32[96,256]{1,0:T(8,128)S(1)}, u32[]{:S(2)}, u32[]{:S(2)}) collective-permute-start(f32[96,256]{1,0:T(8,128)S(1)} %add.122.mine_ref), channel_id=1, source_target_pairs={{0,4},{1,5},{2,6},{3,7},{4,0},{5,1},{6,2},{7,3},{8,12},{9,13},{10,... | collective-permute-start | bytes 294920 | tf_op jit(solution)/shard_map/ppermute | solution.py:63
  79.2 16.0 %collective-permute-start.19 = (f32[64,256]{1,0:T(8,128)S(1)}, f32[64,256]{1,0:T(8,128)S(1)}, u32[]{:S(2)}, u32[]{:S(2)}) collective-permute-start(f32[64,256]{1,0:T(8,128)S(1)} %get-tuple-element.49), channel_id=1, source_target_pairs={{0,16},{1,17},{2,18},{3,19},{4,20},{5,21},{6,22},{7,23},{8,24},{9,... | collective-permute-start | bytes 196616 | tf_op jit(solution)/shard_map/ppermute | solution.py:63
  81.1 14.0 %collective-permute-start.20 = (f32[64,256]{1,0:T(8,128)S(1)}, f32[64,256]{1,0:T(8,128)S(1)}, u32[]{:S(2)}, u32[]{:S(2)}) collective-permute-start(f32[64,256]{1,0:T(8,128)S(1)} %get-tuple-element.51), channel_id=1, source_target_pairs={{0,8},{1,9},{2,10},{3,11},{4,12},{5,13},{6,14},{7,15},{8,16},{9,17... | collective-permute-start | bytes 196616 | tf_op jit(solution)/shard_map/ppermute | solution.py:63
  83.3 11.8 %collective-permute-start.21 = (f32[64,256]{1,0:T(8,128)S(1)}, f32[64,256]{1,0:T(8,128)S(1)}, u32[]{:S(2)}, u32[]{:S(2)}) collective-permute-start(f32[64,256]{1,0:T(8,128)S(1)} %get-tuple-element.50), channel_id=1, source_target_pairs={{0,24},{1,25},{2,26},{3,27},{4,28},{5,29},{6,30},{7,31},{8,0},{9,1... | collective-permute-start | bytes 196616 | tf_op jit(solution)/shard_map/ppermute | solution.py:63
  95.2 7.1 %collective-permute-start.22 = (f32[16,256]{1,0:T(8,128)S(1)}, f32[16,256]{1,0:T(8,128)S(1)}, u32[]{:S(2)}, u32[]{:S(2)}) collective-permute-start(f32[16,256]{1,0:T(8,128)S(1)} %get-tuple-element.54), channel_id=1, source_target_pairs={{0,1},{1,2},{2,3},{3,0},{4,5},{5,6},{6,7},{7,4},{8,9},{9,10},{10,1... | collective-permute-start | bytes 49160 | tf_op jit(solution)/shard_map/ppermute | solution.py:63
  95.3 7.1 %collective-permute-start.23 = (f32[16,256]{1,0:T(8,128)S(1)}, f32[16,256]{1,0:T(8,128)S(1)}, u32[]{:S(2)}, u32[]{:S(2)}) collective-permute-start(f32[16,256]{1,0:T(8,128)S(1)} %get-tuple-element.53), channel_id=1, source_target_pairs={{0,2},{1,3},{2,0},{3,1},{4,6},{5,7},{6,4},{7,5},{8,10},{9,11},{10,... | collective-permute-start | bytes 49160 | tf_op jit(solution)/shard_map/ppermute | solution.py:63
  98.2 4.2 %collective-permute-start.24 = (f32[16,256]{1,0:T(8,128)S(1)}, f32[16,256]{1,0:T(8,128)S(1)}, u32[]{:S(2)}, u32[]{:S(2)}) collective-permute-start(f32[16,256]{1,0:T(8,128)S(1)} %get-tuple-element.52), channel_id=1, source_target_pairs={{0,3},{1,0},{2,1},{3,2},{4,7},{5,4},{6,5},{7,6},{8,11},{9,8},{10,9... | collective-permute-start | bytes 49160 | tf_op jit(solution)/shard_map/ppermute | solution.py:63
  (6 other events, 38.5 us)
